TPU v7x, 256 devices: a whole 4x4x8 slice. The times are simulated.
256 devices in a mesh: grp: 4 (over x), row: 64 (over y, z, core).
Axes of the slice: x: 4, y: 4, z: 8, core: 2. Of those that a mesh axis runs over, the one named last changes fastest.
Arguments:
- serving: bfloat16 [131072, 128], P('row'), may hold values from -1 to 1
- serving_scale: bfloat16 [1024], P('row'), may hold values from 0.099609375 to 1
- hot_blocks: int32 [4, 128], P('grp', 'row'), may hold values from 0 to 15, as said below
- bag_lengths: int32 [256, 256], P(('grp', 'row')), may hold values from 1 to 16, 1024 in all within a row
- bag_indices: int32 [256, 1024], P(('grp', 'row')), may hold values from 0 to 16383, as said below
- dense_act: bfloat16 [65536, 128], P(('grp', 'row')), may hold values from -6 to 6
- labels: float32 [65536], P(('grp', 'row')), may hold values from 0 to 1
- w_top: bfloat16 [256, 1024], replicated, may hold values from -0.375 to 0.375
- w_out: float32 [1024], replicated, may hold values from -0.012 to 0.012
- master: float32 [4, 32768, 128], P('grp', 'row'), may hold values from -0.3 to 0.3
- accum: float32 [4, 32768], P('grp', 'row'), may hold values from 1e-05 to 0.0001
Outputs:
- new_master: float32 [4, 32768, 128], P('grp', 'row')
- new_accum: float32 [4, 32768], P('grp', 'row')
- new_serving: bfloat16 [131072, 128], P('row')
- new_scale: bfloat16 [1024], P('row')
- top_grad: float32 [256, 1024], replicated
Inputs may be any that keep to these rules, and one draw needn't show every extreme that they name: `hot_blocks`: the 2 entries that one group names in one row shard are distinct. `bag_indices`: in each device's line, exactly 8 distinct values lie in each range of 256 consecutive positions that starts at a multiple of 256.
All inputs are finite; a program needn't handle non-finite values. Where the computation divides by a largest or mean magnitude, that divisor is 1e-20 or more.
Results may differ from a plain program's by a relative error of at most 0.012.
Values may be sent and summed in bfloat16 or wider, within the bound.
No kernel may reach another device: no remote copies, remote signals or barrier semaphores. Data moves between devices by JAX's collectives and lax.ppermute only.
A program may use at most 128 MiB of HBM per device.

v0:
```python
import jax
import jax.numpy as jnp
from jax import lax
from jax.experimental import pallas as pl
from jax.experimental.pallas import tpu as pltpu
from jax.sharding import Mesh
from jax.sharding import PartitionSpec as P


ROW = ("row_0", "row_1", "row_2")
CHIPS = ("row_0", "row_1")
GRP_ROW = ("grp", "row_0", "row_1", "row_2")
N_GRP = 4
N_ROW = 64
BLOCK = 128
SPAN = 256
CAP = 8
BAGS = 256
NNZ = 1024
SLOTS = N_ROW * CAP
D = 128
FF = 1024
QUARTER = 512
LR = 0.05
GRANT = 16 << 20
F32 = jnp.float32
BF16 = jnp.bfloat16
I32 = jnp.int32
VM = pl.BlockSpec(memory_space=pltpu.VMEM)
SM = pl.BlockSpec(memory_space=pltpu.SMEM)


def iota(shape, dim):
    return lax.broadcasted_iota(I32, shape, dim)


def dot(a, b, ca=1, cb=0):
    return lax.dot_general(a, b, (((ca,), (cb,)), ((), ())), preferred_element_type=F32)


def ones_where(mask):
    return jnp.where(mask, 1.0, 0.0).astype(BF16)


def call(kernel, outs, specs, args, flops, scratch=()):
    bytes_accessed = sum(a.size * a.dtype.itemsize for a in args) + sum(
        o.size * o.dtype.itemsize for o in outs
    )
    return pl.pallas_call(
        kernel,
        out_shape=outs,
        in_specs=specs,
        out_specs=[VM] * len(outs),
        cost_estimate=pl.CostEstimate(
            flops=flops, bytes_accessed=bytes_accessed, transcendentals=0
        ),
        scratch_shapes=scratch,
        compiler_params=pltpu.CompilerParams(vmem_limit_bytes=GRANT),
    )(*args)


def shard_and_row(idx_ref):
    idx = idx_ref[...]
    shard = lax.shift_right_logical(idx, 8)
    return shard, idx & (SPAN - 1)


def ids_kernel(idx_ref, ids_ref, rank_ref):
    shard, row = shard_and_row(idx_ref)
    in_shard = ones_where(iota((N_ROW, NNZ), 0) == shard)
    at_row = ones_where(iota((SPAN, NNZ), 0) == row)
    used = dot(in_shard, at_row, 1, 1) > 0.5
    before = ones_where(iota((SPAN, SPAN), 0) < iota((SPAN, SPAN), 1))
    rank = dot(ones_where(used), before)
    column = iota((N_ROW, SPAN), 1).astype(F32)
    lane = iota((N_ROW, D), 1)
    ids = jnp.zeros((N_ROW, D), F32)
    for k in range(CAP):
        mine = jnp.sum(
            jnp.where(used & (rank == float(k)), column, 0.0), axis=1, keepdims=True
        )
        ids = jnp.where(lane == k, mine, ids)
    ids_ref[...] = ids.astype(I32)
    rank_ref[...] = rank.astype(BF16)


def counts_kernel(idx_ref, len_ref, rank_ref, use_ref, use_t_ref):
    shard, row = shard_and_row(idx_ref)
    in_shard = ones_where(iota((N_ROW, NNZ), 0) == shard)
    rank_at = dot(rank_ref[...], in_shard, 0, 0)
    rank = jnp.sum(jnp.where(iota((SPAN, NNZ), 0) == row, rank_at, 0.0), axis=0, keepdims=True)
    slot = shard * CAP + rank.astype(I32)
    at_slot = ones_where(iota((SLOTS, NNZ), 0) == slot)
    lengths = jnp.broadcast_to(len_ref[...].astype(F32), (BAGS, BAGS))
    a, b = iota((BAGS, BAGS), 0), iota((BAGS, BAGS), 1)
    starts = jnp.sum(jnp.where(b < a, lengths, 0.0), axis=1, keepdims=True).astype(I32)
    ends = jnp.sum(jnp.where(b <= a, lengths, 0.0), axis=1, keepdims=True).astype(I32)
    place = iota((BAGS, NNZ), 1)
    in_bag = ones_where((place >= starts) & (place < ends))
    use_ref[...] = dot(in_bag, at_slot, 1, 1).astype(BF16)
    use_t_ref[...] = dot(at_slot, in_bag, 1, 1).astype(BF16)


def table_kernel(hot_ref, serving_ref, scale_ref, table_ref, buf, sem):
    copies = [
        pltpu.make_async_copy(
            serving_ref.at[pl.ds(pl.multiple_of(hot_ref[0, j] * BLOCK, BLOCK), BLOCK)],
            buf.at[j],
            sem.at[j],
        )
        for j in range(2)
    ]
    for c in copies:
        c.start()
    scales = scale_ref[...].astype(F32)
    lane = iota(scales.shape, 1)
    for j, c in enumerate(copies):
        own = jnp.sum(jnp.where(lane == hot_ref[0, j], scales, 0.0), axis=1, keepdims=True)
        c.wait()
        table_ref[j * BLOCK : (j + 1) * BLOCK, :] = (buf[j].astype(F32) * own).astype(BF16)


def pick_kernel(ids_ref, table_ref, rows_ref):
    owner = ones_where(lax.shift_right_logical(iota((SLOTS, N_ROW), 0), 3) == iota((SLOTS, N_ROW), 1))
    spread = dot(owner, ids_ref[...].astype(F32).astype(BF16))
    mine = iota((SLOTS, D), 1) == (iota((SLOTS, D), 0) & (CAP - 1))
    column = jnp.sum(jnp.where(mine, spread, 0.0), axis=1, keepdims=True).astype(I32)
    onehot = ones_where(iota((SLOTS, SPAN), 1) == column)
    rows_ref[...] = dot(onehot, table_ref[...]).astype(BF16)


def place_kernel(ids_ref, place_ref):
    owner = ones_where(lax.shift_right_logical(iota((SLOTS, N_ROW), 0), 3) == iota((SLOTS, N_ROW), 1))
    spread = dot(ids_ref[...].astype(F32).astype(BF16), owner, 0, 1)
    mine = iota((D, SLOTS), 0) == (iota((D, SLOTS), 1) & (CAP - 1))
    line = jnp.sum(jnp.where(mine, spread, 0.0), axis=0, keepdims=True).astype(I32)
    place_ref[...] = ones_where(iota((SPAN, SLOTS), 0) == line)


def dense_kernel(dense_ref, w_ref, labels_ref, w_out_ref, pre_ref, labels_out_ref, w_out_out_ref):
    pre_ref[...] = dot(dense_ref[...], w_ref[D : 2 * D, :])
    a, b = iota((BAGS, BAGS), 0), iota((BAGS, BAGS), 1)
    labels = jnp.sum(
        jnp.where(a == b, jnp.broadcast_to(labels_ref[...], (BAGS, BAGS)), 0.0),
        axis=1,
        keepdims=True,
    )
    labels_out_ref[...] = jnp.broadcast_to(labels, (BAGS, D))
    w_out_out_ref[...] = w_out_ref[...]


def step_kernel(
    core_ref, rows_ref, use_ref, dense_ref, pre_ref, labels_ref, w_ref, w_out_ref,
    give_ref, keep_ref, pooled_grad_ref,
):
    pooled = dot(use_ref[...], rows_ref[...]).astype(BF16)
    pre = pre_ref[...] + dot(pooled, w_ref[0:D, :])
    sig = jax.nn.sigmoid(pre)
    w_out = w_out_ref[...]
    logit = jnp.sum(pre * sig * w_out, axis=1, keepdims=True)
    dlogit = jax.nn.sigmoid(logit) - labels_ref[:, 0:1]
    dpre = (dlogit * w_out * (sig * (1.0 + pre * (1.0 - sig)))).astype(BF16)
    first = core_ref[0] == 0
    dense = dense_ref[...]
    give = dot(jnp.where(first, dense, pooled), dpre, 0, 0).astype(BF16)
    keep = dot(jnp.where(first, pooled, dense), dpre, 0, 0)
    for i in range(8):
        for j in range(8):
            tile = slice(i * 16, (i + 1) * 16), slice(j * 128, (j + 1) * 128)
            give_ref[i * 8 + j] = give[tile]
            keep_ref[i * 8 + j] = keep[tile]
    pooled_grad_ref[...] = dot(dpre, w_ref[0:D, :], 1, 1)


def row_grad_kernel(pooled_grad_ref, use_t_ref, out_ref):
    pooled_grad = pooled_grad_ref[...]
    high = pooled_grad.astype(BF16)
    low = (pooled_grad - high.astype(F32)).astype(BF16)
    use_t = use_t_ref[...]
    out_ref[...] = (dot(use_t, high) + dot(use_t, low)).astype(BF16)


def parts_kernel(keep_ref, given_ref, row_grad_ref, out_ref):
    out_ref[:, 0:16, :] = (keep_ref[...] + given_ref[...].astype(F32)).astype(BF16)
    out_ref[:, 16:24, :] = row_grad_ref[...]


def owned_kernel(got_ref, place_ref, hot_ref, out_ref):
    grads = got_ref[:, :, 16:24, :].astype(F32).reshape(SLOTS, D).astype(BF16)
    out_ref[0:SPAN, :] = dot(place_ref[...], grads).astype(BF16)
    for half in range(2):
        at = SPAN + 16 * half
        out_ref[at : at + 16, :] = jnp.sum(
            got_ref[:, half, 0:16, :].astype(F32), axis=0
        ).astype(BF16)
    lane = iota((16, D), 1)
    hot = jnp.where(lane == 0, hot_ref[0, 0], jnp.where(lane == 1, hot_ref[0, 1], 0))
    out_ref[SPAN + 32 : SPAN + 48, :] = hot.astype(F32).astype(BF16)


def top_kernel(me_ref, x0_ref, x1_ref, x2_ref, x3_ref, top_ref, by_group):
    me = me_ref[0]
    for o, ref in enumerate((x0_ref, x1_ref, x2_ref, x3_ref)):
        by_group[(me - o) & 3] = ref[SPAN : SPAN + 32, :]
    top = jnp.zeros((32, D), F32)
    for g in range(N_GRP):
        top = top + by_group[g].astype(F32)
    top_ref[...] = jnp.broadcast_to(top.astype(BF16)[None], (N_ROW // 2, 32, D))


def owner_kernel(master_ref, accum_ref, out_ref):
    out_ref[0:QUARTER, :] = master_ref[...]
    line = iota((8, D), 0)
    accum = jnp.zeros((8, D), F32)
    for q in range(4):
        accum = jnp.where(line == q, accum_ref[:, q * BLOCK : (q + 1) * BLOCK], accum)
    out_ref[QUARTER : QUARTER + 8, :] = accum


def update_kernel(
    me_ref, x0_ref, x1_ref, x2_ref, x3_ref, m0_ref, m1_ref, m2_ref, m3_ref,
    new_master_ref, new_accum_ref, serving_ref, scale_ref, by_group, grads,
):
    me = me_ref[0]
    for o, ref in enumerate((x0_ref, x1_ref, x2_ref, x3_ref)):
        by_group[(me - o) & 3] = ref[...]
    grads[...] = jnp.zeros((16, BLOCK, D), F32)
    for g in range(N_GRP):
        hot = by_group[g, SPAN + 32 : SPAN + 48, :].astype(F32).astype(I32)
        for j in range(2):
            number = jnp.clip(hot[0, j], 0, 15)
            grads[number] = grads[number] + by_group[g, j * BLOCK : (j + 1) * BLOCK, :].astype(F32)
    a, b = iota((BLOCK, BLOCK), 0), iota((BLOCK, BLOCK), 1)
    diagonal = a == b
    lane = iota((1, 16), 1)
    scales = jnp.zeros((1, 16), F32)
    for o, ref in enumerate((m0_ref, m1_ref, m2_ref, m3_ref)):
        for q in range(4):
            number = ((me - o) & 3) * 4 + q
            grad = grads[number]
            accum = jnp.broadcast_to(ref[QUARTER + q : QUARTER + q + 1, :], (BLOCK, BLOCK))
            state = jnp.sum(jnp.where(diagonal, accum, 0.0), axis=1, keepdims=True) + jnp.mean(
                grad * grad, axis=1, keepdims=True
            )
            weights = ref[q * BLOCK : (q + 1) * BLOCK, :] - grad * (LR / jnp.sqrt(state))
            if o == 0:
                new_master_ref[q * BLOCK : (q + 1) * BLOCK, :] = weights
                new_accum_ref[:, q * BLOCK : (q + 1) * BLOCK] = jnp.sum(
                    jnp.where(diagonal, jnp.broadcast_to(state, (BLOCK, BLOCK)), 0.0),
                    axis=0,
                    keepdims=True,
                )
            largest = jnp.max(jnp.max(jnp.abs(weights), axis=0, keepdims=True), axis=1, keepdims=True)
            scale = (largest + 1e-06).astype(BF16).astype(F32)
            at = pl.ds(pl.multiple_of(number * BLOCK, BLOCK), BLOCK)
            serving_ref[at, :] = (weights / scale).astype(BF16)
            scales = jnp.where(lane == number, scale, scales)
    scale_ref[...] = scales.astype(BF16)


def last_kernel(core_ref, mine_ref, other_ref, top_ref):
    for ref, core in ((mine_ref, core_ref[0]), (other_ref, 1 - core_ref[0])):
        for s in range(N_ROW // 2):
            column = pl.multiple_of((s % 4 * 2 + core) * 128, 128)
            for half in range(2):
                line = half * 128 + s // 4 * 16
                top_ref[line : line + 16, pl.ds(column, 128)] = ref[
                    s, half * 16 : (half + 1) * 16, :
                ].astype(F32)


def like(shape, dtype):
    return jax.ShapeDtypeStruct(shape, dtype)


def over_groups(x):
    return [x] + [
        lax.ppermute(x, "grp", [(g, (g + o) % N_GRP) for g in range(N_GRP)]) for o in (1, 2, 3)
    ]


def other_core(x):
    return lax.ppermute(x, "row_2", [(0, 1), (1, 0)])


def exchange(x, axes=ROW):
    return lax.all_to_all(x, axes, 0, 0, tiled=True)


def on_device(
    serving, serving_scale, hot_blocks, bag_lengths, bag_indices, dense_act, labels, w_top, w_out, master, accum,
):
    me = lax.axis_index("grp").astype(I32).reshape(1)
    core = lax.axis_index("row_2").astype(I32).reshape(1)
    ids, rank = call(
        ids_kernel,
        [like((N_ROW, D), I32), like((N_ROW, SPAN), BF16)],
        [VM],
        (bag_indices,),
        1 << 26,
    )
    wanted = exchange(ids.reshape(N_ROW, 1, D)).reshape(N_ROW, D)
    (owner,) = call(
        owner_kernel, [like((QUARTER + 8, D), F32)], [VM] * 2, (master[0], accum), 1 << 16
    )
    use, use_t = call(
        counts_kernel,
        [like((BAGS, SLOTS), BF16), like((SLOTS, BAGS), BF16)],
        [VM] * 3,
        (bag_indices, bag_lengths, rank),
        1 << 29,
    )
    (table,) = call(
        table_kernel,
        [like((SPAN, D), BF16)],
        [SM, pl.BlockSpec(memory_space=pl.ANY), VM],
        (hot_blocks, serving, serving_scale.reshape(1, 16)),
        1 << 20,
        [pltpu.VMEM((2, BLOCK, D), BF16), pltpu.SemaphoreType.DMA((2,))],
    )
    pre, labels_column, w_out_line = call(
        dense_kernel,
        [like((BAGS, FF), F32), like((BAGS, D), F32), like((1, FF), F32)],
        [VM] * 4,
        (dense_act, w_top, labels.reshape(1, BAGS), w_out.reshape(1, FF)),
        1 << 27,
    )
    wanted, table, pre, labels_column, w_out_line = lax.optimization_barrier(
        (wanted, table, pre, labels_column, w_out_line)
    )
    owners = over_groups(owner)
    (rows,) = call(pick_kernel, [like((SLOTS, D), BF16)], [VM] * 2, (wanted, table), 1 << 26)
    fetched = exchange(rows.reshape(N_ROW, CAP, D)).reshape(SLOTS, D)
    (place,) = call(place_kernel, [like((SPAN, SLOTS), BF16)], [VM], (wanted,), 1 << 26)
    give, keep, pooled_grad = call(
        step_kernel,
        [like((N_ROW, 16, D), BF16), like((N_ROW, 16, D), F32), like((BAGS, D), F32)],
        [SM] + [VM] * 7,
        (core, fetched, use, dense_act, pre, labels_column, w_top, w_out_line),
        1 << 29,
    )
    given = other_core(give)
    (row_grad,) = call(
        row_grad_kernel, [like((SLOTS, D), BF16)], [VM] * 2, (pooled_grad, use_t), 1 << 27
    )
    (parts,) = call(
        parts_kernel,
        [like((N_ROW, 24, D), BF16)],
        [VM] * 3,
        (keep, given, row_grad.reshape(N_ROW, CAP, D)),
        1 << 20,
    )
    got = exchange(parts)
    (own,) = call(
        owned_kernel,
        [like((SPAN + 48, D), BF16)],
        [VM, VM, SM],
        (got.reshape(N_ROW // 2, 2, 24, D), place, hot_blocks),
        1 << 26,
    )
    owned = over_groups(own)
    (top_part,) = call(
        top_kernel,
        [like((N_ROW // 2, 32, D), BF16)],
        [SM] + [VM] * 4,
        (me, *owned),
        1 << 16,
        [pltpu.VMEM((N_GRP, 32, D), BF16)],
    )
    top_mine = exchange(top_part, CHIPS)
    new_master, new_accum, fresh, fresh_scale = call(
        update_kernel,
        [
            like((QUARTER, D), F32),
            like((1, QUARTER), F32),
            like((4 * QUARTER, D), BF16),
            like((1, 16), BF16),
        ],
        [SM] + [VM] * 8,
        (me, *owned, *owners),
        1 << 22,
        [pltpu.VMEM((N_GRP, SPAN + 48, D), BF16), pltpu.VMEM((16, BLOCK, D), F32)],
    )
    top_mine, fresh_scale = lax.optimization_barrier((top_mine, fresh_scale))
    (top_grad,) = call(
        last_kernel,
        [like((2 * D, FF), F32)],
        [SM] + [VM] * 2,
        (core, top_mine, other_core(top_mine)),
        1 << 20,
    )
    return new_master[None], new_accum, fresh, fresh_scale.reshape(16), top_grad


def solution(mesh):
    finer = Mesh(
        mesh.devices.reshape(mesh.shape["grp"], 4, 8, 2), ("grp", "row_0", "row_1", "row_2")
    )
    in_specs = (
        P(ROW, None),
        P(ROW),
        P("grp", ROW),
        P(GRP_ROW, None),
        P(GRP_ROW, None),
        P(GRP_ROW, None),
        P(GRP_ROW),
        P(),
        P(),
        P("grp", ROW, None),
        P("grp", ROW),
    )
    out_specs = (P("grp", ROW, None), P("grp", ROW), P(ROW, None), P(ROW), P())
    return jax.shard_map(
        on_device, mesh=finer, in_specs=in_specs, out_specs=out_specs, check_vma=False
    )
```

profile of v0, /device:TPU:8, one launch (start us, length us, event | category | flops | bytes accessed | tf_op | source)
XLA Modules:
  0.0 99.4 jit_solution(15884748444420013010)
XLA Ops:
  0.6 0.0 copy-start
  0.6 0.0 copy-start.10
  0.7 0.7 copy-done.10
  1.4 1.2 %shard_map.146 = (s32[64,128]{1,0:T(8,128)}, bf16[64,256]{1,0:T(8,128)(2,1)S(1)}) custom-call(s32[1,1024]{1,0:T(1,128)S(1)} %copy-done.10), custom_call_target="tpu_custom_call" | custom-call | flops 67108864 | bytes 69632 | tf_op jit(solution)/shard_map/pallas_call | solution.py:49
  2.5 12.1 %all-to-all-start = ((s32[64,1,128]{2,1,0:T(1,128)}), s32[64,1,128]{2,1,0:T(1,128)S(1)}, u32[]{:S(2)}, u32[]{:S(2)}) async-start(s32[64,1,128]{2,1,0:T(1,128)} %bitcast.3), calls=%async_computation | async-start | bytes 65536 | tf_op jit(solution)/shard_map/all_to_all | solution.py:287
  14.7 0.0 copy-start.1
  14.7 1.0 %copy-done.1 = bf16[2048,128]{1,0:T(8,128)(2,1)S(1)} copy-done((bf16[2048,128]{1,0:T(8,128)(2,1)S(1)}, bf16[2048,128]{1,0:T(8,128)(2,1)}, u32[]{:S(2)}) %copy-start.1) | copy-done | bytes 524312
  15.7 0.0 copy-start.6
  15.7 0.7 copy-done.6
  16.4 0.0 copy-start.9
  16.4 0.7 copy-done.9
  17.0 0.0 copy-start.2
  17.0 0.0 copy-start.4
  17.0 0.8 shard_map.147.table_ref
  17.8 0.0 copy-start.8
  17.9 0.0 copy-done
  17.9 0.0 copy-done.2
  17.9 0.0 copy-done.4
  17.9 0.6 copy-done.8
  18.5 0.3 shard_map.148
  18.8 4.4 %all-to-all-done = s32[64,1,128]{2,1,0:T(1,128)S(1)} async-done(((s32[64,1,128]{2,1,0:T(1,128)}), s32[64,1,128]{2,1,0:T(1,128)S(1)}, u32[]{:S(2)}, u32[]{:S(2)}) %all-to-all-start) | async-done | bytes 32800 | tf_op jit(solution)/shard_map/all_to_all | solution.py:287
  23.2 1.1 %shard_map.149 = bf16[512,128]{1,0:T(8,128)(2,1)} custom-call(s32[64,128]{1,0:T(8,128)S(1)} %bitcast.20, bf16[256,128]{1,0:T(8,128)(2,1)S(1)} %shard_map.147.table_ref), custom_call_target="tpu_custom_call" | custom-call | flops 67108864 | bytes 229376 | tf_op jit(solution)/shard_map/pallas_call | solution.py:49
  24.3 5.9 %all-to-all-start.1 = ((bf16[64,8,128]{2,1,0:T(8,128)(2,1)}), bf16[64,8,128]{2,1,0:T(8,128)(2,1)S(1)}, u32[]{:S(2)}, u32[]{:S(2)}) async-start(bf16[64,8,128]{2,1,0:T(8,128)(2,1)} %bitcast.8), calls=%async_computation.1 | async-start | bytes 262144 | tf_op jit(solution)/shard_map/all_to_all | solution.py:287
  30.2 0.0 copy-start.11
  30.3 0.0 copy-start.12
  30.3 0.7 copy-done.11
  30.9 0.0 copy-done.12
  30.9 1.3 %shard_map.150 = (bf16[256,512]{1,0:T(8,128)(2,1)S(1)}, bf16[512,256]{1,0:T(8,128)(2,1)S(1)}) custom-call(s32[1,1024]{1,0:T(1,128)S(1)} %copy-done.11, s32[1,256]{1,0:T(1,128)S(1)} %copy-done.12, bf16[64,256]{1,0:T(8,128)(2,1)S(1)} %get-tuple-element.32.rank_ref), custom_call_target="tpu_custom_call" | custom-call | flops 536870912 | bytes 562176 | tf_op jit(solution)/shard_map/pallas_call | solution.py:49
  32.2 7.4 %all-to-all-done.1 = bf16[64,8,128]{2,1,0:T(8,128)(2,1)S(1)} async-done(((bf16[64,8,128]{2,1,0:T(8,128)(2,1)}), bf16[64,8,128]{2,1,0:T(8,128)(2,1)S(1)}, u32[]{:S(2)}, u32[]{:S(2)}) %all-to-all-start.1) | async-done | bytes 131104 | tf_op jit(solution)/shard_map/all_to_all | solution.py:287
  39.6 1.4 %shard_map.151 = (bf16[64,16,128]{2,1,0:T(8,128)(2,1)S(1)}, f32[64,16,128]{2,1,0:T(8,128)S(1)}, f32[256,128]{1,0:T(8,128)S(1)}) custom-call(s32[1]{0:T(128)} %bitcast.1.core_ref, bf16[512,128]{1,0:T(8,128)(2,1)S(1)} %bitcast.17, bf16[256,512]{1,0:T(8,128)(2,1)S(1)} %get-tuple-element.33.use_ref, bf16[256,128]{1,0:T(8,128)(2,1)S(1)} %copy-done.2, ...), custom_call_target="tpu_custom_call" | custom-call | flops 536870912 | bytes 3084292 | tf_op jit(solution)/shard_map/pallas_call | solution.py:49
  41.0 0.2 collective-permute-start
  41.2 0.3 shard_map.152
  41.6 1.1 %collective-permute-done.given_ref = bf16[64,16,128]{2,1,0:T(8,128)(2,1)S(1)} collective-permute-done((bf16[64,16,128]{2,1,0:T(8,128)(2,1)S(1)}, bf16[64,16,128]{2,1,0:T(8,128)(2,1)S(1)}, u32[]{:S(2)}, u32[]{:S(2)}) %collective-permute-start) | collective-permute-done | bytes 262176 | tf_op jit(solution)/shard_map/ppermute | solution.py:283
  42.7 0.8 shard_map.153
  43.5 5.9 %all-to-all-start.2 = ((bf16[64,24,128]{2,1,0:T(8,128)(2,1)}), bf16[64,24,128]{2,1,0:T(8,128)(2,1)S(1)}, u32[]{:S(2)}, u32[]{:S(2)}) async-start(bf16[64,24,128]{2,1,0:T(8,128)(2,1)} %shard_map.153), calls=%async_computation.2 | async-start | bytes 786432 | tf_op jit(solution)/shard_map/all_to_all | solution.py:287
  49.4 0.3 shard_map.154.place_ref
  49.6 0.0 copy-start.7
  49.7 13.8 %all-to-all-done.2 = bf16[64,24,128]{2,1,0:T(8,128)(2,1)S(1)} async-done(((bf16[64,24,128]{2,1,0:T(8,128)(2,1)}), bf16[64,24,128]{2,1,0:T(8,128)(2,1)S(1)}, u32[]{:S(2)}, u32[]{:S(2)}) %all-to-all-start.2) | async-done | bytes 393248 | tf_op jit(solution)/shard_map/all_to_all | solution.py:287
  63.5 0.0 copy-done.7
  63.5 0.8 shard_map.155.x0_ref
  64.2 1.6 %collective-permute-start.1 = (bf16[304,128]{1,0:T(8,128)(2,1)S(1)}, bf16[304,128]{1,0:T(8,128)(2,1)S(1)}, u32[]{:S(2)}, u32[]{:S(2)}) collective-permute-start(bf16[304,128]{1,0:T(8,128)(2,1)S(1)} %shard_map.155.x0_ref), channel_id=1, source_target_pairs={{0,64},{64,128},{128,192},{192,0},{1,65},{65,129},{129,193},{193,1... | collective-permute-start | bytes 233480 | tf_op jit(solution)/shard_map/ppermute | solution.py:278
  65.8 2.7 %collective-permute-start.2 = (bf16[304,128]{1,0:T(8,128)(2,1)S(1)}, bf16[304,128]{1,0:T(8,128)(2,1)S(1)}, u32[]{:S(2)}, u32[]{:S(2)}) collective-permute-start(bf16[304,128]{1,0:T(8,128)(2,1)S(1)} %shard_map.155.x0_ref), channel_id=1, source_target_pairs={{0,128},{64,192},{128,0},{192,64},{1,129},{65,193},{129,1},{193,65... | collective-permute-start | bytes 233480 | tf_op jit(solution)/shard_map/ppermute | solution.py:278
  68.5 1.4 %collective-permute-start.3 = (bf16[304,128]{1,0:T(8,128)(2,1)S(1)}, bf16[304,128]{1,0:T(8,128)(2,1)S(1)}, u32[]{:S(2)}, u32[]{:S(2)}) collective-permute-start(bf16[304,128]{1,0:T(8,128)(2,1)S(1)} %shard_map.155.x0_ref), channel_id=1, source_target_pairs={{0,192},{64,0},{128,64},{192,128},{1,193},{65,1},{129,65},{193,129... | collective-permute-start | bytes 233480 | tf_op jit(solution)/shard_map/ppermute | solution.py:278
  69.9 0.2 collective-permute-done.1.x1_ref
  70.1 2.6 %collective-permute-done.2.x2_ref = bf16[304,128]{1,0:T(8,128)(2,1)S(1)} collective-permute-done((bf16[304,128]{1,0:T(8,128)(2,1)S(1)}, bf16[304,128]{1,0:T(8,128)(2,1)S(1)}, u32[]{:S(2)}, u32[]{:S(2)}) %collective-permute-start.2) | collective-permute-done | bytes 77856 | tf_op jit(solution)/shard_map/ppermute | solution.py:278
  72.8 0.1 collective-permute-done.3.x3_ref
  72.9 0.7 shard_map.158
  73.6 0.0 copy-start.3
  73.6 0.0 copy-start.5
  73.6 6.4 %all-to-all-start.3 = ((bf16[32,32,128]{2,1,0:T(8,128)(2,1)}), bf16[32,32,128]{2,1,0:T(8,128)(2,1)S(1)}, u32[]{:S(2)}, u32[]{:S(2)}) async-start(bf16[32,32,128]{2,1,0:T(8,128)(2,1)} %shard_map.158), calls=%async_computation.3 | async-start | bytes 524288 | tf_op jit(solution)/shard_map/all_to_all | solution.py:287
  80.1 0.0 copy-done.3
  80.1 0.0 copy-done.5
  80.1 0.8 collective-permute-start.4
  81.0 3.3 %collective-permute-start.5 = (f32[520,128]{1,0:T(8,128)S(1)}, f32[520,128]{1,0:T(8,128)S(1)}, u32[]{:S(2)}, u32[]{:S(2)}) collective-permute-start(f32[520,128]{1,0:T(8,128)S(1)} %shard_map.156.m0_ref), channel_id=1, source_target_pairs={{0,128},{64,192},{128,0},{192,64},{1,129},{65,193},{129,1},{193,65... | collective-permute-start | bytes 798728 | tf_op jit(solution)/shard_map/ppermute | solution.py:278
  84.3 0.6 collective-permute-start.6
  84.9 5.3 %collective-permute-done.4.m1_ref = f32[520,128]{1,0:T(8,128)S(1)} collective-permute-done((f32[520,128]{1,0:T(8,128)S(1)}, f32[520,128]{1,0:T(8,128)S(1)}, u32[]{:S(2)}, u32[]{:S(2)}) %collective-permute-start.4) | collective-permute-done | bytes 266272 | tf_op jit(solution)/shard_map/ppermute | solution.py:278
  90.1 4.3 %collective-permute-done.5.m2_ref = f32[520,128]{1,0:T(8,128)S(1)} collective-permute-done((f32[520,128]{1,0:T(8,128)S(1)}, f32[520,128]{1,0:T(8,128)S(1)}, u32[]{:S(2)}, u32[]{:S(2)}) %collective-permute-start.5) | collective-permute-done | bytes 266272 | tf_op jit(solution)/shard_map/ppermute | solution.py:278
  94.4 0.0 collective-permute-done.6.m3_ref
  94.4 2.4 %shard_map.157 = (f32[512,128]{1,0:T(8,128)}, f32[1,512]{1,0:T(1,128)}, bf16[2048,128]{1,0:T(8,128)(2,1)}, bf16[1,16]{1,0:T(2,128)(2,1)}) custom-call(s32[1]{0:T(128)} %bitcast.me_ref, bf16[304,128]{1,0:T(8,128)(2,1)S(1)} %shard_map.155.x0_ref, bf16[304,128]{1,0:T(8,128)(2,1)S(1)} %collective-permute-done.1.x1_ref, ...), custom_call_target="tpu_custom_call" | custom-call | flops 4194304 | bytes 2164772 | tf_op jit(solution)/shard_map/pallas_call | solution.py:49
  96.8 0.0 all-to-all-done.3.mine_ref
  96.8 0.0 collective-permute-start.7
  96.8 1.5 %collective-permute-done.7.other_ref = bf16[32,32,128]{2,1,0:T(8,128)(2,1)S(1)} collective-permute-done((bf16[32,32,128]{2,1,0:T(8,128)(2,1)S(1)}, bf16[32,32,128]{2,1,0:T(8,128)(2,1)S(1)}, u32[]{:S(2)}, u32[]{:S(2)}) %collective-permute-start.7) | collective-permute-done | bytes 262176 | tf_op jit(solution)/shard_map/ppermute | solution.py:283
  98.3 1.1 %shard_map.159 = f32[256,1024]{1,0:T(8,128)} custom-call(s32[1]{0:T(128)} %bitcast.1.core_ref, bf16[32,32,128]{2,1,0:T(8,128)(2,1)S(1)} %all-to-all-done.3.mine_ref, bf16[32,32,128]{2,1,0:T(8,128)(2,1)S(1)} %collective-permute-done.7.other_ref), custom_call_target="tpu_custom_call" | custom-call | flops 1048576 | bytes 1572868 | tf_op jit(solution)/shard_map/pallas_call | solution.py:49
  (1 shorter events, 0.0 us)
Async XLA Ops:
  0.6 17.2 %copy-start = (bf16[256,1024]{1,0:T(8,128)(2,1)S(1)}, bf16[256,1024]{1,0:T(8,128)(2,1)}, u32[]{:S(2)}) copy-start(bf16[256,1024]{1,0:T(8,128)(2,1)} %w_ref.3) | copy-start | bytes 1572868
  0.6 0.7 copy-start.10
  2.5 20.7 %all-to-all-start = ((s32[64,1,128]{2,1,0:T(1,128)}), s32[64,1,128]{2,1,0:T(1,128)S(1)}, u32[]{:S(2)}, u32[]{:S(2)}) async-start(s32[64,1,128]{2,1,0:T(1,128)} %bitcast.3), calls=%async_computation | async-start | bytes 65536 | tf_op jit(solution)/shard_map/all_to_all | solution.py:287
  14.7 1.0 %copy-start.1 = (bf16[2048,128]{1,0:T(8,128)(2,1)S(1)}, bf16[2048,128]{1,0:T(8,128)(2,1)}, u32[]{:S(2)}) copy-start(bf16[2048,128]{1,0:T(8,128)(2,1)} %serving_ref.1) | copy-start | bytes 1572868
  15.7 0.7 copy-start.6
  16.4 0.7 copy-start.9
  17.0 0.9 copy-start.2
  17.0 0.9 copy-start.4
  17.8 0.7 copy-start.8
  24.3 15.3 %all-to-all-start.1 = ((bf16[64,8,128]{2,1,0:T(8,128)(2,1)}), bf16[64,8,128]{2,1,0:T(8,128)(2,1)S(1)}, u32[]{:S(2)}, u32[]{:S(2)}) async-start(bf16[64,8,128]{2,1,0:T(8,128)(2,1)} %bitcast.8), calls=%async_computation.1 | async-start | bytes 262144 | tf_op jit(solution)/shard_map/all_to_all | solution.py:287
  30.2 0.7 copy-start.11
  30.3 0.7 copy-start.12
  41.0 1.6 %collective-permute-start = (bf16[64,16,128]{2,1,0:T(8,128)(2,1)S(1)}, bf16[64,16,128]{2,1,0:T(8,128)(2,1)S(1)}, u32[]{:S(2)}, u32[]{:S(2)}) collective-permute-start(bf16[64,16,128]{2,1,0:T(8,128)(2,1)S(1)} %get-tuple-element.38), channel_id=1, source_target_pairs={{0,1},{1,0},{2,3},{3,2},{4,5},{5,4},{6,7},{7,6},{8,9},{9,8},{10,11... | collective-permute-start | bytes 786440 | tf_op jit(solution)/shard_map/ppermute | solution.py:283
  43.5 19.9 %all-to-all-start.2 = ((bf16[64,24,128]{2,1,0:T(8,128)(2,1)}), bf16[64,24,128]{2,1,0:T(8,128)(2,1)S(1)}, u32[]{:S(2)}, u32[]{:S(2)}) async-start(bf16[64,24,128]{2,1,0:T(8,128)(2,1)} %shard_map.153), calls=%async_computation.2 | async-start | bytes 786432 | tf_op jit(solution)/shard_map/all_to_all | solution.py:287
  49.6 13.8 %copy-start.7 = (s32[1,2]{1,0:T(1,128)S(1)}, s32[1,2]{1,0:T(1,128)}, u32[]{:S(2)}) copy-start(s32[1,2]{1,0:T(1,128)} %hot_ref.3) | copy-start | bytes 28
  64.2 5.9 %collective-permute-start.1 = (bf16[304,128]{1,0:T(8,128)(2,1)S(1)}, bf16[304,128]{1,0:T(8,128)(2,1)S(1)}, u32[]{:S(2)}, u32[]{:S(2)}) collective-permute-start(bf16[304,128]{1,0:T(8,128)(2,1)S(1)} %shard_map.155.x0_ref), channel_id=1, source_target_pairs={{0,64},{64,128},{128,192},{192,0},{1,65},{65,129},{129,193},{193,1... | collective-permute-start | bytes 233480 | tf_op jit(solution)/shard_map/ppermute | solution.py:278
  65.8 7.0 %collective-permute-start.2 = (bf16[304,128]{1,0:T(8,128)(2,1)S(1)}, bf16[304,128]{1,0:T(8,128)(2,1)S(1)}, u32[]{:S(2)}, u32[]{:S(2)}) collective-permute-start(bf16[304,128]{1,0:T(8,128)(2,1)S(1)} %shard_map.155.x0_ref), channel_id=1, source_target_pairs={{0,128},{64,192},{128,0},{192,64},{1,129},{65,193},{129,1},{193,65... | collective-permute-start | bytes 233480 | tf_op jit(solution)/shard_map/ppermute | solution.py:278
  68.5 4.4 %collective-permute-start.3 = (bf16[304,128]{1,0:T(8,128)(2,1)S(1)}, bf16[304,128]{1,0:T(8,128)(2,1)S(1)}, u32[]{:S(2)}, u32[]{:S(2)}) collective-permute-start(bf16[304,128]{1,0:T(8,128)(2,1)S(1)} %shard_map.155.x0_ref), channel_id=1, source_target_pairs={{0,192},{64,0},{128,64},{192,128},{1,193},{65,1},{129,65},{193,129... | collective-permute-start | bytes 233480 | tf_op jit(solution)/shard_map/ppermute | solution.py:278
  73.6 6.4 %copy-start.3 = (f32[1,512,128]{2,1,0:T(8,128)S(1)}, f32[1,512,128]{2,1,0:T(8,128)}, u32[]{:S(2)}) copy-start(f32[1,512,128]{2,1,0:T(8,128)} %param.20) | copy-start | bytes 786436
  73.6 6.4 %copy-start.5 = (f32[1,512]{1,0:T(1,128)S(1)}, f32[1,512]{1,0:T(1,128)}, u32[]{:S(2)}) copy-start(f32[1,512]{1,0:T(1,128)} %accum_ref.1) | copy-start | bytes 6148
  73.6 23.1 %all-to-all-start.3 = ((bf16[32,32,128]{2,1,0:T(8,128)(2,1)}), bf16[32,32,128]{2,1,0:T(8,128)(2,1)S(1)}, u32[]{:S(2)}, u32[]{:S(2)}) async-start(bf16[32,32,128]{2,1,0:T(8,128)(2,1)} %shard_map.158), calls=%async_computation.3 | async-start | bytes 524288 | tf_op jit(solution)/shard_map/all_to_all | solution.py:287
  80.1 10.0 %collective-permute-start.4 = (f32[520,128]{1,0:T(8,128)S(1)}, f32[520,128]{1,0:T(8,128)S(1)}, u32[]{:S(2)}, u32[]{:S(2)}) collective-permute-start(f32[520,128]{1,0:T(8,128)S(1)} %shard_map.156.m0_ref), channel_id=1, source_target_pairs={{0,64},{64,128},{128,192},{192,0},{1,65},{65,129},{129,193},{193,1... | collective-permute-start | bytes 798728 | tf_op jit(solution)/shard_map/ppermute | solution.py:278
  81.0 13.4 %collective-permute-start.5 = (f32[520,128]{1,0:T(8,128)S(1)}, f32[520,128]{1,0:T(8,128)S(1)}, u32[]{:S(2)}, u32[]{:S(2)}) collective-permute-start(f32[520,128]{1,0:T(8,128)S(1)} %shard_map.156.m0_ref), channel_id=1, source_target_pairs={{0,128},{64,192},{128,0},{192,64},{1,129},{65,193},{129,1},{193,65... | collective-permute-start | bytes 798728 | tf_op jit(solution)/shard_map/ppermute | solution.py:278
  84.3 10.1 %collective-permute-start.6 = (f32[520,128]{1,0:T(8,128)S(1)}, f32[520,128]{1,0:T(8,128)S(1)}, u32[]{:S(2)}, u32[]{:S(2)}) collective-permute-start(f32[520,128]{1,0:T(8,128)S(1)} %shard_map.156.m0_ref), channel_id=1, source_target_pairs={{0,192},{64,0},{128,64},{192,128},{1,193},{65,1},{129,65},{193,129... | collective-permute-start | bytes 798728 | tf_op jit(solution)/shard_map/ppermute | solution.py:278
  96.8 1.5 %collective-permute-start.7 = (bf16[32,32,128]{2,1,0:T(8,128)(2,1)S(1)}, bf16[32,32,128]{2,1,0:T(8,128)(2,1)S(1)}, u32[]{:S(2)}, u32[]{:S(2)}) collective-permute-start(bf16[32,32,128]{2,1,0:T(8,128)(2,1)S(1)} %all-to-all-done.3.mine_ref), channel_id=1, source_target_pairs={{0,1},{1,0},{2,3},{3,2},{4,5},{5,4},{6,7},{7,6},{8,9},{9,8},{10,11... | collective-permute-start | bytes 786440 | tf_op jit(solution)/shard_map/ppermute | solution.py:283
where the time goes:
time: 101 us; the launch traced here: 99.4 us
  starting transfers between devices  41 us (41%)
  waiting for transfers between devices  40.7 us (40%)
  Pallas kernels  12.4 us (12%)
  local copies, waits for them, and re-layouts  4.43 us (4%)
    all_to_all x4, starting transfers between devices, exchange(): return lax.all_to_all(x, axes, 0, 0, tiled=True)  30.3 us
    all_to_all x4, waiting for transfers between devices, exchange(): return lax.all_to_all(x, axes, 0, 0, tiled=True)  25.6 us
    ppermute x6, waiting for transfers between devices, over_groups(): lax.ppermute(x, 'grp', [(g, (g + o) % N_GRP) for g in range(N_GRP)])  12.5 us
    pallas_call x14, Pallas kernels, call(): pl.pallas_call(kernel, out_shape=outs, in_specs=specs, out_specs=[VM] * l...  12.4 us
    ppermute x6, starting transfers between devices, over_groups(): lax.ppermute(x, 'grp', [(g, (g + o) % N_GRP) for g in range(N_GRP)])  10.5 us
    unnamed x26, local copies, waits for them, and re-layouts  4.43 us
    ppermute x2, waiting for transfers between devices, other_core(): return lax.ppermute(x, 'row_2', [(0, 1), (1, 0)])  2.65 us
  transfers between devices with their start and end apart: 12, of which 10 were waited for; matrix products, arithmetic and copies ran while one was open for 0% of the time, Pallas kernels for 5%

commit v1 on v0

--- a/solution.py
+++ b/solution.py
@@ -65,13 +65,16 @@
     return shard, idx & (SPAN - 1)
 
 
-def ids_kernel(idx_ref, ids_ref, rank_ref):
-    shard, row = shard_and_row(idx_ref)
+def ranks(shard, row):
     in_shard = ones_where(iota((N_ROW, NNZ), 0) == shard)
     at_row = ones_where(iota((SPAN, NNZ), 0) == row)
     used = dot(in_shard, at_row, 1, 1) > 0.5
     before = ones_where(iota((SPAN, SPAN), 0) < iota((SPAN, SPAN), 1))
-    rank = dot(ones_where(used), before)
+    return in_shard, used, dot(ones_where(used), before)
+
+
+def ids_kernel(idx_ref, ids_ref):
+    _, used, rank = ranks(*shard_and_row(idx_ref))
     column = iota((N_ROW, SPAN), 1).astype(F32)
     lane = iota((N_ROW, D), 1)
     ids = jnp.zeros((N_ROW, D), F32)
@@ -81,13 +84,12 @@
         )
         ids = jnp.where(lane == k, mine, ids)
     ids_ref[...] = ids.astype(I32)
-    rank_ref[...] = rank.astype(BF16)
-
-
-def counts_kernel(idx_ref, len_ref, rank_ref, use_ref, use_t_ref):
+
+
+def counts_kernel(idx_ref, len_ref, use_ref, use_t_ref):
     shard, row = shard_and_row(idx_ref)
-    in_shard = ones_where(iota((N_ROW, NNZ), 0) == shard)
-    rank_at = dot(rank_ref[...], in_shard, 0, 0)
+    in_shard, _, rank = ranks(shard, row)
+    rank_at = dot(rank.astype(BF16), in_shard, 0, 0)
     rank = jnp.sum(jnp.where(iota((SPAN, NNZ), 0) == row, rank_at, 0.0), axis=0, keepdims=True)
     slot = shard * CAP + rank.astype(I32)
     at_slot = ones_where(iota((SLOTS, NNZ), 0) == slot)
@@ -208,54 +210,50 @@
     top_ref[...] = jnp.broadcast_to(top.astype(BF16)[None], (N_ROW // 2, 32, D))
 
 
-def owner_kernel(master_ref, accum_ref, out_ref):
-    out_ref[0:QUARTER, :] = master_ref[...]
-    line = iota((8, D), 0)
-    accum = jnp.zeros((8, D), F32)
-    for q in range(4):
-        accum = jnp.where(line == q, accum_ref[:, q * BLOCK : (q + 1) * BLOCK], accum)
-    out_ref[QUARTER : QUARTER + 8, :] = accum
-
-
 def update_kernel(
-    me_ref, x0_ref, x1_ref, x2_ref, x3_ref, m0_ref, m1_ref, m2_ref, m3_ref,
-    new_master_ref, new_accum_ref, serving_ref, scale_ref, by_group, grads,
+    me_ref, x0_ref, x1_ref, x2_ref, x3_ref, master_ref, accum_ref,
+    new_master_ref, new_accum_ref, coded_ref, by_group,
 ):
     me = me_ref[0]
     for o, ref in enumerate((x0_ref, x1_ref, x2_ref, x3_ref)):
         by_group[(me - o) & 3] = ref[...]
-    grads[...] = jnp.zeros((16, BLOCK, D), F32)
-    for g in range(N_GRP):
-        hot = by_group[g, SPAN + 32 : SPAN + 48, :].astype(F32).astype(I32)
-        for j in range(2):
-            number = jnp.clip(hot[0, j], 0, 15)
-            grads[number] = grads[number] + by_group[g, j * BLOCK : (j + 1) * BLOCK, :].astype(F32)
+    hot = [by_group[g, SPAN + 32 : SPAN + 48, :].astype(F32)[0:1, :] for g in range(N_GRP)]
     a, b = iota((BLOCK, BLOCK), 0), iota((BLOCK, BLOCK), 1)
     diagonal = a == b
-    lane = iota((1, 16), 1)
-    scales = jnp.zeros((1, 16), F32)
-    for o, ref in enumerate((m0_ref, m1_ref, m2_ref, m3_ref)):
-        for q in range(4):
-            number = ((me - o) & 3) * 4 + q
-            grad = grads[number]
-            accum = jnp.broadcast_to(ref[QUARTER + q : QUARTER + q + 1, :], (BLOCK, BLOCK))
-            state = jnp.sum(jnp.where(diagonal, accum, 0.0), axis=1, keepdims=True) + jnp.mean(
-                grad * grad, axis=1, keepdims=True
-            )
-            weights = ref[q * BLOCK : (q + 1) * BLOCK, :] - grad * (LR / jnp.sqrt(state))
-            if o == 0:
-                new_master_ref[q * BLOCK : (q + 1) * BLOCK, :] = weights
-                new_accum_ref[:, q * BLOCK : (q + 1) * BLOCK] = jnp.sum(
-                    jnp.where(diagonal, jnp.broadcast_to(state, (BLOCK, BLOCK)), 0.0),
-                    axis=0,
-                    keepdims=True,
-                )
-            largest = jnp.max(jnp.max(jnp.abs(weights), axis=0, keepdims=True), axis=1, keepdims=True)
-            scale = (largest + 1e-06).astype(BF16).astype(F32)
-            at = pl.ds(pl.multiple_of(number * BLOCK, BLOCK), BLOCK)
-            serving_ref[at, :] = (weights / scale).astype(BF16)
-            scales = jnp.where(lane == number, scale, scales)
-    scale_ref[...] = scales.astype(BF16)
+    lane = iota((16, D), 1)
+    scale_row = jnp.zeros((16, D), F32)
+    for q in range(4):
+        grad = jnp.zeros((BLOCK, D), F32)
+        number = (me * 4 + q).astype(F32)
+        for g in range(N_GRP):
+            for j in range(2):
+                block = by_group[g, j * BLOCK : (j + 1) * BLOCK, :].astype(F32)
+                grad = grad + jnp.where(hot[g][:, j : j + 1] == number, block, 0.0)
+        at = pl.ds(q * BLOCK, BLOCK)
+        accum = jnp.broadcast_to(accum_ref[:, q * BLOCK : (q + 1) * BLOCK], (BLOCK, BLOCK))
+        state = jnp.sum(jnp.where(diagonal, accum, 0.0), axis=1, keepdims=True) + jnp.mean(
+            grad * grad, axis=1, keepdims=True
+        )
+        new_accum_ref[:, q * BLOCK : (q + 1) * BLOCK] = jnp.sum(
+            jnp.where(diagonal, jnp.broadcast_to(state, (BLOCK, BLOCK)), 0.0), axis=0, keepdims=True
+        )
+        weights = master_ref[at, :] - grad * (LR / jnp.sqrt(state))
+        new_master_ref[at, :] = weights
+        largest = jnp.max(jnp.max(jnp.abs(weights), axis=0, keepdims=True), axis=1, keepdims=True)
+        scale = (largest + 1e-06).astype(BF16).astype(F32)
+        coded_ref[at, :] = (weights / scale).astype(BF16)
+        scale_row = jnp.where(lane == me * 4 + q, scale, scale_row)
+    coded_ref[pl.ds(QUARTER, 16), :] = scale_row.astype(BF16)
+
+
+def fresh_kernel(me_ref, s0_ref, s1_ref, s2_ref, s3_ref, serving_ref, scale_ref):
+    me = me_ref[0]
+    scales = jnp.zeros((16, D), F32)
+    for o, ref in enumerate((s0_ref, s1_ref, s2_ref, s3_ref)):
+        start = pl.multiple_of(((me - o) & 3) * QUARTER, QUARTER)
+        serving_ref[pl.ds(start, QUARTER), :] = ref[0:QUARTER, :]
+        scales = scales + ref[QUARTER : QUARTER + 16, :].astype(F32)
+    scale_ref[...] = scales[0:1, 0:16].astype(BF16)
 
 
 def last_kernel(core_ref, mine_ref, other_ref, top_ref):
@@ -292,22 +290,13 @@
 ):
     me = lax.axis_index("grp").astype(I32).reshape(1)
     core = lax.axis_index("row_2").astype(I32).reshape(1)
-    ids, rank = call(
-        ids_kernel,
-        [like((N_ROW, D), I32), like((N_ROW, SPAN), BF16)],
-        [VM],
-        (bag_indices,),
-        1 << 26,
-    )
+    (ids,) = call(ids_kernel, [like((N_ROW, D), I32)], [VM], (bag_indices,), 1 << 26)
     wanted = exchange(ids.reshape(N_ROW, 1, D)).reshape(N_ROW, D)
-    (owner,) = call(
-        owner_kernel, [like((QUARTER + 8, D), F32)], [VM] * 2, (master[0], accum), 1 << 16
-    )
     use, use_t = call(
         counts_kernel,
         [like((BAGS, SLOTS), BF16), like((SLOTS, BAGS), BF16)],
-        [VM] * 3,
-        (bag_indices, bag_lengths, rank),
+        [VM] * 2,
+        (bag_indices, bag_lengths),
         1 << 29,
     )
     (table,) = call(
@@ -328,7 +317,6 @@
     wanted, table, pre, labels_column, w_out_line = lax.optimization_barrier(
         (wanted, table, pre, labels_column, w_out_line)
     )
-    owners = over_groups(owner)
     (rows,) = call(pick_kernel, [like((SLOTS, D), BF16)], [VM] * 2, (wanted, table), 1 << 26)
     fetched = exchange(rows.reshape(N_ROW, CAP, D)).reshape(SLOTS, D)
     (place,) = call(place_kernel, [like((SPAN, SLOTS), BF16)], [VM], (wanted,), 1 << 26)
@@ -368,26 +356,25 @@
         [pltpu.VMEM((N_GRP, 32, D), BF16)],
     )
     top_mine = exchange(top_part, CHIPS)
-    new_master, new_accum, fresh, fresh_scale = call(
+    new_master, new_accum, coded = call(
         update_kernel,
-        [
-            like((QUARTER, D), F32),
-            like((1, QUARTER), F32),
-            like((4 * QUARTER, D), BF16),
-            like((1, 16), BF16),
-        ],
-        [SM] + [VM] * 8,
-        (me, *owned, *owners),
+        [like((QUARTER, D), F32), like((1, QUARTER), F32), like((QUARTER + 16, D), BF16)],
+        [SM] + [VM] * 6,
+        (me, *owned, master[0], accum),
         1 << 22,
-        [pltpu.VMEM((N_GRP, SPAN + 48, D), BF16), pltpu.VMEM((16, BLOCK, D), F32)],
-    )
-    top_mine, fresh_scale = lax.optimization_barrier((top_mine, fresh_scale))
+        [pltpu.VMEM((N_GRP, SPAN + 48, D), BF16)],
+    )
+    quarters = over_groups(coded)
+    fresh, fresh_scale = call(
+        fresh_kernel,
+        [like((4 * QUARTER, D), BF16), like((1, 16), BF16)],
+        [SM] + [VM] * 4,
+        (me, *quarters),
+        1 << 20,
+    )
+    top_other = other_core(top_mine)
     (top_grad,) = call(
-        last_kernel,
-        [like((2 * D, FF), F32)],
-        [SM] + [VM] * 2,
-        (core, top_mine, other_core(top_mine)),
-        1 << 20,
+        last_kernel, [like((2 * D, FF), F32)], [SM] + [VM] * 2, (core, top_mine, top_other), 1 << 20
     )
     return new_master[None], new_accum, fresh, fresh_scale.reshape(16), top_grad
 

time: 101 us -> 107 us (1.059)
  the two profiles are of different devices: /device:TPU:8 before, /device:TPU:1 now
where the time goes in v1:
time: 107 us
  waiting for transfers between devices  42.3 us (40%)
  starting transfers between devices  32.5 us (30%)
  blocking collectives  14.8 us (14%)
  Pallas kernels  11.9 us (11%)
  local copies, waits for them, and re-layouts  4.44 us (4%)
    all_to_all x3, waiting for transfers between devices, exchange(): return lax.all_to_all(x, axes, 0, 0, tiled=True)  27.1 us
    all_to_all x3, starting transfers between devices, exchange(): return lax.all_to_all(x, axes, 0, 0, tiled=True)  23.2 us
    all_to_all x1, blocking collectives, exchange(): return lax.all_to_all(x, axes, 0, 0, tiled=True)  14.8 us
    ppermute x6, waiting for transfers between devices, over_groups(): lax.ppermute(x, 'grp', [(g, (g + o) % N_GRP) for g in range(N_GRP)])  14.3 us
    pallas_call x14, Pallas kernels, call(): pl.pallas_call(kernel, out_shape=outs, in_specs=specs, out_specs=[VM] * l...  11.9 us
    ppermute x6, starting transfers between devices, over_groups(): lax.ppermute(x, 'grp', [(g, (g + o) % N_GRP) for g in range(N_GRP)])  5.15 us
    unnamed x26, local copies, waits for them, and re-layouts  4.44 us
    ppermute x2, starting transfers between devices, other_core(): return lax.ppermute(x, 'row_2', [(0, 1), (1, 0)])  4.15 us
  transfers between devices with their start and end apart: 11, of which 10 were waited for; matrix products, arithmetic and copies ran while one was open for 0% of the time, Pallas kernels for 5%

profile of v1, /device:TPU:1, one launch (start us, length us, event | category | flops | bytes accessed | tf_op | source)
XLA Modules:
  0.0 106.7 jit_solution(7649695409090118368)
XLA Ops:
  0.6 0.0 copy-start
  0.6 0.0 copy-start.10
  0.7 0.7 copy-done.10
  1.4 1.2 %shard_map.146 = s32[64,128]{1,0:T(8,128)} custom-call(s32[1,1024]{1,0:T(1,128)S(1)} %copy-done.10), custom_call_target="tpu_custom_call" | custom-call | flops 67108864 | bytes 36864 | tf_op jit(solution)/shard_map/pallas_call | solution.py:49
  2.5 13.1 %all-to-all-start = ((s32[64,1,128]{2,1,0:T(1,128)}), s32[64,1,128]{2,1,0:T(1,128)S(1)}, u32[]{:S(2)}, u32[]{:S(2)}) async-start(s32[64,1,128]{2,1,0:T(1,128)} %bitcast.3), calls=%async_computation | async-start | bytes 65536 | tf_op jit(solution)/shard_map/all_to_all | solution.py:285
  15.7 0.0 copy-start.1
  15.7 1.0 copy-done.1
  16.7 0.0 copy-start.6
  16.7 0.7 copy-done.6
  17.4 0.0 copy-start.9
  17.4 0.7 copy-done.9
  18.1 0.0 copy-start.2
  18.1 0.0 copy-start.4
  18.1 0.8 shard_map.147.table_ref
  18.9 0.0 copy-start.8
  18.9 0.0 copy-done
  18.9 0.0 copy-done.2
  18.9 0.0 copy-done.4
  18.9 0.6 copy-done.8
  19.6 0.3 shard_map.148
  19.8 5.1 %all-to-all-done = s32[64,1,128]{2,1,0:T(1,128)S(1)} async-done(((s32[64,1,128]{2,1,0:T(1,128)}), s32[64,1,128]{2,1,0:T(1,128)S(1)}, u32[]{:S(2)}, u32[]{:S(2)}) %all-to-all-start) | async-done | bytes 32800 | tf_op jit(solution)/shard_map/all_to_all | solution.py:285
  24.9 1.1 %shard_map.149 = bf16[512,128]{1,0:T(8,128)(2,1)} custom-call(s32[64,128]{1,0:T(8,128)S(1)} %bitcast.20, bf16[256,128]{1,0:T(8,128)(2,1)S(1)} %shard_map.147.table_ref), custom_call_target="tpu_custom_call" | custom-call | flops 67108864 | bytes 229376 | tf_op jit(solution)/shard_map/pallas_call | solution.py:49
  26.0 5.2 %all-to-all-start.1 = ((bf16[64,8,128]{2,1,0:T(8,128)(2,1)}), bf16[64,8,128]{2,1,0:T(8,128)(2,1)S(1)}, u32[]{:S(2)}, u32[]{:S(2)}) async-start(bf16[64,8,128]{2,1,0:T(8,128)(2,1)} %bitcast.8), calls=%async_computation.1 | async-start | bytes 262144 | tf_op jit(solution)/shard_map/all_to_all | solution.py:285
  31.3 0.0 copy-start.11
  31.3 0.0 copy-start.12
  31.3 0.7 copy-done.11
  32.0 0.0 copy-done.12
  32.0 1.9 %shard_map.150 = (bf16[256,512]{1,0:T(8,128)(2,1)S(1)}, bf16[512,256]{1,0:T(8,128)(2,1)S(1)}) custom-call(s32[1,1024]{1,0:T(1,128)S(1)} %copy-done.11, s32[1,256]{1,0:T(1,128)S(1)} %copy-done.12), custom_call_target="tpu_custom_call" | custom-call | flops 536870912 | bytes 529408 | tf_op jit(solution)/shard_map/pallas_call | solution.py:49
  33.9 7.7 %all-to-all-done.1 = bf16[64,8,128]{2,1,0:T(8,128)(2,1)S(1)} async-done(((bf16[64,8,128]{2,1,0:T(8,128)(2,1)}), bf16[64,8,128]{2,1,0:T(8,128)(2,1)S(1)}, u32[]{:S(2)}, u32[]{:S(2)}) %all-to-all-start.1) | async-done | bytes 131104 | tf_op jit(solution)/shard_map/all_to_all | solution.py:285
  41.6 1.4 %shard_map.151 = (bf16[64,16,128]{2,1,0:T(8,128)(2,1)S(1)}, f32[64,16,128]{2,1,0:T(8,128)S(1)}, f32[256,128]{1,0:T(8,128)S(1)}) custom-call(s32[1]{0:T(128)} %bitcast.1.core_ref, bf16[512,128]{1,0:T(8,128)(2,1)S(1)} %bitcast.17, bf16[256,512]{1,0:T(8,128)(2,1)S(1)} %get-tuple-element.28.use_ref, bf16[256,128]{1,0:T(8,128)(2,1)S(1)} %copy-done.2, ...), custom_call_target="tpu_custom_call" | custom-call | flops 536870912 | bytes 3084292 | tf_op jit(solution)/shard_map/pallas_call | solution.py:49
  43.0 0.5 collective-permute-start
  43.5 0.3 shard_map.152
  43.8 0.9 collective-permute-done.given_ref
  44.7 0.8 shard_map.153
  45.5 4.9 %all-to-all-start.2 = ((bf16[64,24,128]{2,1,0:T(8,128)(2,1)}), bf16[64,24,128]{2,1,0:T(8,128)(2,1)S(1)}, u32[]{:S(2)}, u32[]{:S(2)}) async-start(bf16[64,24,128]{2,1,0:T(8,128)(2,1)} %shard_map.153), calls=%async_computation.2 | async-start | bytes 786432 | tf_op jit(solution)/shard_map/all_to_all | solution.py:285
  50.4 0.3 shard_map.154.place_ref
  50.7 0.0 copy-start.7
  50.7 14.3 %all-to-all-done.2 = bf16[64,24,128]{2,1,0:T(8,128)(2,1)S(1)} async-done(((bf16[64,24,128]{2,1,0:T(8,128)(2,1)}), bf16[64,24,128]{2,1,0:T(8,128)(2,1)S(1)}, u32[]{:S(2)}, u32[]{:S(2)}) %all-to-all-start.2) | async-done | bytes 393248 | tf_op jit(solution)/shard_map/all_to_all | solution.py:285
  64.9 0.0 copy-done.7
  64.9 0.8 shard_map.155.x0_ref
  65.7 2.5 %collective-permute-start.3 = (bf16[304,128]{1,0:T(8,128)(2,1)S(1)}, bf16[304,128]{1,0:T(8,128)(2,1)S(1)}, u32[]{:S(2)}, u32[]{:S(2)}) collective-permute-start(bf16[304,128]{1,0:T(8,128)(2,1)S(1)} %shard_map.155.x0_ref), channel_id=1, source_target_pairs={{0,192},{64,0},{128,64},{192,128},{1,193},{65,1},{129,65},{193,129... | collective-permute-start | bytes 233480 | tf_op jit(solution)/shard_map/ppermute | solution.py:276
  68.3 0.5 collective-permute-start.2
  68.8 0.6 collective-permute-start.1
  69.4 0.3 collective-permute-done.3.x3_ref
  69.7 3.4 %collective-permute-done.2.x2_ref = bf16[304,128]{1,0:T(8,128)(2,1)S(1)} collective-permute-done((bf16[304,128]{1,0:T(8,128)(2,1)S(1)}, bf16[304,128]{1,0:T(8,128)(2,1)S(1)}, u32[]{:S(2)}, u32[]{:S(2)}) %collective-permute-start.2) | collective-permute-done | bytes 77856 | tf_op jit(solution)/shard_map/ppermute | solution.py:276
  73.1 2.2 %collective-permute-done.1.x1_ref = bf16[304,128]{1,0:T(8,128)(2,1)S(1)} collective-permute-done((bf16[304,128]{1,0:T(8,128)(2,1)S(1)}, bf16[304,128]{1,0:T(8,128)(2,1)S(1)}, u32[]{:S(2)}, u32[]{:S(2)}) %collective-permute-start.1) | collective-permute-done | bytes 77856 | tf_op jit(solution)/shard_map/ppermute | solution.py:276
  75.3 0.0 copy-start.3
  75.3 0.0 copy-start.5
  75.3 14.8 %all_to_all.20.mine_ref = bf16[32,32,128]{2,1,0:T(8,128)(2,1)S(1)} all-to-all(bf16[32,32,128]{2,1,0:T(8,128)(2,1)S(1)} %shard_map.158), channel_id=1, replica_groups=mesh['grp'=4,'row_0'=4,'row_1'=8,'row_2'=2] {'row_0','row_1'}, dimensions={0} | all-to-all | bytes 524288 | tf_op jit(solution)/shard_map/all_to_all | solution.py:285
  90.1 3.7 %collective-permute-start.7 = (bf16[32,32,128]{2,1,0:T(8,128)(2,1)S(1)}, bf16[32,32,128]{2,1,0:T(8,128)(2,1)S(1)}, u32[]{:S(2)}, u32[]{:S(2)}) collective-permute-start(bf16[32,32,128]{2,1,0:T(8,128)(2,1)S(1)} %all_to_all.20.mine_ref), channel_id=1, source_target_pairs={{0,1},{1,0},{2,3},{3,2},{4,5},{5,4},{6,7},{7,6},{8,9},{9,8},{10,11... | collective-permute-start | bytes 786440 | tf_op jit(solution)/shard_map/ppermute | solution.py:281
  93.7 0.0 copy-done.3
  93.7 0.0 copy-done.5
  93.7 1.2 %shard_map.156 = (f32[512,128]{1,0:T(8,128)}, f32[1,512]{1,0:T(1,128)}, bf16[528,128]{1,0:T(8,128)(2,1)S(1)}) custom-call(s32[1]{0:T(128)} %bitcast.me_ref, bf16[304,128]{1,0:T(8,128)(2,1)S(1)} %shard_map.155.x0_ref, bf16[304,128]{1,0:T(8,128)(2,1)S(1)} %collective-permute-done.1.x1_ref, bf16[304,128]{1,0:T(8,128)(2,1)S(1)} %collective-permute-done.2.x2_ref, ...), custom_call_target="tpu_custom_call" | custom-call | flops 4194304 | bytes 974852 | tf_op jit(solution)/shard_map/pallas_call | solution.py:49
  94.9 0.0 collective-permute-start.6
  94.9 0.2 collective-permute-start.5
  95.1 1.2 %collective-permute-start.4 = (bf16[528,128]{1,0:T(8,128)(2,1)S(1)}, bf16[528,128]{1,0:T(8,128)(2,1)S(1)}, u32[]{:S(2)}, u32[]{:S(2)}) collective-permute-start(bf16[528,128]{1,0:T(8,128)(2,1)S(1)} %get-tuple-element.38.s0_ref), channel_id=1, source_target_pairs={{0,64},{64,128},{128,192},{192,0},{1,65},{65,129},{129,193},{193,1... | collective-permute-start | bytes 405512 | tf_op jit(solution)/shard_map/ppermute | solution.py:276
  96.4 3.7 %collective-permute-done.6.s3_ref = bf16[528,128]{1,0:T(8,128)(2,1)S(1)} collective-permute-done((bf16[528,128]{1,0:T(8,128)(2,1)S(1)}, bf16[528,128]{1,0:T(8,128)(2,1)S(1)}, u32[]{:S(2)}, u32[]{:S(2)}) %collective-permute-start.6) | collective-permute-done | bytes 135200 | tf_op jit(solution)/shard_map/ppermute | solution.py:276
  100.0 1.5 %collective-permute-done.5.s2_ref = bf16[528,128]{1,0:T(8,128)(2,1)S(1)} collective-permute-done((bf16[528,128]{1,0:T(8,128)(2,1)S(1)}, bf16[528,128]{1,0:T(8,128)(2,1)S(1)}, u32[]{:S(2)}, u32[]{:S(2)}) %collective-permute-start.5) | collective-permute-done | bytes 135200 | tf_op jit(solution)/shard_map/ppermute | solution.py:276
  101.6 3.3 %collective-permute-done.4.s1_ref = bf16[528,128]{1,0:T(8,128)(2,1)S(1)} collective-permute-done((bf16[528,128]{1,0:T(8,128)(2,1)S(1)}, bf16[528,128]{1,0:T(8,128)(2,1)S(1)}, u32[]{:S(2)}, u32[]{:S(2)}) %collective-permute-start.4) | collective-permute-done | bytes 135200 | tf_op jit(solution)/shard_map/ppermute | solution.py:276
  104.8 0.8 shard_map.157
  105.7 0.0 collective-permute-done.7.other_ref
  105.7 1.1 shard_map.159
  (1 shorter events, 0.0 us)
Async XLA Ops:
  0.6 18.3 %copy-start = (bf16[256,1024]{1,0:T(8,128)(2,1)S(1)}, bf16[256,1024]{1,0:T(8,128)(2,1)}, u32[]{:S(2)}) copy-start(bf16[256,1024]{1,0:T(8,128)(2,1)} %w_ref.3) | copy-start | bytes 1572868
  0.6 0.7 copy-start.10
  2.5 22.4 %all-to-all-start = ((s32[64,1,128]{2,1,0:T(1,128)}), s32[64,1,128]{2,1,0:T(1,128)S(1)}, u32[]{:S(2)}, u32[]{:S(2)}) async-start(s32[64,1,128]{2,1,0:T(1,128)} %bitcast.3), calls=%async_computation | async-start | bytes 65536 | tf_op jit(solution)/shard_map/all_to_all | solution.py:285
  15.7 1.0 copy-start.1
  16.7 0.7 copy-start.6
  17.4 0.7 copy-start.9
  18.1 0.9 copy-start.2
  18.1 0.9 copy-start.4
  18.9 0.7 copy-start.8
  26.0 15.6 %all-to-all-start.1 = ((bf16[64,8,128]{2,1,0:T(8,128)(2,1)}), bf16[64,8,128]{2,1,0:T(8,128)(2,1)S(1)}, u32[]{:S(2)}, u32[]{:S(2)}) async-start(bf16[64,8,128]{2,1,0:T(8,128)(2,1)} %bitcast.8), calls=%async_computation.1 | async-start | bytes 262144 | tf_op jit(solution)/shard_map/all_to_all | solution.py:285
  31.3 0.7 copy-start.11
  31.3 0.7 copy-start.12
  43.0 1.6 %collective-permute-start = (bf16[64,16,128]{2,1,0:T(8,128)(2,1)S(1)}, bf16[64,16,128]{2,1,0:T(8,128)(2,1)S(1)}, u32[]{:S(2)}, u32[]{:S(2)}) collective-permute-start(bf16[64,16,128]{2,1,0:T(8,128)(2,1)S(1)} %get-tuple-element.33), channel_id=1, source_target_pairs={{0,1},{1,0},{2,3},{3,2},{4,5},{5,4},{6,7},{7,6},{8,9},{9,8},{10,11... | collective-permute-start | bytes 786440 | tf_op jit(solution)/shard_map/ppermute | solution.py:281
  45.5 19.4 %all-to-all-start.2 = ((bf16[64,24,128]{2,1,0:T(8,128)(2,1)}), bf16[64,24,128]{2,1,0:T(8,128)(2,1)S(1)}, u32[]{:S(2)}, u32[]{:S(2)}) async-start(bf16[64,24,128]{2,1,0:T(8,128)(2,1)} %shard_map.153), calls=%async_computation.2 | async-start | bytes 786432 | tf_op jit(solution)/shard_map/all_to_all | solution.py:285
  50.7 14.3 %copy-start.7 = (s32[1,2]{1,0:T(1,128)S(1)}, s32[1,2]{1,0:T(1,128)}, u32[]{:S(2)}) copy-start(s32[1,2]{1,0:T(1,128)} %hot_ref.3) | copy-start | bytes 28
  65.7 4.0 %collective-permute-start.3 = (bf16[304,128]{1,0:T(8,128)(2,1)S(1)}, bf16[304,128]{1,0:T(8,128)(2,1)S(1)}, u32[]{:S(2)}, u32[]{:S(2)}) collective-permute-start(bf16[304,128]{1,0:T(8,128)(2,1)S(1)} %shard_map.155.x0_ref), channel_id=1, source_target_pairs={{0,192},{64,0},{128,64},{192,128},{1,193},{65,1},{129,65},{193,129... | collective-permute-start | bytes 233480 | tf_op jit(solution)/shard_map/ppermute | solution.py:276
  68.3 4.8 %collective-permute-start.2 = (bf16[304,128]{1,0:T(8,128)(2,1)S(1)}, bf16[304,128]{1,0:T(8,128)(2,1)S(1)}, u32[]{:S(2)}, u32[]{:S(2)}) collective-permute-start(bf16[304,128]{1,0:T(8,128)(2,1)S(1)} %shard_map.155.x0_ref), channel_id=1, source_target_pairs={{0,128},{64,192},{128,0},{192,64},{1,129},{65,193},{129,1},{193,65... | collective-permute-start | bytes 233480 | tf_op jit(solution)/shard_map/ppermute | solution.py:276
  68.8 6.4 %collective-permute-start.1 = (bf16[304,128]{1,0:T(8,128)(2,1)S(1)}, bf16[304,128]{1,0:T(8,128)(2,1)S(1)}, u32[]{:S(2)}, u32[]{:S(2)}) collective-permute-start(bf16[304,128]{1,0:T(8,128)(2,1)S(1)} %shard_map.155.x0_ref), channel_id=1, source_target_pairs={{0,64},{64,128},{128,192},{192,0},{1,65},{65,129},{129,193},{193,1... | collective-permute-start | bytes 233480 | tf_op jit(solution)/shard_map/ppermute | solution.py:276
  75.3 18.5 %copy-start.3 = (f32[1,512,128]{2,1,0:T(8,128)S(1)}, f32[1,512,128]{2,1,0:T(8,128)}, u32[]{:S(2)}) copy-start(f32[1,512,128]{2,1,0:T(8,128)} %param.20) | copy-start | bytes 786436
  75.3 18.5 %copy-start.5 = (f32[1,512]{1,0:T(1,128)S(1)}, f32[1,512]{1,0:T(1,128)}, u32[]{:S(2)}) copy-start(f32[1,512]{1,0:T(1,128)} %accum_ref.1) | copy-start | bytes 6148
  90.1 15.6 %collective-permute-start.7 = (bf16[32,32,128]{2,1,0:T(8,128)(2,1)S(1)}, bf16[32,32,128]{2,1,0:T(8,128)(2,1)S(1)}, u32[]{:S(2)}, u32[]{:S(2)}) collective-permute-start(bf16[32,32,128]{2,1,0:T(8,128)(2,1)S(1)} %all_to_all.20.mine_ref), channel_id=1, source_target_pairs={{0,1},{1,0},{2,3},{3,2},{4,5},{5,4},{6,7},{7,6},{8,9},{9,8},{10,11... | collective-permute-start | bytes 786440 | tf_op jit(solution)/shard_map/ppermute | solution.py:281
  94.9 5.1 %collective-permute-start.6 = (bf16[528,128]{1,0:T(8,128)(2,1)S(1)}, bf16[528,128]{1,0:T(8,128)(2,1)S(1)}, u32[]{:S(2)}, u32[]{:S(2)}) collective-permute-start(bf16[528,128]{1,0:T(8,128)(2,1)S(1)} %get-tuple-element.38.s0_ref), channel_id=1, source_target_pairs={{0,192},{64,0},{128,64},{192,128},{1,193},{65,1},{129,65},{193,129... | collective-permute-start | bytes 405512 | tf_op jit(solution)/shard_map/ppermute | solution.py:276
  94.9 6.6 %collective-permute-start.5 = (bf16[528,128]{1,0:T(8,128)(2,1)S(1)}, bf16[528,128]{1,0:T(8,128)(2,1)S(1)}, u32[]{:S(2)}, u32[]{:S(2)}) collective-permute-start(bf16[528,128]{1,0:T(8,128)(2,1)S(1)} %get-tuple-element.38.s0_ref), channel_id=1, source_target_pairs={{0,128},{64,192},{128,0},{192,64},{1,129},{65,193},{129,1},{193,65... | collective-permute-start | bytes 405512 | tf_op jit(solution)/shard_map/ppermute | solution.py:276
  95.1 9.7 %collective-permute-start.4 = (bf16[528,128]{1,0:T(8,128)(2,1)S(1)}, bf16[528,128]{1,0:T(8,128)(2,1)S(1)}, u32[]{:S(2)}, u32[]{:S(2)}) collective-permute-start(bf16[528,128]{1,0:T(8,128)(2,1)S(1)} %get-tuple-element.38.s0_ref), channel_id=1, source_target_pairs={{0,64},{64,128},{128,192},{192,0},{1,65},{65,129},{129,193},{193,1... | collective-permute-start | bytes 405512 | tf_op jit(solution)/shard_map/ppermute | solution.py:276

commit v2 on v1

--- a/solution.py
+++ b/solution.py
@@ -122,18 +122,23 @@
         table_ref[j * BLOCK : (j + 1) * BLOCK, :] = (buf[j].astype(F32) * own).astype(BF16)
 
 
-def pick_kernel(ids_ref, table_ref, rows_ref):
+def pick_kernel(core_ref, ids_ref, table_ref, other_ref, rows_ref):
     owner = ones_where(lax.shift_right_logical(iota((SLOTS, N_ROW), 0), 3) == iota((SLOTS, N_ROW), 1))
     spread = dot(owner, ids_ref[...].astype(F32).astype(BF16))
     mine = iota((SLOTS, D), 1) == (iota((SLOTS, D), 0) & (CAP - 1))
     column = jnp.sum(jnp.where(mine, spread, 0.0), axis=1, keepdims=True).astype(I32)
-    onehot = ones_where(iota((SLOTS, SPAN), 1) == column)
-    rows_ref[...] = dot(onehot, table_ref[...]).astype(BF16)
-
-
-def place_kernel(ids_ref, place_ref):
-    owner = ones_where(lax.shift_right_logical(iota((SLOTS, N_ROW), 0), 3) == iota((SLOTS, N_ROW), 1))
-    spread = dot(ids_ref[...].astype(F32).astype(BF16), owner, 0, 1)
+    here = lax.shift_right_logical(iota((SLOTS, SPAN), 0), 3) & 1 == core_ref[0]
+    match = iota((SLOTS, SPAN), 1) == column
+    rows = dot(ones_where(match & here), table_ref[...])
+    rows_ref[...] = (rows + dot(ones_where(match & ~here), other_ref[...])).astype(BF16)
+
+
+def place_kernel(core_ref, ids_ref, other_ref, place_ref):
+    slot = iota((SLOTS, N_ROW), 0)
+    line = lax.shift_right_logical(slot, 4) * 2 + core_ref[0] == iota((SLOTS, N_ROW), 1)
+    here = lax.shift_right_logical(slot, 3) & 1 == core_ref[0]
+    spread = dot(ids_ref[...].astype(F32).astype(BF16), ones_where(line & here), 0, 1)
+    spread = spread + dot(other_ref[...].astype(F32).astype(BF16), ones_where(line & ~here), 0, 1)
     mine = iota((D, SLOTS), 0) == (iota((D, SLOTS), 1) & (CAP - 1))
     line = jnp.sum(jnp.where(mine, spread, 0.0), axis=0, keepdims=True).astype(I32)
     place_ref[...] = ones_where(iota((SPAN, SLOTS), 0) == line)
@@ -272,9 +277,10 @@
 
 
 def over_groups(x):
-    return [x] + [
-        lax.ppermute(x, "grp", [(g, (g + o) % N_GRP) for g in range(N_GRP)]) for o in (1, 2, 3)
-    ]
+    parts = [x]
+    for o in (1, 2, 3):
+        parts.append(lax.ppermute(x, "grp", [(g, (g + o) % N_GRP) for g in range(N_GRP)]))
+    return parts
 
 
 def other_core(x):
@@ -291,7 +297,7 @@
     me = lax.axis_index("grp").astype(I32).reshape(1)
     core = lax.axis_index("row_2").astype(I32).reshape(1)
     (ids,) = call(ids_kernel, [like((N_ROW, D), I32)], [VM], (bag_indices,), 1 << 26)
-    wanted = exchange(ids.reshape(N_ROW, 1, D)).reshape(N_ROW, D)
+    wanted = exchange(ids.reshape(N_ROW // 2, 2, D), CHIPS).reshape(N_ROW, D)
     use, use_t = call(
         counts_kernel,
         [like((BAGS, SLOTS), BF16), like((SLOTS, BAGS), BF16)],
@@ -314,12 +320,26 @@
         (dense_act, w_top, labels.reshape(1, BAGS), w_out.reshape(1, FF)),
         1 << 27,
     )
-    wanted, table, pre, labels_column, w_out_line = lax.optimization_barrier(
-        (wanted, table, pre, labels_column, w_out_line)
-    )
-    (rows,) = call(pick_kernel, [like((SLOTS, D), BF16)], [VM] * 2, (wanted, table), 1 << 26)
-    fetched = exchange(rows.reshape(N_ROW, CAP, D)).reshape(SLOTS, D)
-    (place,) = call(place_kernel, [like((SPAN, SLOTS), BF16)], [VM], (wanted,), 1 << 26)
+    other_table = other_core(table)
+    wanted, table, other_table, pre, labels_column, w_out_line = lax.optimization_barrier(
+        (wanted, table, other_table, pre, labels_column, w_out_line)
+    )
+    (rows,) = call(
+        pick_kernel,
+        [like((SLOTS, D), BF16)],
+        [SM] + [VM] * 3,
+        (core, wanted, table, other_table),
+        1 << 26,
+    )
+    fetched = exchange(rows.reshape(N_ROW // 2, 2 * CAP, D), CHIPS).reshape(SLOTS, D)
+    other_wanted = other_core(wanted)
+    (place,) = call(
+        place_kernel,
+        [like((SPAN, SLOTS), BF16)],
+        [SM] + [VM] * 2,
+        (core, wanted, other_wanted),
+        1 << 26,
+    )
     give, keep, pooled_grad = call(
         step_kernel,
         [like((N_ROW, 16, D), BF16), like((N_ROW, 16, D), F32), like((BAGS, D), F32)],

time: 107 us -> 109 us (1.019)
  waiting for transfers between devices: 42.3 us -> 43.8 us
  local copies, waits for them, and re-layouts: 4.44 us -> 3.1 us
  starting transfers between devices: 32.5 us -> 33.6 us
    ppermute x2 -> x4, starting transfers between devices: 4.15 us -> 10.4 us  [other_core(): return lax.ppermute(x, 'row_2', [(0, 1), (1, 0)])]
    all_to_all x3, starting transfers between devices: 23.2 us -> 18.1 us  [exchange(): return lax.all_to_all(x, axes, 0, 0, tiled=True)]
    unnamed x26 -> x24, local copies, waits for them, and re-layouts: 4.44 us -> 3.1 us
  transfers between devices with their start and end apart: 11 -> 13, of which waited for: 10 -> 11; matrix products, arithmetic and copies ran while one was open for 0% -> 0% of each run, Pallas kernels for 5% -> 6%
where the time goes in v2:
time: 109 us; the launch traced here: 108 us
  waiting for transfers between devices  43.8 us (40%)
  starting transfers between devices  33.6 us (31%)
  blocking collectives  14.8 us (14%)
  Pallas kernels  12.1 us (11%)
  local copies, waits for them, and re-layouts  3.1 us (3%)
    all_to_all x3, waiting for transfers between devices, exchange(): return lax.all_to_all(x, axes, 0, 0, tiled=True)  27.8 us
    all_to_all x3, starting transfers between devices, exchange(): return lax.all_to_all(x, axes, 0, 0, tiled=True)  18.1 us
    all_to_all x1, blocking collectives, exchange(): return lax.all_to_all(x, axes, 0, 0, tiled=True)  14.8 us
    ppermute x6, waiting for transfers between devices, over_groups(): lax.ppermute(x, 'grp', [(g, (g + o) % N_GRP) for g in range(N_GRP)])  14.3 us
    pallas_call x14, Pallas kernels, call(): pl.pallas_call(kernel, out_shape=outs, in_specs=specs, out_specs=[VM] * l...  12.1 us
    ppermute x4, starting transfers between devices, other_core(): return lax.ppermute(x, 'row_2', [(0, 1), (1, 0)])  10.4 us
    ppermute x6, starting transfers between devices, over_groups(): lax.ppermute(x, 'grp', [(g, (g + o) % N_GRP) for g in range(N_GRP)])  5.14 us
    unnamed x24, local copies, waits for them, and re-layouts  3.1 us
  transfers between devices with their start and end apart: 13, of which 11 were waited for; matrix products, arithmetic and copies ran while one was open for 0% of the time, Pallas kernels for 6%

profile of v2, /device:TPU:1, one launch (start us, length us, event | category | flops | bytes accessed | tf_op | source)
XLA Modules:
  0.0 108.1 jit_solution(15240924630851024908)
XLA Ops:
  0.6 0.0 copy-start
  0.6 0.0 copy-start.1
  0.7 1.1 %copy-done.1 = bf16[2048,128]{1,0:T(8,128)(2,1)S(1)} copy-done((bf16[2048,128]{1,0:T(8,128)(2,1)S(1)}, bf16[2048,128]{1,0:T(8,128)(2,1)}, u32[]{:S(2)}) %copy-start.1) | copy-done | bytes 524312
  1.7 0.0 copy-start.6
  1.7 0.7 copy-done.6
  2.4 0.0 copy-start.9
  2.4 0.7 copy-done.9
  3.1 0.0 copy-start.10
  3.1 0.8 shard_map.147.table_ref
  3.9 3.3 %collective-permute-start = (bf16[256,128]{1,0:T(8,128)(2,1)S(1)}, bf16[256,128]{1,0:T(8,128)(2,1)S(1)}, u32[]{:S(2)}, u32[]{:S(2)}) collective-permute-start(bf16[256,128]{1,0:T(8,128)(2,1)S(1)} %shard_map.147.table_ref), channel_id=1, source_target_pairs={{0,1},{1,0},{2,3},{3,2},{4,5},{5,4},{6,7},{7,6},{8,9},{9,8},{10,11... | collective-permute-start | bytes 196616 | tf_op jit(solution)/shard_map/ppermute | solution.py:287
  7.2 0.0 copy-done.10
  7.2 1.2 %shard_map.146 = s32[64,128]{1,0:T(8,128)} custom-call(s32[1,1024]{1,0:T(1,128)S(1)} %copy-done.10), custom_call_target="tpu_custom_call" | custom-call | flops 67108864 | bytes 36864 | tf_op jit(solution)/shard_map/pallas_call | solution.py:49
  8.3 0.0 copy-start.2
  8.3 9.6 %all-to-all-start = ((s32[32,2,128]{2,1,0:T(2,128)}), s32[32,2,128]{2,1,0:T(2,128)S(1)}, u32[]{:S(2)}, u32[]{:S(2)}) async-start(s32[32,2,128]{2,1,0:T(2,128)} %bitcast.2), calls=%async_computation | async-start | bytes 65536 | tf_op jit(solution)/shard_map/all_to_all | solution.py:291
  18.0 0.0 copy-start.4
  18.0 0.0 copy-start.8
  18.0 0.0 copy-done
  18.0 0.0 copy-done.2
  18.0 0.6 copy-done.4
  18.7 0.0 copy-done.8
  18.7 0.3 shard_map.148
  19.0 7.8 %all-to-all-done = s32[32,2,128]{2,1,0:T(2,128)S(1)} async-done(((s32[32,2,128]{2,1,0:T(2,128)}), s32[32,2,128]{2,1,0:T(2,128)S(1)}, u32[]{:S(2)}, u32[]{:S(2)}) %all-to-all-start) | async-done | bytes 32800 | tf_op jit(solution)/shard_map/all_to_all | solution.py:291
  26.7 0.0 collective-permute-done.other_ref
  26.7 1.2 %shard_map.149 = bf16[512,128]{1,0:T(8,128)(2,1)} custom-call(s32[1]{0:T(128)} %bitcast.1.core_ref, s32[64,128]{1,0:T(8,128)S(1)} %bitcast.17, bf16[256,128]{1,0:T(8,128)(2,1)S(1)} %shard_map.147.table_ref, bf16[256,128]{1,0:T(8,128)(2,1)S(1)} %collective-permute-done.other_ref), custom_call_target="tpu_custom_call" | custom-call | flops 67108864 | bytes 294916 | tf_op jit(solution)/shard_map/pallas_call | solution.py:49
  27.9 0.0 copy-start.11
  27.9 4.0 %all-to-all-start.1 = ((bf16[32,16,128]{2,1,0:T(8,128)(2,1)}), bf16[32,16,128]{2,1,0:T(8,128)(2,1)S(1)}, u32[]{:S(2)}, u32[]{:S(2)}) async-start(bf16[32,16,128]{2,1,0:T(8,128)(2,1)} %bitcast.7), calls=%async_computation.1 | async-start | bytes 262144 | tf_op jit(solution)/shard_map/all_to_all | solution.py:291
  31.9 0.0 copy-done.11
  31.9 1.9 %shard_map.150 = (bf16[256,512]{1,0:T(8,128)(2,1)S(1)}, bf16[512,256]{1,0:T(8,128)(2,1)S(1)}) custom-call(s32[1,1024]{1,0:T(1,128)S(1)} %copy-done.10, s32[1,256]{1,0:T(1,128)S(1)} %copy-done.11), custom_call_target="tpu_custom_call" | custom-call | flops 536870912 | bytes 529408 | tf_op jit(solution)/shard_map/pallas_call | solution.py:49
  33.8 7.2 %all-to-all-done.1 = bf16[32,16,128]{2,1,0:T(8,128)(2,1)S(1)} async-done(((bf16[32,16,128]{2,1,0:T(8,128)(2,1)}), bf16[32,16,128]{2,1,0:T(8,128)(2,1)S(1)}, u32[]{:S(2)}, u32[]{:S(2)}) %all-to-all-start.1) | async-done | bytes 131104 | tf_op jit(solution)/shard_map/all_to_all | solution.py:291
  41.1 1.4 %shard_map.151 = (bf16[64,16,128]{2,1,0:T(8,128)(2,1)S(1)}, f32[64,16,128]{2,1,0:T(8,128)S(1)}, f32[256,128]{1,0:T(8,128)S(1)}) custom-call(s32[1]{0:T(128)} %bitcast.1.core_ref, bf16[512,128]{1,0:T(8,128)(2,1)S(1)} %bitcast.15, bf16[256,512]{1,0:T(8,128)(2,1)S(1)} %get-tuple-element.30.use_ref, bf16[256,128]{1,0:T(8,128)(2,1)S(1)} %copy-done.2, ...), custom_call_target="tpu_custom_call" | custom-call | flops 536870912 | bytes 3084292 | tf_op jit(solution)/shard_map/pallas_call | solution.py:49
  42.5 2.7 %collective-permute-start.1 = (bf16[64,16,128]{2,1,0:T(8,128)(2,1)S(1)}, bf16[64,16,128]{2,1,0:T(8,128)(2,1)S(1)}, u32[]{:S(2)}, u32[]{:S(2)}) collective-permute-start(bf16[64,16,128]{2,1,0:T(8,128)(2,1)S(1)} %get-tuple-element.35), channel_id=1, source_target_pairs={{0,1},{1,0},{2,3},{3,2},{4,5},{5,4},{6,7},{7,6},{8,9},{9,8},{10,11... | collective-permute-start | bytes 786440 | tf_op jit(solution)/shard_map/ppermute | solution.py:287
  45.2 0.3 shard_map.152
  45.5 0.9 collective-permute-done.1.given_ref
  46.4 0.8 shard_map.153
  47.2 4.4 %all-to-all-start.2 = ((bf16[64,24,128]{2,1,0:T(8,128)(2,1)}), bf16[64,24,128]{2,1,0:T(8,128)(2,1)S(1)}, u32[]{:S(2)}, u32[]{:S(2)}) async-start(bf16[64,24,128]{2,1,0:T(8,128)(2,1)} %shard_map.153), calls=%async_computation.2 | async-start | bytes 786432 | tf_op jit(solution)/shard_map/all_to_all | solution.py:291
  51.7 0.7 collective-permute-start.2
  52.3 0.9 collective-permute-done.2.other_ref
  53.2 0.4 shard_map.154.place_ref
  53.6 0.0 copy-start.7
  53.6 12.8 %all-to-all-done.2 = bf16[64,24,128]{2,1,0:T(8,128)(2,1)S(1)} async-done(((bf16[64,24,128]{2,1,0:T(8,128)(2,1)}), bf16[64,24,128]{2,1,0:T(8,128)(2,1)S(1)}, u32[]{:S(2)}, u32[]{:S(2)}) %all-to-all-start.2) | async-done | bytes 393248 | tf_op jit(solution)/shard_map/all_to_all | solution.py:291
  66.3 0.0 copy-done.7
  66.3 0.8 shard_map.155.x0_ref
  67.1 2.6 %collective-permute-start.5 = (bf16[304,128]{1,0:T(8,128)(2,1)S(1)}, bf16[304,128]{1,0:T(8,128)(2,1)S(1)}, u32[]{:S(2)}, u32[]{:S(2)}) collective-permute-start(bf16[304,128]{1,0:T(8,128)(2,1)S(1)} %shard_map.155.x0_ref), channel_id=1, source_target_pairs={{0,192},{64,0},{128,64},{192,128},{1,193},{65,1},{129,65},{193,129... | collective-permute-start | bytes 233480 | tf_op jit(solution)/shard_map/ppermute | solution.py:282
  69.6 0.5 collective-permute-start.4
  70.2 0.6 collective-permute-start.3
  70.8 0.3 collective-permute-done.5.x3_ref
  71.1 3.4 %collective-permute-done.4.x2_ref = bf16[304,128]{1,0:T(8,128)(2,1)S(1)} collective-permute-done((bf16[304,128]{1,0:T(8,128)(2,1)S(1)}, bf16[304,128]{1,0:T(8,128)(2,1)S(1)}, u32[]{:S(2)}, u32[]{:S(2)}) %collective-permute-start.4) | collective-permute-done | bytes 77856 | tf_op jit(solution)/shard_map/ppermute | solution.py:282
  74.5 2.2 %collective-permute-done.3.x1_ref = bf16[304,128]{1,0:T(8,128)(2,1)S(1)} collective-permute-done((bf16[304,128]{1,0:T(8,128)(2,1)S(1)}, bf16[304,128]{1,0:T(8,128)(2,1)S(1)}, u32[]{:S(2)}, u32[]{:S(2)}) %collective-permute-start.3) | collective-permute-done | bytes 77856 | tf_op jit(solution)/shard_map/ppermute | solution.py:282
  76.7 0.0 copy-start.3
  76.7 0.0 copy-start.5
  76.7 14.8 %all_to_all.20.mine_ref = bf16[32,32,128]{2,1,0:T(8,128)(2,1)S(1)} all-to-all(bf16[32,32,128]{2,1,0:T(8,128)(2,1)S(1)} %shard_map.158), channel_id=1, replica_groups=mesh['grp'=4,'row_0'=4,'row_1'=8,'row_2'=2] {'row_0','row_1'}, dimensions={0} | all-to-all | bytes 524288 | tf_op jit(solution)/shard_map/all_to_all | solution.py:291
  91.5 3.7 %collective-permute-start.9 = (bf16[32,32,128]{2,1,0:T(8,128)(2,1)S(1)}, bf16[32,32,128]{2,1,0:T(8,128)(2,1)S(1)}, u32[]{:S(2)}, u32[]{:S(2)}) collective-permute-start(bf16[32,32,128]{2,1,0:T(8,128)(2,1)S(1)} %all_to_all.20.mine_ref), channel_id=1, source_target_pairs={{0,1},{1,0},{2,3},{3,2},{4,5},{5,4},{6,7},{7,6},{8,9},{9,8},{10,11... | collective-permute-start | bytes 786440 | tf_op jit(solution)/shard_map/ppermute | solution.py:287
  95.2 0.0 copy-done.3
  95.2 0.0 copy-done.5
  95.2 1.2 %shard_map.156 = (f32[512,128]{1,0:T(8,128)}, f32[1,512]{1,0:T(1,128)}, bf16[528,128]{1,0:T(8,128)(2,1)S(1)}) custom-call(s32[1]{0:T(128)} %bitcast.me_ref, bf16[304,128]{1,0:T(8,128)(2,1)S(1)} %shard_map.155.x0_ref, bf16[304,128]{1,0:T(8,128)(2,1)S(1)} %collective-permute-done.3.x1_ref, bf16[304,128]{1,0:T(8,128)(2,1)S(1)} %collective-permute-done.4.x2_ref, ...), custom_call_target="tpu_custom_call" | custom-call | flops 4194304 | bytes 974852 | tf_op jit(solution)/shard_map/pallas_call | solution.py:49
  96.3 0.0 collective-permute-start.8
  96.3 0.4 collective-permute-start.7
  96.7 1.1 %collective-permute-start.6 = (bf16[528,128]{1,0:T(8,128)(2,1)S(1)}, bf16[528,128]{1,0:T(8,128)(2,1)S(1)}, u32[]{:S(2)}, u32[]{:S(2)}) collective-permute-start(bf16[528,128]{1,0:T(8,128)(2,1)S(1)} %get-tuple-element.40.s0_ref), channel_id=1, source_target_pairs={{0,64},{64,128},{128,192},{192,0},{1,65},{65,129},{129,193},{193,1... | collective-permute-start | bytes 405512 | tf_op jit(solution)/shard_map/ppermute | solution.py:282
  97.8 3.7 %collective-permute-done.8.s3_ref = bf16[528,128]{1,0:T(8,128)(2,1)S(1)} collective-permute-done((bf16[528,128]{1,0:T(8,128)(2,1)S(1)}, bf16[528,128]{1,0:T(8,128)(2,1)S(1)}, u32[]{:S(2)}, u32[]{:S(2)}) %collective-permute-start.8) | collective-permute-done | bytes 135200 | tf_op jit(solution)/shard_map/ppermute | solution.py:282
  101.5 1.5 %collective-permute-done.7.s2_ref = bf16[528,128]{1,0:T(8,128)(2,1)S(1)} collective-permute-done((bf16[528,128]{1,0:T(8,128)(2,1)S(1)}, bf16[528,128]{1,0:T(8,128)(2,1)S(1)}, u32[]{:S(2)}, u32[]{:S(2)}) %collective-permute-start.7) | collective-permute-done | bytes 135200 | tf_op jit(solution)/shard_map/ppermute | solution.py:282
  103.0 3.3 %collective-permute-done.6.s1_ref = bf16[528,128]{1,0:T(8,128)(2,1)S(1)} collective-permute-done((bf16[528,128]{1,0:T(8,128)(2,1)S(1)}, bf16[528,128]{1,0:T(8,128)(2,1)S(1)}, u32[]{:S(2)}, u32[]{:S(2)}) %collective-permute-start.6) | collective-permute-done | bytes 135200 | tf_op jit(solution)/shard_map/ppermute | solution.py:282
  106.3 0.8 shard_map.157
  107.1 0.0 collective-permute-done.9.other_ref
  107.1 1.1 shard_map.159
  (1 shorter events, 0.0 us)
Async XLA Ops:
  0.6 17.4 %copy-start = (bf16[256,1024]{1,0:T(8,128)(2,1)S(1)}, bf16[256,1024]{1,0:T(8,128)(2,1)}, u32[]{:S(2)}) copy-start(bf16[256,1024]{1,0:T(8,128)(2,1)} %w_ref.3) | copy-start | bytes 1572868
  0.6 1.1 %copy-start.1 = (bf16[2048,128]{1,0:T(8,128)(2,1)S(1)}, bf16[2048,128]{1,0:T(8,128)(2,1)}, u32[]{:S(2)}) copy-start(bf16[2048,128]{1,0:T(8,128)(2,1)} %serving_ref.1) | copy-start | bytes 1572868
  1.7 0.7 copy-start.6
  2.4 0.7 copy-start.9
  3.1 4.1 %copy-start.10 = (s32[1,1024]{1,0:T(1,128)S(1)}, s32[1,1024]{1,0:T(1,128)}, u32[]{:S(2)}) copy-start(s32[1,1024]{1,0:T(1,128)} %idx_ref.3) | copy-start | bytes 12292
  3.9 22.9 %collective-permute-start = (bf16[256,128]{1,0:T(8,128)(2,1)S(1)}, bf16[256,128]{1,0:T(8,128)(2,1)S(1)}, u32[]{:S(2)}, u32[]{:S(2)}) collective-permute-start(bf16[256,128]{1,0:T(8,128)(2,1)S(1)} %shard_map.147.table_ref), channel_id=1, source_target_pairs={{0,1},{1,0},{2,3},{3,2},{4,5},{5,4},{6,7},{7,6},{8,9},{9,8},{10,11... | collective-permute-start | bytes 196616 | tf_op jit(solution)/shard_map/ppermute | solution.py:287
  8.3 9.7 %copy-start.2 = (bf16[256,128]{1,0:T(8,128)(2,1)S(1)}, bf16[256,128]{1,0:T(8,128)(2,1)}, u32[]{:S(2)}) copy-start(bf16[256,128]{1,0:T(8,128)(2,1)} %dense_ref.3) | copy-start | bytes 196612
  8.3 18.4 %all-to-all-start = ((s32[32,2,128]{2,1,0:T(2,128)}), s32[32,2,128]{2,1,0:T(2,128)S(1)}, u32[]{:S(2)}, u32[]{:S(2)}) async-start(s32[32,2,128]{2,1,0:T(2,128)} %bitcast.2), calls=%async_computation | async-start | bytes 65536 | tf_op jit(solution)/shard_map/all_to_all | solution.py:291
  18.0 0.7 copy-start.4
  18.0 0.7 copy-start.8
  27.9 4.0 %copy-start.11 = (s32[1,256]{1,0:T(1,128)S(1)}, s32[1,256]{1,0:T(1,128)}, u32[]{:S(2)}) copy-start(s32[1,256]{1,0:T(1,128)} %len_ref.1) | copy-start | bytes 3076
  27.9 13.1 %all-to-all-start.1 = ((bf16[32,16,128]{2,1,0:T(8,128)(2,1)}), bf16[32,16,128]{2,1,0:T(8,128)(2,1)S(1)}, u32[]{:S(2)}, u32[]{:S(2)}) async-start(bf16[32,16,128]{2,1,0:T(8,128)(2,1)} %bitcast.7), calls=%async_computation.1 | async-start | bytes 262144 | tf_op jit(solution)/shard_map/all_to_all | solution.py:291
  42.5 3.9 %collective-permute-start.1 = (bf16[64,16,128]{2,1,0:T(8,128)(2,1)S(1)}, bf16[64,16,128]{2,1,0:T(8,128)(2,1)S(1)}, u32[]{:S(2)}, u32[]{:S(2)}) collective-permute-start(bf16[64,16,128]{2,1,0:T(8,128)(2,1)S(1)} %get-tuple-element.35), channel_id=1, source_target_pairs={{0,1},{1,0},{2,3},{3,2},{4,5},{5,4},{6,7},{7,6},{8,9},{9,8},{10,11... | collective-permute-start | bytes 786440 | tf_op jit(solution)/shard_map/ppermute | solution.py:287
  47.2 19.1 %all-to-all-start.2 = ((bf16[64,24,128]{2,1,0:T(8,128)(2,1)}), bf16[64,24,128]{2,1,0:T(8,128)(2,1)S(1)}, u32[]{:S(2)}, u32[]{:S(2)}) async-start(bf16[64,24,128]{2,1,0:T(8,128)(2,1)} %shard_map.153), calls=%async_computation.2 | async-start | bytes 786432 | tf_op jit(solution)/shard_map/all_to_all | solution.py:291
  51.7 1.5 %collective-permute-start.2 = (s32[64,128]{1,0:T(8,128)S(1)}, s32[64,128]{1,0:T(8,128)S(1)}, u32[]{:S(2)}, u32[]{:S(2)}) collective-permute-start(s32[64,128]{1,0:T(8,128)S(1)} %bitcast.18), channel_id=1, source_target_pairs={{0,1},{1,0},{2,3},{3,2},{4,5},{5,4},{6,7},{7,6},{8,9},{9,8},{10,11... | collective-permute-start | bytes 98312 | tf_op jit(solution)/shard_map/ppermute | solution.py:287
  53.6 12.8 %copy-start.7 = (s32[1,2]{1,0:T(1,128)S(1)}, s32[1,2]{1,0:T(1,128)}, u32[]{:S(2)}) copy-start(s32[1,2]{1,0:T(1,128)} %hot_ref.3) | copy-start | bytes 28
  67.1 4.0 %collective-permute-start.5 = (bf16[304,128]{1,0:T(8,128)(2,1)S(1)}, bf16[304,128]{1,0:T(8,128)(2,1)S(1)}, u32[]{:S(2)}, u32[]{:S(2)}) collective-permute-start(bf16[304,128]{1,0:T(8,128)(2,1)S(1)} %shard_map.155.x0_ref), channel_id=1, source_target_pairs={{0,192},{64,0},{128,64},{192,128},{1,193},{65,1},{129,65},{193,129... | collective-permute-start | bytes 233480 | tf_op jit(solution)/shard_map/ppermute | solution.py:282
  69.6 4.8 %collective-permute-start.4 = (bf16[304,128]{1,0:T(8,128)(2,1)S(1)}, bf16[304,128]{1,0:T(8,128)(2,1)S(1)}, u32[]{:S(2)}, u32[]{:S(2)}) collective-permute-start(bf16[304,128]{1,0:T(8,128)(2,1)S(1)} %shard_map.155.x0_ref), channel_id=1, source_target_pairs={{0,128},{64,192},{128,0},{192,64},{1,129},{65,193},{129,1},{193,65... | collective-permute-start | bytes 233480 | tf_op jit(solution)/shard_map/ppermute | solution.py:282
  70.2 6.5 %collective-permute-start.3 = (bf16[304,128]{1,0:T(8,128)(2,1)S(1)}, bf16[304,128]{1,0:T(8,128)(2,1)S(1)}, u32[]{:S(2)}, u32[]{:S(2)}) collective-permute-start(bf16[304,128]{1,0:T(8,128)(2,1)S(1)} %shard_map.155.x0_ref), channel_id=1, source_target_pairs={{0,64},{64,128},{128,192},{192,0},{1,65},{65,129},{129,193},{193,1... | collective-permute-start | bytes 233480 | tf_op jit(solution)/shard_map/ppermute | solution.py:282
  76.7 18.5 %copy-start.3 = (f32[1,512,128]{2,1,0:T(8,128)S(1)}, f32[1,512,128]{2,1,0:T(8,128)}, u32[]{:S(2)}) copy-start(f32[1,512,128]{2,1,0:T(8,128)} %param.20) | copy-start | bytes 786436
  76.7 18.5 %copy-start.5 = (f32[1,512]{1,0:T(1,128)S(1)}, f32[1,512]{1,0:T(1,128)}, u32[]{:S(2)}) copy-start(f32[1,512]{1,0:T(1,128)} %accum_ref.1) | copy-start | bytes 6148
  91.5 15.6 %collective-permute-start.9 = (bf16[32,32,128]{2,1,0:T(8,128)(2,1)S(1)}, bf16[32,32,128]{2,1,0:T(8,128)(2,1)S(1)}, u32[]{:S(2)}, u32[]{:S(2)}) collective-permute-start(bf16[32,32,128]{2,1,0:T(8,128)(2,1)S(1)} %all_to_all.20.mine_ref), channel_id=1, source_target_pairs={{0,1},{1,0},{2,3},{3,2},{4,5},{5,4},{6,7},{7,6},{8,9},{9,8},{10,11... | collective-permute-start | bytes 786440 | tf_op jit(solution)/shard_map/ppermute | solution.py:287
  96.3 5.1 %collective-permute-start.8 = (bf16[528,128]{1,0:T(8,128)(2,1)S(1)}, bf16[528,128]{1,0:T(8,128)(2,1)S(1)}, u32[]{:S(2)}, u32[]{:S(2)}) collective-permute-start(bf16[528,128]{1,0:T(8,128)(2,1)S(1)} %get-tuple-element.40.s0_ref), channel_id=1, source_target_pairs={{0,192},{64,0},{128,64},{192,128},{1,193},{65,1},{129,65},{193,129... | collective-permute-start | bytes 405512 | tf_op jit(solution)/shard_map/ppermute | solution.py:282
  96.3 6.6 %collective-permute-start.7 = (bf16[528,128]{1,0:T(8,128)(2,1)S(1)}, bf16[528,128]{1,0:T(8,128)(2,1)S(1)}, u32[]{:S(2)}, u32[]{:S(2)}) collective-permute-start(bf16[528,128]{1,0:T(8,128)(2,1)S(1)} %get-tuple-element.40.s0_ref), channel_id=1, source_target_pairs={{0,128},{64,192},{128,0},{192,64},{1,129},{65,193},{129,1},{193,65... | collective-permute-start | bytes 405512 | tf_op jit(solution)/shard_map/ppermute | solution.py:282
  96.7 9.6 %collective-permute-start.6 = (bf16[528,128]{1,0:T(8,128)(2,1)S(1)}, bf16[528,128]{1,0:T(8,128)(2,1)S(1)}, u32[]{:S(2)}, u32[]{:S(2)}) collective-permute-start(bf16[528,128]{1,0:T(8,128)(2,1)S(1)} %get-tuple-element.40.s0_ref), channel_id=1, source_target_pairs={{0,64},{64,128},{128,192},{192,0},{1,65},{65,129},{129,193},{193,1... | collective-permute-start | bytes 405512 | tf_op jit(solution)/shard_map/ppermute | solution.py:282

commit v3 on v2

--- a/solution.py
+++ b/solution.py
@@ -156,9 +156,15 @@
     w_out_out_ref[...] = w_out_ref[...]
 
 
+def by_tile(ref, value):
+    for i in range(8):
+        for j in range(8):
+            ref[i * 8 + j] = value[i * 16 : (i + 1) * 16, j * 128 : (j + 1) * 128]
+
+
 def step_kernel(
     core_ref, rows_ref, use_ref, dense_ref, pre_ref, labels_ref, w_ref, w_out_ref,
-    give_ref, keep_ref, pooled_grad_ref,
+    give_ref, keep_ref, dpre_ref,
 ):
     pooled = dot(use_ref[...], rows_ref[...]).astype(BF16)
     pre = pre_ref[...] + dot(pooled, w_ref[0:D, :])
@@ -167,24 +173,21 @@
     logit = jnp.sum(pre * sig * w_out, axis=1, keepdims=True)
     dlogit = jax.nn.sigmoid(logit) - labels_ref[:, 0:1]
     dpre = (dlogit * w_out * (sig * (1.0 + pre * (1.0 - sig)))).astype(BF16)
+    dpre_ref[...] = dpre
     first = core_ref[0] == 0
     dense = dense_ref[...]
-    give = dot(jnp.where(first, dense, pooled), dpre, 0, 0).astype(BF16)
-    keep = dot(jnp.where(first, pooled, dense), dpre, 0, 0)
-    for i in range(8):
-        for j in range(8):
-            tile = slice(i * 16, (i + 1) * 16), slice(j * 128, (j + 1) * 128)
-            give_ref[i * 8 + j] = give[tile]
-            keep_ref[i * 8 + j] = keep[tile]
-    pooled_grad_ref[...] = dot(dpre, w_ref[0:D, :], 1, 1)
-
-
-def row_grad_kernel(pooled_grad_ref, use_t_ref, out_ref):
-    pooled_grad = pooled_grad_ref[...]
+    by_tile(give_ref, dot(jnp.where(first, dense, pooled), dpre, 0, 0).astype(BF16))
+    keep_ref[...] = jnp.where(first, pooled, dense)
+
+
+def rest_kernel(keep_ref, dpre_ref, w_ref, use_t_ref, kept_ref, out_ref):
+    dpre = dpre_ref[...]
+    pooled_grad = dot(dpre, w_ref[0:D, :], 1, 1)
     high = pooled_grad.astype(BF16)
     low = (pooled_grad - high.astype(F32)).astype(BF16)
     use_t = use_t_ref[...]
     out_ref[...] = (dot(use_t, high) + dot(use_t, low)).astype(BF16)
+    by_tile(kept_ref, dot(keep_ref[...], dpre, 0, 0))
 
 
 def parts_kernel(keep_ref, given_ref, row_grad_ref, out_ref):
@@ -340,22 +343,26 @@
         (core, wanted, other_wanted),
         1 << 26,
     )
-    give, keep, pooled_grad = call(
+    give, keep, dpre = call(
         step_kernel,
-        [like((N_ROW, 16, D), BF16), like((N_ROW, 16, D), F32), like((BAGS, D), F32)],
+        [like((N_ROW, 16, D), BF16), like((BAGS, D), BF16), like((BAGS, FF), BF16)],
         [SM] + [VM] * 7,
         (core, fetched, use, dense_act, pre, labels_column, w_top, w_out_line),
         1 << 29,
     )
     given = other_core(give)
-    (row_grad,) = call(
-        row_grad_kernel, [like((SLOTS, D), BF16)], [VM] * 2, (pooled_grad, use_t), 1 << 27
+    kept, row_grad = call(
+        rest_kernel,
+        [like((N_ROW, 16, D), F32), like((SLOTS, D), BF16)],
+        [VM] * 4,
+        (keep, dpre, w_top, use_t),
+        1 << 28,
     )
     (parts,) = call(
         parts_kernel,
         [like((N_ROW, 24, D), BF16)],
         [VM] * 3,
-        (keep, given, row_grad.reshape(N_ROW, CAP, D)),
+        (kept, given, row_grad.reshape(N_ROW, CAP, D)),
         1 << 20,
     )
     got = exchange(parts)

time: 109 us -> 108 us (level)
  no operation moved by 1% of the time
where the time goes in v3:
time: 108 us
  waiting for transfers between devices  43.3 us (40%)
  starting transfers between devices  33.6 us (31%)
  blocking collectives  14.8 us (14%)
  Pallas kernels  12.2 us (11%)
  local copies, waits for them, and re-layouts  3.1 us (3%)
    all_to_all x3, waiting for transfers between devices, exchange(): return lax.all_to_all(x, axes, 0, 0, tiled=True)  27.8 us
    all_to_all x3, starting transfers between devices, exchange(): return lax.all_to_all(x, axes, 0, 0, tiled=True)  18.1 us
    all_to_all x1, blocking collectives, exchange(): return lax.all_to_all(x, axes, 0, 0, tiled=True)  14.8 us
    ppermute x6, waiting for transfers between devices, over_groups(): lax.ppermute(x, 'grp', [(g, (g + o) % N_GRP) for g in range(N_GRP)])  14.3 us
    pallas_call x14, Pallas kernels, call(): pl.pallas_call(kernel, out_shape=outs, in_specs=specs, out_specs=[VM] * l...  12.2 us
    ppermute x4, starting transfers between devices, other_core(): return lax.ppermute(x, 'row_2', [(0, 1), (1, 0)])  10.4 us
    ppermute x6, starting transfers between devices, over_groups(): lax.ppermute(x, 'grp', [(g, (g + o) % N_GRP) for g in range(N_GRP)])  5.15 us
    unnamed x24, local copies, waits for them, and re-layouts  3.1 us
  transfers between devices with their start and end apart: 13, of which 11 were waited for; matrix products, arithmetic and copies ran while one was open for 0% of the time, Pallas kernels for 6%

profile of v3, /device:TPU:1, one launch (start us, length us, event | category | flops | bytes accessed | tf_op | source)
XLA Modules:
  0.0 107.7 jit_solution(5254700338361332648)
XLA Ops:
  0.6 0.0 copy-start
  0.6 0.0 copy-start.1
  0.7 1.1 %copy-done.1 = bf16[2048,128]{1,0:T(8,128)(2,1)S(1)} copy-done((bf16[2048,128]{1,0:T(8,128)(2,1)S(1)}, bf16[2048,128]{1,0:T(8,128)(2,1)}, u32[]{:S(2)}) %copy-start.1) | copy-done | bytes 524312
  1.7 0.0 copy-start.6
  1.7 0.7 copy-done.6
  2.4 0.0 copy-start.9
  2.4 0.7 copy-done.9
  3.1 0.0 copy-start.10
  3.1 0.8 shard_map.147.table_ref
  3.9 3.3 %collective-permute-start = (bf16[256,128]{1,0:T(8,128)(2,1)S(1)}, bf16[256,128]{1,0:T(8,128)(2,1)S(1)}, u32[]{:S(2)}, u32[]{:S(2)}) collective-permute-start(bf16[256,128]{1,0:T(8,128)(2,1)S(1)} %shard_map.147.table_ref), channel_id=1, source_target_pairs={{0,1},{1,0},{2,3},{3,2},{4,5},{5,4},{6,7},{7,6},{8,9},{9,8},{10,11... | collective-permute-start | bytes 196616 | tf_op jit(solution)/shard_map/ppermute | solution.py:290
  7.2 0.0 copy-done.10
  7.2 1.2 %shard_map.146 = s32[64,128]{1,0:T(8,128)} custom-call(s32[1,1024]{1,0:T(1,128)S(1)} %copy-done.10), custom_call_target="tpu_custom_call" | custom-call | flops 67108864 | bytes 36864 | tf_op jit(solution)/shard_map/pallas_call | solution.py:49
  8.3 0.0 copy-start.2
  8.3 9.6 %all-to-all-start = ((s32[32,2,128]{2,1,0:T(2,128)}), s32[32,2,128]{2,1,0:T(2,128)S(1)}, u32[]{:S(2)}, u32[]{:S(2)}) async-start(s32[32,2,128]{2,1,0:T(2,128)} %bitcast.2), calls=%async_computation | async-start | bytes 65536 | tf_op jit(solution)/shard_map/all_to_all | solution.py:294
  18.0 0.0 copy-start.4
  18.0 0.0 copy-start.8
  18.0 0.0 copy-done
  18.0 0.0 copy-done.2
  18.0 0.6 copy-done.4
  18.7 0.0 copy-done.8
  18.7 0.3 shard_map.148
  19.0 7.8 %all-to-all-done = s32[32,2,128]{2,1,0:T(2,128)S(1)} async-done(((s32[32,2,128]{2,1,0:T(2,128)}), s32[32,2,128]{2,1,0:T(2,128)S(1)}, u32[]{:S(2)}, u32[]{:S(2)}) %all-to-all-start) | async-done | bytes 32800 | tf_op jit(solution)/shard_map/all_to_all | solution.py:294
  26.7 0.0 collective-permute-done.other_ref
  26.7 1.2 %shard_map.149 = bf16[512,128]{1,0:T(8,128)(2,1)} custom-call(s32[1]{0:T(128)} %bitcast.1.core_ref, s32[64,128]{1,0:T(8,128)S(1)} %bitcast.16, bf16[256,128]{1,0:T(8,128)(2,1)S(1)} %shard_map.147.table_ref, bf16[256,128]{1,0:T(8,128)(2,1)S(1)} %collective-permute-done.other_ref), custom_call_target="tpu_custom_call" | custom-call | flops 67108864 | bytes 294916 | tf_op jit(solution)/shard_map/pallas_call | solution.py:49
  27.9 0.0 copy-start.11
  27.9 4.0 %all-to-all-start.1 = ((bf16[32,16,128]{2,1,0:T(8,128)(2,1)}), bf16[32,16,128]{2,1,0:T(8,128)(2,1)S(1)}, u32[]{:S(2)}, u32[]{:S(2)}) async-start(bf16[32,16,128]{2,1,0:T(8,128)(2,1)} %bitcast.7), calls=%async_computation.1 | async-start | bytes 262144 | tf_op jit(solution)/shard_map/all_to_all | solution.py:294
  31.9 0.0 copy-done.11
  31.9 1.9 %shard_map.150 = (bf16[256,512]{1,0:T(8,128)(2,1)S(1)}, bf16[512,256]{1,0:T(8,128)(2,1)S(1)}) custom-call(s32[1,1024]{1,0:T(1,128)S(1)} %copy-done.10, s32[1,256]{1,0:T(1,128)S(1)} %copy-done.11), custom_call_target="tpu_custom_call" | custom-call | flops 536870912 | bytes 529408 | tf_op jit(solution)/shard_map/pallas_call | solution.py:49
  33.8 7.2 %all-to-all-done.1 = bf16[32,16,128]{2,1,0:T(8,128)(2,1)S(1)} async-done(((bf16[32,16,128]{2,1,0:T(8,128)(2,1)}), bf16[32,16,128]{2,1,0:T(8,128)(2,1)S(1)}, u32[]{:S(2)}, u32[]{:S(2)}) %all-to-all-start.1) | async-done | bytes 131104 | tf_op jit(solution)/shard_map/all_to_all | solution.py:294
  41.1 1.0 shard_map.151
  42.1 2.8 %collective-permute-start.1 = (bf16[64,16,128]{2,1,0:T(8,128)(2,1)S(1)}, bf16[64,16,128]{2,1,0:T(8,128)(2,1)S(1)}, u32[]{:S(2)}, u32[]{:S(2)}) collective-permute-start(bf16[64,16,128]{2,1,0:T(8,128)(2,1)S(1)} %get-tuple-element.40), channel_id=1, source_target_pairs={{0,1},{1,0},{2,3},{3,2},{4,5},{5,4},{6,7},{7,6},{8,9},{9,8},{10,11... | collective-permute-start | bytes 786440 | tf_op jit(solution)/shard_map/ppermute | solution.py:290
  44.8 0.9 shard_map.152
  45.7 0.3 collective-permute-done.1.given_ref
  46.0 0.8 shard_map.153
  46.8 4.4 %all-to-all-start.2 = ((bf16[64,24,128]{2,1,0:T(8,128)(2,1)}), bf16[64,24,128]{2,1,0:T(8,128)(2,1)S(1)}, u32[]{:S(2)}, u32[]{:S(2)}) async-start(bf16[64,24,128]{2,1,0:T(8,128)(2,1)} %shard_map.153), calls=%async_computation.2 | async-start | bytes 786432 | tf_op jit(solution)/shard_map/all_to_all | solution.py:294
  51.2 0.7 collective-permute-start.2
  51.9 0.9 collective-permute-done.2.other_ref
  52.8 0.4 shard_map.154.place_ref
  53.1 0.0 copy-start.7
  53.2 12.8 %all-to-all-done.2 = bf16[64,24,128]{2,1,0:T(8,128)(2,1)S(1)} async-done(((bf16[64,24,128]{2,1,0:T(8,128)(2,1)}), bf16[64,24,128]{2,1,0:T(8,128)(2,1)S(1)}, u32[]{:S(2)}, u32[]{:S(2)}) %all-to-all-start.2) | async-done | bytes 393248 | tf_op jit(solution)/shard_map/all_to_all | solution.py:294
  65.9 0.0 copy-done.7
  65.9 0.8 shard_map.155.x0_ref
  66.7 2.6 %collective-permute-start.5 = (bf16[304,128]{1,0:T(8,128)(2,1)S(1)}, bf16[304,128]{1,0:T(8,128)(2,1)S(1)}, u32[]{:S(2)}, u32[]{:S(2)}) collective-permute-start(bf16[304,128]{1,0:T(8,128)(2,1)S(1)} %shard_map.155.x0_ref), channel_id=1, source_target_pairs={{0,192},{64,0},{128,64},{192,128},{1,193},{65,1},{129,65},{193,129... | collective-permute-start | bytes 233480 | tf_op jit(solution)/shard_map/ppermute | solution.py:285
  69.2 0.5 collective-permute-start.4
  69.7 0.6 collective-permute-start.3
  70.3 0.3 collective-permute-done.5.x3_ref
  70.7 3.4 %collective-permute-done.4.x2_ref = bf16[304,128]{1,0:T(8,128)(2,1)S(1)} collective-permute-done((bf16[304,128]{1,0:T(8,128)(2,1)S(1)}, bf16[304,128]{1,0:T(8,128)(2,1)S(1)}, u32[]{:S(2)}, u32[]{:S(2)}) %collective-permute-start.4) | collective-permute-done | bytes 77856 | tf_op jit(solution)/shard_map/ppermute | solution.py:285
  74.0 2.2 %collective-permute-done.3.x1_ref = bf16[304,128]{1,0:T(8,128)(2,1)S(1)} collective-permute-done((bf16[304,128]{1,0:T(8,128)(2,1)S(1)}, bf16[304,128]{1,0:T(8,128)(2,1)S(1)}, u32[]{:S(2)}, u32[]{:S(2)}) %collective-permute-start.3) | collective-permute-done | bytes 77856 | tf_op jit(solution)/shard_map/ppermute | solution.py:285
  76.2 0.0 copy-start.3
  76.3 0.0 copy-start.5
  76.3 14.8 %all_to_all.20.mine_ref = bf16[32,32,128]{2,1,0:T(8,128)(2,1)S(1)} all-to-all(bf16[32,32,128]{2,1,0:T(8,128)(2,1)S(1)} %shard_map.158), channel_id=1, replica_groups=mesh['grp'=4,'row_0'=4,'row_1'=8,'row_2'=2] {'row_0','row_1'}, dimensions={0} | all-to-all | bytes 524288 | tf_op jit(solution)/shard_map/all_to_all | solution.py:294
  91.1 3.7 %collective-permute-start.9 = (bf16[32,32,128]{2,1,0:T(8,128)(2,1)S(1)}, bf16[32,32,128]{2,1,0:T(8,128)(2,1)S(1)}, u32[]{:S(2)}, u32[]{:S(2)}) collective-permute-start(bf16[32,32,128]{2,1,0:T(8,128)(2,1)S(1)} %all_to_all.20.mine_ref), channel_id=1, source_target_pairs={{0,1},{1,0},{2,3},{3,2},{4,5},{5,4},{6,7},{7,6},{8,9},{9,8},{10,11... | collective-permute-start | bytes 786440 | tf_op jit(solution)/shard_map/ppermute | solution.py:290
  94.7 0.0 copy-done.3
  94.7 0.0 copy-done.5
  94.7 1.2 %shard_map.156 = (f32[512,128]{1,0:T(8,128)}, f32[1,512]{1,0:T(1,128)}, bf16[528,128]{1,0:T(8,128)(2,1)S(1)}) custom-call(s32[1]{0:T(128)} %bitcast.me_ref, bf16[304,128]{1,0:T(8,128)(2,1)S(1)} %shard_map.155.x0_ref, bf16[304,128]{1,0:T(8,128)(2,1)S(1)} %collective-permute-done.3.x1_ref, bf16[304,128]{1,0:T(8,128)(2,1)S(1)} %collective-permute-done.4.x2_ref, ...), custom_call_target="tpu_custom_call" | custom-call | flops 4194304 | bytes 974852 | tf_op jit(solution)/shard_map/pallas_call | solution.py:49
  95.9 0.0 collective-permute-start.8
  95.9 0.4 collective-permute-start.7
  96.2 1.1 %collective-permute-start.6 = (bf16[528,128]{1,0:T(8,128)(2,1)S(1)}, bf16[528,128]{1,0:T(8,128)(2,1)S(1)}, u32[]{:S(2)}, u32[]{:S(2)}) collective-permute-start(bf16[528,128]{1,0:T(8,128)(2,1)S(1)} %get-tuple-element.44.s0_ref), channel_id=1, source_target_pairs={{0,64},{64,128},{128,192},{192,0},{1,65},{65,129},{129,193},{193,1... | collective-permute-start | bytes 405512 | tf_op jit(solution)/shard_map/ppermute | solution.py:285
  97.4 3.7 %collective-permute-done.8.s3_ref = bf16[528,128]{1,0:T(8,128)(2,1)S(1)} collective-permute-done((bf16[528,128]{1,0:T(8,128)(2,1)S(1)}, bf16[528,128]{1,0:T(8,128)(2,1)S(1)}, u32[]{:S(2)}, u32[]{:S(2)}) %collective-permute-start.8) | collective-permute-done | bytes 135200 | tf_op jit(solution)/shard_map/ppermute | solution.py:285
  101.0 1.5 %collective-permute-done.7.s2_ref = bf16[528,128]{1,0:T(8,128)(2,1)S(1)} collective-permute-done((bf16[528,128]{1,0:T(8,128)(2,1)S(1)}, bf16[528,128]{1,0:T(8,128)(2,1)S(1)}, u32[]{:S(2)}, u32[]{:S(2)}) %collective-permute-start.7) | collective-permute-done | bytes 135200 | tf_op jit(solution)/shard_map/ppermute | solution.py:285
  102.5 3.3 %collective-permute-done.6.s1_ref = bf16[528,128]{1,0:T(8,128)(2,1)S(1)} collective-permute-done((bf16[528,128]{1,0:T(8,128)(2,1)S(1)}, bf16[528,128]{1,0:T(8,128)(2,1)S(1)}, u32[]{:S(2)}, u32[]{:S(2)}) %collective-permute-start.6) | collective-permute-done | bytes 135200 | tf_op jit(solution)/shard_map/ppermute | solution.py:285
  105.8 0.8 shard_map.157
  106.7 0.0 collective-permute-done.9.other_ref
  106.7 1.1 shard_map.159
  (1 shorter events, 0.0 us)
Async XLA Ops:
  0.6 17.4 %copy-start = (bf16[256,1024]{1,0:T(8,128)(2,1)S(1)}, bf16[256,1024]{1,0:T(8,128)(2,1)}, u32[]{:S(2)}) copy-start(bf16[256,1024]{1,0:T(8,128)(2,1)} %w_ref.5) | copy-start | bytes 1572868
  0.6 1.1 %copy-start.1 = (bf16[2048,128]{1,0:T(8,128)(2,1)S(1)}, bf16[2048,128]{1,0:T(8,128)(2,1)}, u32[]{:S(2)}) copy-start(bf16[2048,128]{1,0:T(8,128)(2,1)} %serving_ref.1) | copy-start | bytes 1572868
  1.7 0.7 copy-start.6
  2.4 0.7 copy-start.9
  3.1 4.1 %copy-start.10 = (s32[1,1024]{1,0:T(1,128)S(1)}, s32[1,1024]{1,0:T(1,128)}, u32[]{:S(2)}) copy-start(s32[1,1024]{1,0:T(1,128)} %idx_ref.3) | copy-start | bytes 12292
  3.9 22.9 %collective-permute-start = (bf16[256,128]{1,0:T(8,128)(2,1)S(1)}, bf16[256,128]{1,0:T(8,128)(2,1)S(1)}, u32[]{:S(2)}, u32[]{:S(2)}) collective-permute-start(bf16[256,128]{1,0:T(8,128)(2,1)S(1)} %shard_map.147.table_ref), channel_id=1, source_target_pairs={{0,1},{1,0},{2,3},{3,2},{4,5},{5,4},{6,7},{7,6},{8,9},{9,8},{10,11... | collective-permute-start | bytes 196616 | tf_op jit(solution)/shard_map/ppermute | solution.py:290
  8.3 9.7 %copy-start.2 = (bf16[256,128]{1,0:T(8,128)(2,1)S(1)}, bf16[256,128]{1,0:T(8,128)(2,1)}, u32[]{:S(2)}) copy-start(bf16[256,128]{1,0:T(8,128)(2,1)} %dense_ref.3) | copy-start | bytes 196612
  8.3 18.4 %all-to-all-start = ((s32[32,2,128]{2,1,0:T(2,128)}), s32[32,2,128]{2,1,0:T(2,128)S(1)}, u32[]{:S(2)}, u32[]{:S(2)}) async-start(s32[32,2,128]{2,1,0:T(2,128)} %bitcast.2), calls=%async_computation | async-start | bytes 65536 | tf_op jit(solution)/shard_map/all_to_all | solution.py:294
  18.0 0.7 copy-start.4
  18.0 0.7 copy-start.8
  27.9 4.0 %copy-start.11 = (s32[1,256]{1,0:T(1,128)S(1)}, s32[1,256]{1,0:T(1,128)}, u32[]{:S(2)}) copy-start(s32[1,256]{1,0:T(1,128)} %len_ref.1) | copy-start | bytes 3076
  27.9 13.1 %all-to-all-start.1 = ((bf16[32,16,128]{2,1,0:T(8,128)(2,1)}), bf16[32,16,128]{2,1,0:T(8,128)(2,1)S(1)}, u32[]{:S(2)}, u32[]{:S(2)}) async-start(bf16[32,16,128]{2,1,0:T(8,128)(2,1)} %bitcast.7), calls=%async_computation.1 | async-start | bytes 262144 | tf_op jit(solution)/shard_map/all_to_all | solution.py:294
  42.1 3.9 %collective-permute-start.1 = (bf16[64,16,128]{2,1,0:T(8,128)(2,1)S(1)}, bf16[64,16,128]{2,1,0:T(8,128)(2,1)S(1)}, u32[]{:S(2)}, u32[]{:S(2)}) collective-permute-start(bf16[64,16,128]{2,1,0:T(8,128)(2,1)S(1)} %get-tuple-element.40), channel_id=1, source_target_pairs={{0,1},{1,0},{2,3},{3,2},{4,5},{5,4},{6,7},{7,6},{8,9},{9,8},{10,11... | collective-permute-start | bytes 786440 | tf_op jit(solution)/shard_map/ppermute | solution.py:290
  46.8 19.1 %all-to-all-start.2 = ((bf16[64,24,128]{2,1,0:T(8,128)(2,1)}), bf16[64,24,128]{2,1,0:T(8,128)(2,1)S(1)}, u32[]{:S(2)}, u32[]{:S(2)}) async-start(bf16[64,24,128]{2,1,0:T(8,128)(2,1)} %shard_map.153), calls=%async_computation.2 | async-start | bytes 786432 | tf_op jit(solution)/shard_map/all_to_all | solution.py:294
  51.2 1.5 %collective-permute-start.2 = (s32[64,128]{1,0:T(8,128)S(1)}, s32[64,128]{1,0:T(8,128)S(1)}, u32[]{:S(2)}, u32[]{:S(2)}) collective-permute-start(s32[64,128]{1,0:T(8,128)S(1)} %bitcast.17), channel_id=1, source_target_pairs={{0,1},{1,0},{2,3},{3,2},{4,5},{5,4},{6,7},{7,6},{8,9},{9,8},{10,11... | collective-permute-start | bytes 98312 | tf_op jit(solution)/shard_map/ppermute | solution.py:290
  53.1 12.8 %copy-start.7 = (s32[1,2]{1,0:T(1,128)S(1)}, s32[1,2]{1,0:T(1,128)}, u32[]{:S(2)}) copy-start(s32[1,2]{1,0:T(1,128)} %hot_ref.3) | copy-start | bytes 28
  66.7 4.0 %collective-permute-start.5 = (bf16[304,128]{1,0:T(8,128)(2,1)S(1)}, bf16[304,128]{1,0:T(8,128)(2,1)S(1)}, u32[]{:S(2)}, u32[]{:S(2)}) collective-permute-start(bf16[304,128]{1,0:T(8,128)(2,1)S(1)} %shard_map.155.x0_ref), channel_id=1, source_target_pairs={{0,192},{64,0},{128,64},{192,128},{1,193},{65,1},{129,65},{193,129... | collective-permute-start | bytes 233480 | tf_op jit(solution)/shard_map/ppermute | solution.py:285
  69.2 4.8 %collective-permute-start.4 = (bf16[304,128]{1,0:T(8,128)(2,1)S(1)}, bf16[304,128]{1,0:T(8,128)(2,1)S(1)}, u32[]{:S(2)}, u32[]{:S(2)}) collective-permute-start(bf16[304,128]{1,0:T(8,128)(2,1)S(1)} %shard_map.155.x0_ref), channel_id=1, source_target_pairs={{0,128},{64,192},{128,0},{192,64},{1,129},{65,193},{129,1},{193,65... | collective-permute-start | bytes 233480 | tf_op jit(solution)/shard_map/ppermute | solution.py:285
  69.7 6.5 %collective-permute-start.3 = (bf16[304,128]{1,0:T(8,128)(2,1)S(1)}, bf16[304,128]{1,0:T(8,128)(2,1)S(1)}, u32[]{:S(2)}, u32[]{:S(2)}) collective-permute-start(bf16[304,128]{1,0:T(8,128)(2,1)S(1)} %shard_map.155.x0_ref), channel_id=1, source_target_pairs={{0,64},{64,128},{128,192},{192,0},{1,65},{65,129},{129,193},{193,1... | collective-permute-start | bytes 233480 | tf_op jit(solution)/shard_map/ppermute | solution.py:285
  76.2 18.5 %copy-start.3 = (f32[1,512,128]{2,1,0:T(8,128)S(1)}, f32[1,512,128]{2,1,0:T(8,128)}, u32[]{:S(2)}) copy-start(f32[1,512,128]{2,1,0:T(8,128)} %param.20) | copy-start | bytes 786436
  76.3 18.5 %copy-start.5 = (f32[1,512]{1,0:T(1,128)S(1)}, f32[1,512]{1,0:T(1,128)}, u32[]{:S(2)}) copy-start(f32[1,512]{1,0:T(1,128)} %accum_ref.1) | copy-start | bytes 6148
  91.1 15.6 %collective-permute-start.9 = (bf16[32,32,128]{2,1,0:T(8,128)(2,1)S(1)}, bf16[32,32,128]{2,1,0:T(8,128)(2,1)S(1)}, u32[]{:S(2)}, u32[]{:S(2)}) collective-permute-start(bf16[32,32,128]{2,1,0:T(8,128)(2,1)S(1)} %all_to_all.20.mine_ref), channel_id=1, source_target_pairs={{0,1},{1,0},{2,3},{3,2},{4,5},{5,4},{6,7},{7,6},{8,9},{9,8},{10,11... | collective-permute-start | bytes 786440 | tf_op jit(solution)/shard_map/ppermute | solution.py:290
  95.9 5.1 %collective-permute-start.8 = (bf16[528,128]{1,0:T(8,128)(2,1)S(1)}, bf16[528,128]{1,0:T(8,128)(2,1)S(1)}, u32[]{:S(2)}, u32[]{:S(2)}) collective-permute-start(bf16[528,128]{1,0:T(8,128)(2,1)S(1)} %get-tuple-element.44.s0_ref), channel_id=1, source_target_pairs={{0,192},{64,0},{128,64},{192,128},{1,193},{65,1},{129,65},{193,129... | collective-permute-start | bytes 405512 | tf_op jit(solution)/shard_map/ppermute | solution.py:285
  95.9 6.6 %collective-permute-start.7 = (bf16[528,128]{1,0:T(8,128)(2,1)S(1)}, bf16[528,128]{1,0:T(8,128)(2,1)S(1)}, u32[]{:S(2)}, u32[]{:S(2)}) collective-permute-start(bf16[528,128]{1,0:T(8,128)(2,1)S(1)} %get-tuple-element.44.s0_ref), channel_id=1, source_target_pairs={{0,128},{64,192},{128,0},{192,64},{1,129},{65,193},{129,1},{193,65... | collective-permute-start | bytes 405512 | tf_op jit(solution)/shard_map/ppermute | solution.py:285
  96.2 9.6 %collective-permute-start.6 = (bf16[528,128]{1,0:T(8,128)(2,1)S(1)}, bf16[528,128]{1,0:T(8,128)(2,1)S(1)}, u32[]{:S(2)}, u32[]{:S(2)}) collective-permute-start(bf16[528,128]{1,0:T(8,128)(2,1)S(1)} %get-tuple-element.44.s0_ref), channel_id=1, source_target_pairs={{0,64},{64,128},{128,192},{192,0},{1,65},{65,129},{129,193},{193,1... | collective-permute-start | bytes 405512 | tf_op jit(solution)/shard_map/ppermute | solution.py:285

commit v4 on v3

--- a/solution.py
+++ b/solution.py
@@ -133,7 +133,9 @@
     rows_ref[...] = (rows + dot(ones_where(match & ~here), other_ref[...])).astype(BF16)
 
 
-def place_kernel(core_ref, ids_ref, other_ref, place_ref):
+def place_kernel(core_ref, hot_ref, ids_ref, other_ref, place_ref, hot_out_ref):
+    lane = iota((8, D), 1)
+    hot_out_ref[...] = jnp.where(lane == 0, hot_ref[0, 0], jnp.where(lane == 1, hot_ref[0, 1], 0))
     slot = iota((SLOTS, N_ROW), 0)
     line = lax.shift_right_logical(slot, 4) * 2 + core_ref[0] == iota((SLOTS, N_ROW), 1)
     here = lax.shift_right_logical(slot, 3) & 1 == core_ref[0]
@@ -195,7 +197,13 @@
     out_ref[:, 16:24, :] = row_grad_ref[...]
 
 
-def owned_kernel(got_ref, place_ref, hot_ref, out_ref):
+def hots_kernel(me_ref, h0_ref, h1_ref, h2_ref, h3_ref, out_ref):
+    me = me_ref[0]
+    for o, ref in enumerate((h0_ref, h1_ref, h2_ref, h3_ref)):
+        out_ref[(me - o) & 3] = ref[...]
+
+
+def owned_kernel(got_ref, place_ref, out_ref):
     grads = got_ref[:, :, 16:24, :].astype(F32).reshape(SLOTS, D).astype(BF16)
     out_ref[0:SPAN, :] = dot(place_ref[...], grads).astype(BF16)
     for half in range(2):
@@ -203,9 +211,6 @@
         out_ref[at : at + 16, :] = jnp.sum(
             got_ref[:, half, 0:16, :].astype(F32), axis=0
         ).astype(BF16)
-    lane = iota((16, D), 1)
-    hot = jnp.where(lane == 0, hot_ref[0, 0], jnp.where(lane == 1, hot_ref[0, 1], 0))
-    out_ref[SPAN + 32 : SPAN + 48, :] = hot.astype(F32).astype(BF16)
 
 
 def top_kernel(me_ref, x0_ref, x1_ref, x2_ref, x3_ref, top_ref, by_group):
@@ -219,20 +224,20 @@
 
 
 def update_kernel(
-    me_ref, x0_ref, x1_ref, x2_ref, x3_ref, master_ref, accum_ref,
+    me_ref, x0_ref, x1_ref, x2_ref, x3_ref, hots_ref, master_ref, accum_ref,
     new_master_ref, new_accum_ref, coded_ref, by_group,
 ):
     me = me_ref[0]
     for o, ref in enumerate((x0_ref, x1_ref, x2_ref, x3_ref)):
         by_group[(me - o) & 3] = ref[...]
-    hot = [by_group[g, SPAN + 32 : SPAN + 48, :].astype(F32)[0:1, :] for g in range(N_GRP)]
+    hot = [hots_ref[g, 0:1, :] for g in range(N_GRP)]
     a, b = iota((BLOCK, BLOCK), 0), iota((BLOCK, BLOCK), 1)
     diagonal = a == b
     lane = iota((16, D), 1)
     scale_row = jnp.zeros((16, D), F32)
     for q in range(4):
         grad = jnp.zeros((BLOCK, D), F32)
-        number = (me * 4 + q).astype(F32)
+        number = me * 4 + q
         for g in range(N_GRP):
             for j in range(2):
                 block = by_group[g, j * BLOCK : (j + 1) * BLOCK, :].astype(F32)
@@ -336,11 +341,11 @@
     )
     fetched = exchange(rows.reshape(N_ROW // 2, 2 * CAP, D), CHIPS).reshape(SLOTS, D)
     other_wanted = other_core(wanted)
-    (place,) = call(
+    place, hot = call(
         place_kernel,
-        [like((SPAN, SLOTS), BF16)],
-        [SM] + [VM] * 2,
-        (core, wanted, other_wanted),
+        [like((SPAN, SLOTS), BF16), like((8, D), I32)],
+        [SM] * 2 + [VM] * 2,
+        (core, hot_blocks, wanted, other_wanted),
         1 << 26,
     )
     give, keep, dpre = call(
@@ -366,11 +371,14 @@
         1 << 20,
     )
     got = exchange(parts)
+    (hots,) = call(
+        hots_kernel, [like((N_GRP, 8, D), I32)], [SM] + [VM] * 4, (me, *over_groups(hot)), 1 << 12
+    )
     (own,) = call(
         owned_kernel,
-        [like((SPAN + 48, D), BF16)],
-        [VM, VM, SM],
-        (got.reshape(N_ROW // 2, 2, 24, D), place, hot_blocks),
+        [like((SPAN + 32, D), BF16)],
+        [VM, VM],
+        (got.reshape(N_ROW // 2, 2, 24, D), place),
         1 << 26,
     )
     owned = over_groups(own)
@@ -386,10 +394,10 @@
     new_master, new_accum, coded = call(
         update_kernel,
         [like((QUARTER, D), F32), like((1, QUARTER), F32), like((QUARTER + 16, D), BF16)],
-        [SM] + [VM] * 6,
-        (me, *owned, master[0], accum),
+        [SM] + [VM] * 7,
+        (me, *owned, hots, master[0], accum),
         1 << 22,
-        [pltpu.VMEM((N_GRP, SPAN + 48, D), BF16)],
+        [pltpu.VMEM((N_GRP, SPAN + 32, D), BF16)],
     )
     quarters = over_groups(coded)
     fresh, fresh_scale = call(

time: 108 us -> 113 us (1.046)
  the two profiles are of different devices: /device:TPU:1 before, /device:TPU:8 now
where the time goes in v4:
time: 113 us; the launch traced here: 111 us
  waiting for transfers between devices  46 us (41%)
  starting transfers between devices  32.7 us (29%)
  blocking collectives  16.6 us (15%)
  Pallas kernels  12.2 us (11%)
  local copies, waits for them, and re-layouts  3.09 us (3%)
    all_to_all x3, waiting for transfers between devices, exchange(): return lax.all_to_all(x, axes, 0, 0, tiled=True)  27 us
    all_to_all x3, starting transfers between devices, exchange(): return lax.all_to_all(x, axes, 0, 0, tiled=True)  22.6 us
    ppermute x9, waiting for transfers between devices, over_groups(): lax.ppermute(x, 'grp', [(g, (g + o) % N_GRP) for g in range(N_GRP)])  17.2 us
    all_to_all x1, blocking collectives, exchange(): return lax.all_to_all(x, axes, 0, 0, tiled=True)  16.6 us
    pallas_call x15, Pallas kernels, call(): pl.pallas_call(kernel, out_shape=outs, in_specs=specs, out_specs=[VM] * l...  12.2 us
    ppermute x9, starting transfers between devices, over_groups(): lax.ppermute(x, 'grp', [(g, (g + o) % N_GRP) for g in range(N_GRP)])  9.66 us
    unnamed x24, local copies, waits for them, and re-layouts  3.09 us
  transfers between devices with their start and end apart: 16, of which 14 were waited for; matrix products, arithmetic and copies ran while one was open for 0% of the time, Pallas kernels for 6%

profile of v4, /device:TPU:8, one launch (start us, length us, event | category | flops | bytes accessed | tf_op | source)
XLA Modules:
  0.0 111.4 jit_solution(2323858895550813895)
XLA Ops:
  0.6 0.0 copy-start
  0.6 0.0 copy-start.1
  0.7 1.1 copy-done.1
  1.7 0.7 copy-done.7
  2.4 0.7 copy-done.8
  3.1 0.8 shard_map.147.table_ref
  3.9 0.1 collective-permute-start
  4.0 0.0 copy-done.10
  4.0 1.2 %shard_map.146 = s32[64,128]{1,0:T(8,128)} custom-call(s32[1,1024]{1,0:T(1,128)S(1)} %copy-done.10), custom_call_target="tpu_custom_call" | custom-call | flops 67108864 | bytes 36864 | tf_op jit(solution)/shard_map/pallas_call | solution.py:49
  5.2 11.8 %all-to-all-start = ((s32[32,2,128]{2,1,0:T(2,128)}), s32[32,2,128]{2,1,0:T(2,128)S(1)}, u32[]{:S(2)}, u32[]{:S(2)}) async-start(s32[32,2,128]{2,1,0:T(2,128)} %bitcast.2), calls=%async_computation | async-start | bytes 65536 | tf_op jit(solution)/shard_map/all_to_all | solution.py:299
  17.0 0.0 copy-start.4
  17.0 0.0 copy-start.6
  17.0 0.0 copy-done
  17.0 0.0 copy-done.2
  17.0 0.6 copy-done.4
  17.7 0.0 copy-done.6
  17.7 0.3 shard_map.148
  18.0 7.7 %all-to-all-done = s32[32,2,128]{2,1,0:T(2,128)S(1)} async-done(((s32[32,2,128]{2,1,0:T(2,128)}), s32[32,2,128]{2,1,0:T(2,128)S(1)}, u32[]{:S(2)}, u32[]{:S(2)}) %all-to-all-start) | async-done | bytes 32800 | tf_op jit(solution)/shard_map/all_to_all | solution.py:299
  25.7 0.0 collective-permute-done.other_ref
  25.7 1.2 %shard_map.149 = bf16[512,128]{1,0:T(8,128)(2,1)} custom-call(s32[1]{0:T(128)} %bitcast.1.core_ref, s32[64,128]{1,0:T(8,128)S(1)} %bitcast.18, bf16[256,128]{1,0:T(8,128)(2,1)S(1)} %shard_map.147.table_ref, bf16[256,128]{1,0:T(8,128)(2,1)S(1)} %collective-permute-done.other_ref), custom_call_target="tpu_custom_call" | custom-call | flops 67108864 | bytes 294916 | tf_op jit(solution)/shard_map/pallas_call | solution.py:49
  26.9 5.1 %all-to-all-start.1 = ((bf16[32,16,128]{2,1,0:T(8,128)(2,1)}), bf16[32,16,128]{2,1,0:T(8,128)(2,1)S(1)}, u32[]{:S(2)}, u32[]{:S(2)}) async-start(bf16[32,16,128]{2,1,0:T(8,128)(2,1)} %bitcast.7), calls=%async_computation.1 | async-start | bytes 262144 | tf_op jit(solution)/shard_map/all_to_all | solution.py:299
  32.0 0.0 copy-done.11
  32.0 1.9 %shard_map.150 = (bf16[256,512]{1,0:T(8,128)(2,1)S(1)}, bf16[512,256]{1,0:T(8,128)(2,1)S(1)}) custom-call(s32[1,1024]{1,0:T(1,128)S(1)} %copy-done.10, s32[1,256]{1,0:T(1,128)S(1)} %copy-done.11), custom_call_target="tpu_custom_call" | custom-call | flops 536870912 | bytes 529408 | tf_op jit(solution)/shard_map/pallas_call | solution.py:49
  33.9 7.4 %all-to-all-done.1 = bf16[32,16,128]{2,1,0:T(8,128)(2,1)S(1)} async-done(((bf16[32,16,128]{2,1,0:T(8,128)(2,1)}), bf16[32,16,128]{2,1,0:T(8,128)(2,1)S(1)}, u32[]{:S(2)}, u32[]{:S(2)}) %all-to-all-start.1) | async-done | bytes 131104 | tf_op jit(solution)/shard_map/all_to_all | solution.py:299
  41.3 1.0 shard_map.151
  42.3 0.1 collective-permute-start.1
  42.4 0.9 shard_map.152
  43.3 0.6 collective-permute-done.1.given_ref
  43.9 0.8 shard_map.153
  44.7 5.7 %all-to-all-start.2 = ((bf16[64,24,128]{2,1,0:T(8,128)(2,1)}), bf16[64,24,128]{2,1,0:T(8,128)(2,1)S(1)}, u32[]{:S(2)}, u32[]{:S(2)}) async-start(bf16[64,24,128]{2,1,0:T(8,128)(2,1)} %shard_map.153), calls=%async_computation.2 | async-start | bytes 786432 | tf_op jit(solution)/shard_map/all_to_all | solution.py:299
  50.4 0.2 collective-permute-start.2
  50.6 1.1 collective-permute-done.2.other_ref
  51.7 0.0 copy-done.9
  51.7 0.9 shard_map.154
  52.7 11.9 %all-to-all-done.2 = bf16[64,24,128]{2,1,0:T(8,128)(2,1)S(1)} async-done(((bf16[64,24,128]{2,1,0:T(8,128)(2,1)}), bf16[64,24,128]{2,1,0:T(8,128)(2,1)S(1)}, u32[]{:S(2)}, u32[]{:S(2)}) %all-to-all-start.2) | async-done | bytes 393248 | tf_op jit(solution)/shard_map/all_to_all | solution.py:299
  64.6 0.2 shard_map.155.x0_ref
  64.8 2.8 %collective-permute-start.5 = (bf16[288,128]{1,0:T(8,128)(2,1)S(1)}, bf16[288,128]{1,0:T(8,128)(2,1)S(1)}, u32[]{:S(2)}, u32[]{:S(2)}) collective-permute-start(bf16[288,128]{1,0:T(8,128)(2,1)S(1)} %shard_map.155.x0_ref), channel_id=1, source_target_pairs={{0,192},{64,0},{128,64},{192,128},{1,193},{65,1},{129,65},{193,129... | collective-permute-start | bytes 221192 | tf_op jit(solution)/shard_map/ppermute | solution.py:290
  67.6 0.8 collective-permute-start.4
  68.4 0.9 collective-permute-start.3
  69.3 2.0 %collective-permute-done.5.x3_ref = bf16[288,128]{1,0:T(8,128)(2,1)S(1)} collective-permute-done((bf16[288,128]{1,0:T(8,128)(2,1)S(1)}, bf16[288,128]{1,0:T(8,128)(2,1)S(1)}, u32[]{:S(2)}, u32[]{:S(2)}) %collective-permute-start.5) | collective-permute-done | bytes 73760 | tf_op jit(solution)/shard_map/ppermute | solution.py:290
  71.3 2.9 %collective-permute-done.4.x2_ref = bf16[288,128]{1,0:T(8,128)(2,1)S(1)} collective-permute-done((bf16[288,128]{1,0:T(8,128)(2,1)S(1)}, bf16[288,128]{1,0:T(8,128)(2,1)S(1)}, u32[]{:S(2)}, u32[]{:S(2)}) %collective-permute-start.4) | collective-permute-done | bytes 73760 | tf_op jit(solution)/shard_map/ppermute | solution.py:290
  74.2 0.8 collective-permute-done.3.x1_ref
  75.0 0.0 copy-start.3
  75.0 0.0 copy-start.5
  75.0 16.6 %all_to_all.20.mine_ref = bf16[32,32,128]{2,1,0:T(8,128)(2,1)S(1)} all-to-all(bf16[32,32,128]{2,1,0:T(8,128)(2,1)S(1)} %shard_map.159), channel_id=1, replica_groups=mesh['grp'=4,'row_0'=4,'row_1'=8,'row_2'=2] {'row_0','row_1'}, dimensions={0} | all-to-all | bytes 524288 | tf_op jit(solution)/shard_map/all_to_all | solution.py:299
  91.6 0.0 collective-permute-start.12
  91.7 0.0 collective-permute-start.8
  91.7 0.8 collective-permute-start.7
  92.4 1.4 %collective-permute-start.6 = (s32[8,128]{1,0:T(8,128)S(1)}, s32[8,128]{1,0:T(8,128)S(1)}, u32[]{:S(2)}, u32[]{:S(2)}) collective-permute-start(s32[8,128]{1,0:T(8,128)S(1)} %get-tuple-element.45.h0_ref), channel_id=1, source_target_pairs={{0,64},{64,128},{128,192},{192,0},{1,65},{65,129},{129,193},{193,1... | collective-permute-start | bytes 12296 | tf_op jit(solution)/shard_map/ppermute | solution.py:290
  93.9 1.4 %collective-permute-done.8.h3_ref = s32[8,128]{1,0:T(8,128)S(1)} collective-permute-done((s32[8,128]{1,0:T(8,128)S(1)}, s32[8,128]{1,0:T(8,128)S(1)}, u32[]{:S(2)}, u32[]{:S(2)}) %collective-permute-start.8) | collective-permute-done | bytes 4128 | tf_op jit(solution)/shard_map/ppermute | solution.py:290
  95.3 1.5 %collective-permute-done.7.h2_ref = s32[8,128]{1,0:T(8,128)S(1)} collective-permute-done((s32[8,128]{1,0:T(8,128)S(1)}, s32[8,128]{1,0:T(8,128)S(1)}, u32[]{:S(2)}, u32[]{:S(2)}) %collective-permute-start.7) | collective-permute-done | bytes 4128 | tf_op jit(solution)/shard_map/ppermute | solution.py:290
  96.8 1.2 %collective-permute-done.6.h1_ref = s32[8,128]{1,0:T(8,128)S(1)} collective-permute-done((s32[8,128]{1,0:T(8,128)S(1)}, s32[8,128]{1,0:T(8,128)S(1)}, u32[]{:S(2)}, u32[]{:S(2)}) %collective-permute-start.6) | collective-permute-done | bytes 4128 | tf_op jit(solution)/shard_map/ppermute | solution.py:290
  97.9 0.0 copy-done.3
  97.9 0.0 copy-done.5
  97.9 1.2 %shard_map.157 = (f32[512,128]{1,0:T(8,128)}, f32[1,512]{1,0:T(1,128)}, bf16[528,128]{1,0:T(8,128)(2,1)S(1)}) custom-call(s32[1]{0:T(128)} %bitcast.me_ref, bf16[288,128]{1,0:T(8,128)(2,1)S(1)} %shard_map.155.x0_ref, bf16[288,128]{1,0:T(8,128)(2,1)S(1)} %collective-permute-done.3.x1_ref, bf16[288,128]{1,0:T(8,128)(2,1)S(1)} %collective-permute-done.4.x2_ref, ...), custom_call_target="tpu_custom_call" | custom-call | flops 4194304 | bytes 974852 | tf_op jit(solution)/shard_map/pallas_call | solution.py:49
  99.1 2.0 %collective-permute-start.11 = (bf16[528,128]{1,0:T(8,128)(2,1)S(1)}, bf16[528,128]{1,0:T(8,128)(2,1)S(1)}, u32[]{:S(2)}, u32[]{:S(2)}) collective-permute-start(bf16[528,128]{1,0:T(8,128)(2,1)S(1)} %get-tuple-element.48.s0_ref), channel_id=1, source_target_pairs={{0,192},{64,0},{128,64},{192,128},{1,193},{65,1},{129,65},{193,129... | collective-permute-start | bytes 405512 | tf_op jit(solution)/shard_map/ppermute | solution.py:290
  101.1 0.9 collective-permute-start.10
  102.0 0.0 collective-permute-start.9
  102.0 3.8 %collective-permute-done.11.s3_ref = bf16[528,128]{1,0:T(8,128)(2,1)S(1)} collective-permute-done((bf16[528,128]{1,0:T(8,128)(2,1)S(1)}, bf16[528,128]{1,0:T(8,128)(2,1)S(1)}, u32[]{:S(2)}, u32[]{:S(2)}) %collective-permute-start.11) | collective-permute-done | bytes 135200 | tf_op jit(solution)/shard_map/ppermute | solution.py:290
  105.9 2.2 %collective-permute-done.10.s2_ref = bf16[528,128]{1,0:T(8,128)(2,1)S(1)} collective-permute-done((bf16[528,128]{1,0:T(8,128)(2,1)S(1)}, bf16[528,128]{1,0:T(8,128)(2,1)S(1)}, u32[]{:S(2)}, u32[]{:S(2)}) %collective-permute-start.10) | collective-permute-done | bytes 135200 | tf_op jit(solution)/shard_map/ppermute | solution.py:290
  108.1 1.4 %collective-permute-done.9.s1_ref = bf16[528,128]{1,0:T(8,128)(2,1)S(1)} collective-permute-done((bf16[528,128]{1,0:T(8,128)(2,1)S(1)}, bf16[528,128]{1,0:T(8,128)(2,1)S(1)}, u32[]{:S(2)}, u32[]{:S(2)}) %collective-permute-start.9) | collective-permute-done | bytes 135200 | tf_op jit(solution)/shard_map/ppermute | solution.py:290
  109.5 0.8 shard_map.158
  110.4 0.0 collective-permute-done.12.other_ref
  110.4 1.1 shard_map.160
  (8 shorter events, 0.0 us)
Async XLA Ops:
  0.6 16.4 %copy-start = (bf16[256,1024]{1,0:T(8,128)(2,1)S(1)}, bf16[256,1024]{1,0:T(8,128)(2,1)}, u32[]{:S(2)}) copy-start(bf16[256,1024]{1,0:T(8,128)(2,1)} %w_ref.5) | copy-start | bytes 1572868
  0.6 1.1 copy-start.1
  1.7 0.7 copy-start.7
  2.4 0.7 copy-start.8
  3.1 0.9 copy-start.10
  3.9 21.8 %collective-permute-start = (bf16[256,128]{1,0:T(8,128)(2,1)S(1)}, bf16[256,128]{1,0:T(8,128)(2,1)S(1)}, u32[]{:S(2)}, u32[]{:S(2)}) collective-permute-start(bf16[256,128]{1,0:T(8,128)(2,1)S(1)} %shard_map.147.table_ref), channel_id=1, source_target_pairs={{0,1},{1,0},{2,3},{3,2},{4,5},{5,4},{6,7},{7,6},{8,9},{9,8},{10,11... | collective-permute-start | bytes 196616 | tf_op jit(solution)/shard_map/ppermute | solution.py:295
  5.1 11.9 %copy-start.2 = (bf16[256,128]{1,0:T(8,128)(2,1)S(1)}, bf16[256,128]{1,0:T(8,128)(2,1)}, u32[]{:S(2)}) copy-start(bf16[256,128]{1,0:T(8,128)(2,1)} %dense_ref.3) | copy-start | bytes 196612
  5.2 20.6 %all-to-all-start = ((s32[32,2,128]{2,1,0:T(2,128)}), s32[32,2,128]{2,1,0:T(2,128)S(1)}, u32[]{:S(2)}, u32[]{:S(2)}) async-start(s32[32,2,128]{2,1,0:T(2,128)} %bitcast.2), calls=%async_computation | async-start | bytes 65536 | tf_op jit(solution)/shard_map/all_to_all | solution.py:299
  17.0 0.7 copy-start.4
  17.0 0.7 copy-start.6
  26.9 5.1 %copy-start.11 = (s32[1,256]{1,0:T(1,128)S(1)}, s32[1,256]{1,0:T(1,128)}, u32[]{:S(2)}) copy-start(s32[1,256]{1,0:T(1,128)} %len_ref.1) | copy-start | bytes 3076
  26.9 14.4 %all-to-all-start.1 = ((bf16[32,16,128]{2,1,0:T(8,128)(2,1)}), bf16[32,16,128]{2,1,0:T(8,128)(2,1)S(1)}, u32[]{:S(2)}, u32[]{:S(2)}) async-start(bf16[32,16,128]{2,1,0:T(8,128)(2,1)} %bitcast.7), calls=%async_computation.1 | async-start | bytes 262144 | tf_op jit(solution)/shard_map/all_to_all | solution.py:299
  42.3 1.6 %collective-permute-start.1 = (bf16[64,16,128]{2,1,0:T(8,128)(2,1)S(1)}, bf16[64,16,128]{2,1,0:T(8,128)(2,1)S(1)}, u32[]{:S(2)}, u32[]{:S(2)}) collective-permute-start(bf16[64,16,128]{2,1,0:T(8,128)(2,1)S(1)} %get-tuple-element.42), channel_id=1, source_target_pairs={{0,1},{1,0},{2,3},{3,2},{4,5},{5,4},{6,7},{7,6},{8,9},{9,8},{10,11... | collective-permute-start | bytes 786440 | tf_op jit(solution)/shard_map/ppermute | solution.py:295
  44.7 7.0 %copy-start.9 = (s32[1,2]{1,0:T(1,128)S(1)}, s32[1,2]{1,0:T(1,128)}, u32[]{:S(2)}) copy-start(s32[1,2]{1,0:T(1,128)} %hot_ref.3) | copy-start | bytes 28
  44.7 19.8 %all-to-all-start.2 = ((bf16[64,24,128]{2,1,0:T(8,128)(2,1)}), bf16[64,24,128]{2,1,0:T(8,128)(2,1)S(1)}, u32[]{:S(2)}, u32[]{:S(2)}) async-start(bf16[64,24,128]{2,1,0:T(8,128)(2,1)} %shard_map.153), calls=%async_computation.2 | async-start | bytes 786432 | tf_op jit(solution)/shard_map/all_to_all | solution.py:299
  50.4 1.3 %collective-permute-start.2 = (s32[64,128]{1,0:T(8,128)S(1)}, s32[64,128]{1,0:T(8,128)S(1)}, u32[]{:S(2)}, u32[]{:S(2)}) collective-permute-start(s32[64,128]{1,0:T(8,128)S(1)} %bitcast.19), channel_id=1, source_target_pairs={{0,1},{1,0},{2,3},{3,2},{4,5},{5,4},{6,7},{7,6},{8,9},{9,8},{10,11... | collective-permute-start | bytes 98312 | tf_op jit(solution)/shard_map/ppermute | solution.py:295
  64.8 6.5 %collective-permute-start.5 = (bf16[288,128]{1,0:T(8,128)(2,1)S(1)}, bf16[288,128]{1,0:T(8,128)(2,1)S(1)}, u32[]{:S(2)}, u32[]{:S(2)}) collective-permute-start(bf16[288,128]{1,0:T(8,128)(2,1)S(1)} %shard_map.155.x0_ref), channel_id=1, source_target_pairs={{0,192},{64,0},{128,64},{192,128},{1,193},{65,1},{129,65},{193,129... | collective-permute-start | bytes 221192 | tf_op jit(solution)/shard_map/ppermute | solution.py:290
  67.6 6.6 %collective-permute-start.4 = (bf16[288,128]{1,0:T(8,128)(2,1)S(1)}, bf16[288,128]{1,0:T(8,128)(2,1)S(1)}, u32[]{:S(2)}, u32[]{:S(2)}) collective-permute-start(bf16[288,128]{1,0:T(8,128)(2,1)S(1)} %shard_map.155.x0_ref), channel_id=1, source_target_pairs={{0,128},{64,192},{128,0},{192,64},{1,129},{65,193},{129,1},{193,65... | collective-permute-start | bytes 221192 | tf_op jit(solution)/shard_map/ppermute | solution.py:290
  68.4 6.6 %collective-permute-start.3 = (bf16[288,128]{1,0:T(8,128)(2,1)S(1)}, bf16[288,128]{1,0:T(8,128)(2,1)S(1)}, u32[]{:S(2)}, u32[]{:S(2)}) collective-permute-start(bf16[288,128]{1,0:T(8,128)(2,1)S(1)} %shard_map.155.x0_ref), channel_id=1, source_target_pairs={{0,64},{64,128},{128,192},{192,0},{1,65},{65,129},{129,193},{193,1... | collective-permute-start | bytes 221192 | tf_op jit(solution)/shard_map/ppermute | solution.py:290
  75.0 23.0 %copy-start.3 = (f32[1,512,128]{2,1,0:T(8,128)S(1)}, f32[1,512,128]{2,1,0:T(8,128)}, u32[]{:S(2)}) copy-start(f32[1,512,128]{2,1,0:T(8,128)} %param.20) | copy-start | bytes 786436
  75.0 22.9 %copy-start.5 = (f32[1,512]{1,0:T(1,128)S(1)}, f32[1,512]{1,0:T(1,128)}, u32[]{:S(2)}) copy-start(f32[1,512]{1,0:T(1,128)} %accum_ref.1) | copy-start | bytes 6148
  91.6 18.7 %collective-permute-start.12 = (bf16[32,32,128]{2,1,0:T(8,128)(2,1)S(1)}, bf16[32,32,128]{2,1,0:T(8,128)(2,1)S(1)}, u32[]{:S(2)}, u32[]{:S(2)}) collective-permute-start(bf16[32,32,128]{2,1,0:T(8,128)(2,1)S(1)} %all_to_all.20.mine_ref), channel_id=1, source_target_pairs={{0,1},{1,0},{2,3},{3,2},{4,5},{5,4},{6,7},{7,6},{8,9},{9,8},{10,11... | collective-permute-start | bytes 786440 | tf_op jit(solution)/shard_map/ppermute | solution.py:295
  91.7 3.6 %collective-permute-start.8 = (s32[8,128]{1,0:T(8,128)S(1)}, s32[8,128]{1,0:T(8,128)S(1)}, u32[]{:S(2)}, u32[]{:S(2)}) collective-permute-start(s32[8,128]{1,0:T(8,128)S(1)} %get-tuple-element.45.h0_ref), channel_id=1, source_target_pairs={{0,192},{64,0},{128,64},{192,128},{1,193},{65,1},{129,65},{193,129... | collective-permute-start | bytes 12296 | tf_op jit(solution)/shard_map/ppermute | solution.py:290
  91.7 5.1 %collective-permute-start.7 = (s32[8,128]{1,0:T(8,128)S(1)}, s32[8,128]{1,0:T(8,128)S(1)}, u32[]{:S(2)}, u32[]{:S(2)}) collective-permute-start(s32[8,128]{1,0:T(8,128)S(1)} %get-tuple-element.45.h0_ref), channel_id=1, source_target_pairs={{0,128},{64,192},{128,0},{192,64},{1,129},{65,193},{129,1},{193,65... | collective-permute-start | bytes 12296 | tf_op jit(solution)/shard_map/ppermute | solution.py:290
  92.4 5.5 %collective-permute-start.6 = (s32[8,128]{1,0:T(8,128)S(1)}, s32[8,128]{1,0:T(8,128)S(1)}, u32[]{:S(2)}, u32[]{:S(2)}) collective-permute-start(s32[8,128]{1,0:T(8,128)S(1)} %get-tuple-element.45.h0_ref), channel_id=1, source_target_pairs={{0,64},{64,128},{128,192},{192,0},{1,65},{65,129},{129,193},{193,1... | collective-permute-start | bytes 12296 | tf_op jit(solution)/shard_map/ppermute | solution.py:290
  99.1 6.8 %collective-permute-start.11 = (bf16[528,128]{1,0:T(8,128)(2,1)S(1)}, bf16[528,128]{1,0:T(8,128)(2,1)S(1)}, u32[]{:S(2)}, u32[]{:S(2)}) collective-permute-start(bf16[528,128]{1,0:T(8,128)(2,1)S(1)} %get-tuple-element.48.s0_ref), channel_id=1, source_target_pairs={{0,192},{64,0},{128,64},{192,128},{1,193},{65,1},{129,65},{193,129... | collective-permute-start | bytes 405512 | tf_op jit(solution)/shard_map/ppermute | solution.py:290
  101.1 7.0 %collective-permute-start.10 = (bf16[528,128]{1,0:T(8,128)(2,1)S(1)}, bf16[528,128]{1,0:T(8,128)(2,1)S(1)}, u32[]{:S(2)}, u32[]{:S(2)}) collective-permute-start(bf16[528,128]{1,0:T(8,128)(2,1)S(1)} %get-tuple-element.48.s0_ref), channel_id=1, source_target_pairs={{0,128},{64,192},{128,0},{192,64},{1,129},{65,193},{129,1},{193,65... | collective-permute-start | bytes 405512 | tf_op jit(solution)/shard_map/ppermute | solution.py:290
  102.0 7.5 %collective-permute-start.9 = (bf16[528,128]{1,0:T(8,128)(2,1)S(1)}, bf16[528,128]{1,0:T(8,128)(2,1)S(1)}, u32[]{:S(2)}, u32[]{:S(2)}) collective-permute-start(bf16[528,128]{1,0:T(8,128)(2,1)S(1)} %get-tuple-element.48.s0_ref), channel_id=1, source_target_pairs={{0,64},{64,128},{128,192},{192,0},{1,65},{65,129},{129,193},{193,1... | collective-permute-start | bytes 405512 | tf_op jit(solution)/shard_map/ppermute | solution.py:290

commit v5 on v3

--- a/solution.py
+++ b/solution.py
@@ -211,7 +211,7 @@
 def top_kernel(me_ref, x0_ref, x1_ref, x2_ref, x3_ref, top_ref, by_group):
     me = me_ref[0]
     for o, ref in enumerate((x0_ref, x1_ref, x2_ref, x3_ref)):
-        by_group[(me - o) & 3] = ref[SPAN : SPAN + 32, :]
+        by_group[me ^ o] = ref[SPAN : SPAN + 32, :]
     top = jnp.zeros((32, D), F32)
     for g in range(N_GRP):
         top = top + by_group[g].astype(F32)
@@ -224,7 +224,7 @@
 ):
     me = me_ref[0]
     for o, ref in enumerate((x0_ref, x1_ref, x2_ref, x3_ref)):
-        by_group[(me - o) & 3] = ref[...]
+        by_group[me ^ o] = ref[...]
     hot = [by_group[g, SPAN + 32 : SPAN + 48, :].astype(F32)[0:1, :] for g in range(N_GRP)]
     a, b = iota((BLOCK, BLOCK), 0), iota((BLOCK, BLOCK), 1)
     diagonal = a == b
@@ -258,7 +258,7 @@
     me = me_ref[0]
     scales = jnp.zeros((16, D), F32)
     for o, ref in enumerate((s0_ref, s1_ref, s2_ref, s3_ref)):
-        start = pl.multiple_of(((me - o) & 3) * QUARTER, QUARTER)
+        start = pl.multiple_of((me ^ o) * QUARTER, QUARTER)
         serving_ref[pl.ds(start, QUARTER), :] = ref[0:QUARTER, :]
         scales = scales + ref[QUARTER : QUARTER + 16, :].astype(F32)
     scale_ref[...] = scales[0:1, 0:16].astype(BF16)
@@ -282,7 +282,7 @@
 def over_groups(x):
     parts = [x]
     for o in (1, 2, 3):
-        parts.append(lax.ppermute(x, "grp", [(g, (g + o) % N_GRP) for g in range(N_GRP)]))
+        parts.append(lax.ppermute(x, "grp", [(g, g ^ o) for g in range(N_GRP)]))
     return parts
 
 

time: 108 us -> 106 us (0.981)
  the two profiles are of different devices: /device:TPU:1 before, /device:TPU:8 now
where the time goes in v5:
time: 106 us; the launch traced here: 104 us
  waiting for transfers between devices  41.3 us (39%)
  starting transfers between devices  31.2 us (29%)
  blocking collectives  15.8 us (15%)
  Pallas kernels  12.2 us (12%)
  local copies, waits for them, and re-layouts  3.1 us (3%)
    all_to_all x3, waiting for transfers between devices, exchange(): return lax.all_to_all(x, axes, 0, 0, tiled=True)  27.5 us
    all_to_all x3, starting transfers between devices, exchange(): return lax.all_to_all(x, axes, 0, 0, tiled=True)  22.5 us
    all_to_all x1, blocking collectives, exchange(): return lax.all_to_all(x, axes, 0, 0, tiled=True)  15.8 us
    pallas_call x14, Pallas kernels, call(): pl.pallas_call(kernel, out_shape=outs, in_specs=specs, out_specs=[VM] * l...  12.2 us
    ppermute x6, waiting for transfers between devices, over_groups(): parts.append(lax.ppermute(x, 'grp', [(g, g ^ o) for g in range(N_GRP)]))  12 us
    ppermute x6, starting transfers between devices, over_groups(): parts.append(lax.ppermute(x, 'grp', [(g, g ^ o) for g in range(N_GRP)]))  8.27 us
    unnamed x24, local copies, waits for them, and re-layouts  3.1 us
  transfers between devices with their start and end apart: 13, of which 9 were waited for; matrix products, arithmetic and copies ran while one was open for 0% of the time, Pallas kernels for 6%

profile of v5, /device:TPU:8, one launch (start us, length us, event | category | flops | bytes accessed | tf_op | source)
XLA Modules:
  0.0 104.4 jit_solution(13469656360635566595)
XLA Ops:
  0.6 0.0 copy-start
  0.6 0.0 copy-start.1
  0.7 1.1 %copy-done.1 = bf16[2048,128]{1,0:T(8,128)(2,1)S(1)} copy-done((bf16[2048,128]{1,0:T(8,128)(2,1)S(1)}, bf16[2048,128]{1,0:T(8,128)(2,1)}, u32[]{:S(2)}) %copy-start.1) | copy-done | bytes 524312
  1.7 0.0 copy-start.6
  1.7 0.7 copy-done.6
  2.4 0.0 copy-start.9
  2.4 0.7 copy-done.9
  3.1 0.0 copy-start.10
  3.1 0.8 shard_map.147.table_ref
  3.9 0.1 collective-permute-start
  4.0 0.0 copy-done.10
  4.0 1.2 %shard_map.146 = s32[64,128]{1,0:T(8,128)} custom-call(s32[1,1024]{1,0:T(1,128)S(1)} %copy-done.10), custom_call_target="tpu_custom_call" | custom-call | flops 67108864 | bytes 36864 | tf_op jit(solution)/shard_map/pallas_call | solution.py:49
  5.1 0.0 copy-start.2
  5.2 11.8 %all-to-all-start = ((s32[32,2,128]{2,1,0:T(2,128)}), s32[32,2,128]{2,1,0:T(2,128)S(1)}, u32[]{:S(2)}, u32[]{:S(2)}) async-start(s32[32,2,128]{2,1,0:T(2,128)} %bitcast.2), calls=%async_computation | async-start | bytes 65536 | tf_op jit(solution)/shard_map/all_to_all | solution.py:294
  17.0 0.0 copy-start.4
  17.0 0.0 copy-start.8
  17.0 0.0 copy-done
  17.0 0.0 copy-done.2
  17.0 0.6 copy-done.4
  17.7 0.0 copy-done.8
  17.7 0.3 shard_map.148
  18.0 7.7 %all-to-all-done = s32[32,2,128]{2,1,0:T(2,128)S(1)} async-done(((s32[32,2,128]{2,1,0:T(2,128)}), s32[32,2,128]{2,1,0:T(2,128)S(1)}, u32[]{:S(2)}, u32[]{:S(2)}) %all-to-all-start) | async-done | bytes 32800 | tf_op jit(solution)/shard_map/all_to_all | solution.py:294
  25.7 0.0 collective-permute-done.other_ref
  25.7 1.2 %shard_map.149 = bf16[512,128]{1,0:T(8,128)(2,1)} custom-call(s32[1]{0:T(128)} %bitcast.1.core_ref, s32[64,128]{1,0:T(8,128)S(1)} %bitcast.16, bf16[256,128]{1,0:T(8,128)(2,1)S(1)} %shard_map.147.table_ref, bf16[256,128]{1,0:T(8,128)(2,1)S(1)} %collective-permute-done.other_ref), custom_call_target="tpu_custom_call" | custom-call | flops 67108864 | bytes 294916 | tf_op jit(solution)/shard_map/pallas_call | solution.py:49
  26.9 0.0 copy-start.11
  26.9 5.1 %all-to-all-start.1 = ((bf16[32,16,128]{2,1,0:T(8,128)(2,1)}), bf16[32,16,128]{2,1,0:T(8,128)(2,1)S(1)}, u32[]{:S(2)}, u32[]{:S(2)}) async-start(bf16[32,16,128]{2,1,0:T(8,128)(2,1)} %bitcast.7), calls=%async_computation.1 | async-start | bytes 262144 | tf_op jit(solution)/shard_map/all_to_all | solution.py:294
  32.0 0.0 copy-done.11
  32.0 1.9 %shard_map.150 = (bf16[256,512]{1,0:T(8,128)(2,1)S(1)}, bf16[512,256]{1,0:T(8,128)(2,1)S(1)}) custom-call(s32[1,1024]{1,0:T(1,128)S(1)} %copy-done.10, s32[1,256]{1,0:T(1,128)S(1)} %copy-done.11), custom_call_target="tpu_custom_call" | custom-call | flops 536870912 | bytes 529408 | tf_op jit(solution)/shard_map/pallas_call | solution.py:49
  33.9 7.4 %all-to-all-done.1 = bf16[32,16,128]{2,1,0:T(8,128)(2,1)S(1)} async-done(((bf16[32,16,128]{2,1,0:T(8,128)(2,1)}), bf16[32,16,128]{2,1,0:T(8,128)(2,1)S(1)}, u32[]{:S(2)}, u32[]{:S(2)}) %all-to-all-start.1) | async-done | bytes 131104 | tf_op jit(solution)/shard_map/all_to_all | solution.py:294
  41.3 1.0 shard_map.151
  42.3 0.1 collective-permute-start.1
  42.4 0.9 shard_map.152
  43.3 0.6 collective-permute-done.1.given_ref
  43.9 0.8 shard_map.153
  44.7 5.6 %all-to-all-start.2 = ((bf16[64,24,128]{2,1,0:T(8,128)(2,1)}), bf16[64,24,128]{2,1,0:T(8,128)(2,1)S(1)}, u32[]{:S(2)}, u32[]{:S(2)}) async-start(bf16[64,24,128]{2,1,0:T(8,128)(2,1)} %shard_map.153), calls=%async_computation.2 | async-start | bytes 786432 | tf_op jit(solution)/shard_map/all_to_all | solution.py:294
  50.3 0.2 collective-permute-start.2
  50.5 1.1 %collective-permute-done.2.other_ref = s32[64,128]{1,0:T(8,128)S(1)} collective-permute-done((s32[64,128]{1,0:T(8,128)S(1)}, s32[64,128]{1,0:T(8,128)S(1)}, u32[]{:S(2)}, u32[]{:S(2)}) %collective-permute-start.2) | collective-permute-done | bytes 32800 | tf_op jit(solution)/shard_map/ppermute | solution.py:290
  51.6 0.4 shard_map.154.place_ref
  52.0 0.0 copy-start.7
  52.0 12.4 %all-to-all-done.2 = bf16[64,24,128]{2,1,0:T(8,128)(2,1)S(1)} async-done(((bf16[64,24,128]{2,1,0:T(8,128)(2,1)}), bf16[64,24,128]{2,1,0:T(8,128)(2,1)S(1)}, u32[]{:S(2)}, u32[]{:S(2)}) %all-to-all-start.2) | async-done | bytes 393248 | tf_op jit(solution)/shard_map/all_to_all | solution.py:294
  64.4 0.0 copy-done.7
  64.4 0.8 shard_map.155.x0_ref
  65.2 2.8 %collective-permute-start.5 = (bf16[304,128]{1,0:T(8,128)(2,1)S(1)}, bf16[304,128]{1,0:T(8,128)(2,1)S(1)}, u32[]{:S(2)}, u32[]{:S(2)}) collective-permute-start(bf16[304,128]{1,0:T(8,128)(2,1)S(1)} %shard_map.155.x0_ref), channel_id=1, source_target_pairs={{0,192},{64,128},{128,64},{192,0},{1,193},{65,129},{129,65},{193,1... | collective-permute-start | bytes 233480 | tf_op jit(solution)/shard_map/ppermute | solution.py:285
  68.0 0.8 collective-permute-start.4
  68.8 0.5 collective-permute-start.3
  69.4 2.5 %collective-permute-done.5.x3_ref = bf16[304,128]{1,0:T(8,128)(2,1)S(1)} collective-permute-done((bf16[304,128]{1,0:T(8,128)(2,1)S(1)}, bf16[304,128]{1,0:T(8,128)(2,1)S(1)}, u32[]{:S(2)}, u32[]{:S(2)}) %collective-permute-start.5) | collective-permute-done | bytes 77856 | tf_op jit(solution)/shard_map/ppermute | solution.py:285
  71.9 2.8 %collective-permute-done.4.x2_ref = bf16[304,128]{1,0:T(8,128)(2,1)S(1)} collective-permute-done((bf16[304,128]{1,0:T(8,128)(2,1)S(1)}, bf16[304,128]{1,0:T(8,128)(2,1)S(1)}, u32[]{:S(2)}, u32[]{:S(2)}) %collective-permute-start.4) | collective-permute-done | bytes 77856 | tf_op jit(solution)/shard_map/ppermute | solution.py:285
  74.7 0.0 collective-permute-done.3.x1_ref
  74.8 0.0 copy-start.3
  74.8 0.0 copy-start.5
  74.8 15.8 %all_to_all.20.mine_ref = bf16[32,32,128]{2,1,0:T(8,128)(2,1)S(1)} all-to-all(bf16[32,32,128]{2,1,0:T(8,128)(2,1)S(1)} %shard_map.158), channel_id=1, replica_groups=mesh['grp'=4,'row_0'=4,'row_1'=8,'row_2'=2] {'row_0','row_1'}, dimensions={0} | all-to-all | bytes 524288 | tf_op jit(solution)/shard_map/all_to_all | solution.py:294
  90.6 0.0 collective-permute-start.9
  90.6 0.0 copy-done.3
  90.6 0.0 copy-done.5
  90.6 1.2 %shard_map.156 = (f32[512,128]{1,0:T(8,128)}, f32[1,512]{1,0:T(1,128)}, bf16[528,128]{1,0:T(8,128)(2,1)S(1)}) custom-call(s32[1]{0:T(128)} %bitcast.me_ref, bf16[304,128]{1,0:T(8,128)(2,1)S(1)} %shard_map.155.x0_ref, bf16[304,128]{1,0:T(8,128)(2,1)S(1)} %collective-permute-done.3.x1_ref, bf16[304,128]{1,0:T(8,128)(2,1)S(1)} %collective-permute-done.4.x2_ref, ...), custom_call_target="tpu_custom_call" | custom-call | flops 4194304 | bytes 974852 | tf_op jit(solution)/shard_map/pallas_call | solution.py:49
  91.8 1.6 %collective-permute-start.8 = (bf16[528,128]{1,0:T(8,128)(2,1)S(1)}, bf16[528,128]{1,0:T(8,128)(2,1)S(1)}, u32[]{:S(2)}, u32[]{:S(2)}) collective-permute-start(bf16[528,128]{1,0:T(8,128)(2,1)S(1)} %get-tuple-element.44.s0_ref), channel_id=1, source_target_pairs={{0,192},{64,128},{128,64},{192,0},{1,193},{65,129},{129,65},{193,1... | collective-permute-start | bytes 405512 | tf_op jit(solution)/shard_map/ppermute | solution.py:285
  93.4 0.8 collective-permute-start.7
  94.2 1.6 %collective-permute-start.6 = (bf16[528,128]{1,0:T(8,128)(2,1)S(1)}, bf16[528,128]{1,0:T(8,128)(2,1)S(1)}, u32[]{:S(2)}, u32[]{:S(2)}) collective-permute-start(bf16[528,128]{1,0:T(8,128)(2,1)S(1)} %get-tuple-element.44.s0_ref), channel_id=1, source_target_pairs={{0,64},{64,0},{128,192},{192,128},{1,65},{65,1},{129,193},{193,129... | collective-permute-start | bytes 405512 | tf_op jit(solution)/shard_map/ppermute | solution.py:285
  95.9 6.0 %collective-permute-done.8.s3_ref = bf16[528,128]{1,0:T(8,128)(2,1)S(1)} collective-permute-done((bf16[528,128]{1,0:T(8,128)(2,1)S(1)}, bf16[528,128]{1,0:T(8,128)(2,1)S(1)}, u32[]{:S(2)}, u32[]{:S(2)}) %collective-permute-start.8) | collective-permute-done | bytes 135200 | tf_op jit(solution)/shard_map/ppermute | solution.py:285
  101.9 0.0 collective-permute-done.7.s2_ref
  101.9 0.6 collective-permute-done.6.s1_ref
  102.5 0.8 shard_map.157
  103.3 0.0 collective-permute-done.9.other_ref
  103.3 1.1 %shard_map.159 = f32[256,1024]{1,0:T(8,128)} custom-call(s32[1]{0:T(128)} %bitcast.1.core_ref, bf16[32,32,128]{2,1,0:T(8,128)(2,1)S(1)} %all_to_all.20.mine_ref, bf16[32,32,128]{2,1,0:T(8,128)(2,1)S(1)} %collective-permute-done.9.other_ref), custom_call_target="tpu_custom_call" | custom-call | flops 1048576 | bytes 1572868 | tf_op jit(solution)/shard_map/pallas_call | solution.py:49
  (1 shorter events, 0.0 us)
Async XLA Ops:
  0.6 16.4 %copy-start = (bf16[256,1024]{1,0:T(8,128)(2,1)S(1)}, bf16[256,1024]{1,0:T(8,128)(2,1)}, u32[]{:S(2)}) copy-start(bf16[256,1024]{1,0:T(8,128)(2,1)} %w_ref.5) | copy-start | bytes 1572868
  0.6 1.1 %copy-start.1 = (bf16[2048,128]{1,0:T(8,128)(2,1)S(1)}, bf16[2048,128]{1,0:T(8,128)(2,1)}, u32[]{:S(2)}) copy-start(bf16[2048,128]{1,0:T(8,128)(2,1)} %serving_ref.1) | copy-start | bytes 1572868
  1.7 0.7 copy-start.6
  2.4 0.7 copy-start.9
  3.1 0.9 copy-start.10
  3.9 21.8 %collective-permute-start = (bf16[256,128]{1,0:T(8,128)(2,1)S(1)}, bf16[256,128]{1,0:T(8,128)(2,1)S(1)}, u32[]{:S(2)}, u32[]{:S(2)}) collective-permute-start(bf16[256,128]{1,0:T(8,128)(2,1)S(1)} %shard_map.147.table_ref), channel_id=1, source_target_pairs={{0,1},{1,0},{2,3},{3,2},{4,5},{5,4},{6,7},{7,6},{8,9},{9,8},{10,11... | collective-permute-start | bytes 196616 | tf_op jit(solution)/shard_map/ppermute | solution.py:290
  5.1 11.9 %copy-start.2 = (bf16[256,128]{1,0:T(8,128)(2,1)S(1)}, bf16[256,128]{1,0:T(8,128)(2,1)}, u32[]{:S(2)}) copy-start(bf16[256,128]{1,0:T(8,128)(2,1)} %dense_ref.3) | copy-start | bytes 196612
  5.2 20.6 %all-to-all-start = ((s32[32,2,128]{2,1,0:T(2,128)}), s32[32,2,128]{2,1,0:T(2,128)S(1)}, u32[]{:S(2)}, u32[]{:S(2)}) async-start(s32[32,2,128]{2,1,0:T(2,128)} %bitcast.2), calls=%async_computation | async-start | bytes 65536 | tf_op jit(solution)/shard_map/all_to_all | solution.py:294
  17.0 0.7 copy-start.4
  17.0 0.7 copy-start.8
  26.9 5.1 %copy-start.11 = (s32[1,256]{1,0:T(1,128)S(1)}, s32[1,256]{1,0:T(1,128)}, u32[]{:S(2)}) copy-start(s32[1,256]{1,0:T(1,128)} %len_ref.1) | copy-start | bytes 3076
  26.9 14.4 %all-to-all-start.1 = ((bf16[32,16,128]{2,1,0:T(8,128)(2,1)}), bf16[32,16,128]{2,1,0:T(8,128)(2,1)S(1)}, u32[]{:S(2)}, u32[]{:S(2)}) async-start(bf16[32,16,128]{2,1,0:T(8,128)(2,1)} %bitcast.7), calls=%async_computation.1 | async-start | bytes 262144 | tf_op jit(solution)/shard_map/all_to_all | solution.py:294
  42.3 1.6 %collective-permute-start.1 = (bf16[64,16,128]{2,1,0:T(8,128)(2,1)S(1)}, bf16[64,16,128]{2,1,0:T(8,128)(2,1)S(1)}, u32[]{:S(2)}, u32[]{:S(2)}) collective-permute-start(bf16[64,16,128]{2,1,0:T(8,128)(2,1)S(1)} %get-tuple-element.40), channel_id=1, source_target_pairs={{0,1},{1,0},{2,3},{3,2},{4,5},{5,4},{6,7},{7,6},{8,9},{9,8},{10,11... | collective-permute-start | bytes 786440 | tf_op jit(solution)/shard_map/ppermute | solution.py:290
  44.7 19.7 %all-to-all-start.2 = ((bf16[64,24,128]{2,1,0:T(8,128)(2,1)}), bf16[64,24,128]{2,1,0:T(8,128)(2,1)S(1)}, u32[]{:S(2)}, u32[]{:S(2)}) async-start(bf16[64,24,128]{2,1,0:T(8,128)(2,1)} %shard_map.153), calls=%async_computation.2 | async-start | bytes 786432 | tf_op jit(solution)/shard_map/all_to_all | solution.py:294
  50.3 1.3 %collective-permute-start.2 = (s32[64,128]{1,0:T(8,128)S(1)}, s32[64,128]{1,0:T(8,128)S(1)}, u32[]{:S(2)}, u32[]{:S(2)}) collective-permute-start(s32[64,128]{1,0:T(8,128)S(1)} %bitcast.17), channel_id=1, source_target_pairs={{0,1},{1,0},{2,3},{3,2},{4,5},{5,4},{6,7},{7,6},{8,9},{9,8},{10,11... | collective-permute-start | bytes 98312 | tf_op jit(solution)/shard_map/ppermute | solution.py:290
  52.0 12.4 %copy-start.7 = (s32[1,2]{1,0:T(1,128)S(1)}, s32[1,2]{1,0:T(1,128)}, u32[]{:S(2)}) copy-start(s32[1,2]{1,0:T(1,128)} %hot_ref.3) | copy-start | bytes 28
  65.2 6.7 %collective-permute-start.5 = (bf16[304,128]{1,0:T(8,128)(2,1)S(1)}, bf16[304,128]{1,0:T(8,128)(2,1)S(1)}, u32[]{:S(2)}, u32[]{:S(2)}) collective-permute-start(bf16[304,128]{1,0:T(8,128)(2,1)S(1)} %shard_map.155.x0_ref), channel_id=1, source_target_pairs={{0,192},{64,128},{128,64},{192,0},{1,193},{65,129},{129,65},{193,1... | collective-permute-start | bytes 233480 | tf_op jit(solution)/shard_map/ppermute | solution.py:285
  68.0 6.7 %collective-permute-start.4 = (bf16[304,128]{1,0:T(8,128)(2,1)S(1)}, bf16[304,128]{1,0:T(8,128)(2,1)S(1)}, u32[]{:S(2)}, u32[]{:S(2)}) collective-permute-start(bf16[304,128]{1,0:T(8,128)(2,1)S(1)} %shard_map.155.x0_ref), channel_id=1, source_target_pairs={{0,128},{64,192},{128,0},{192,64},{1,129},{65,193},{129,1},{193,65... | collective-permute-start | bytes 233480 | tf_op jit(solution)/shard_map/ppermute | solution.py:285
  68.8 5.9 %collective-permute-start.3 = (bf16[304,128]{1,0:T(8,128)(2,1)S(1)}, bf16[304,128]{1,0:T(8,128)(2,1)S(1)}, u32[]{:S(2)}, u32[]{:S(2)}) collective-permute-start(bf16[304,128]{1,0:T(8,128)(2,1)S(1)} %shard_map.155.x0_ref), channel_id=1, source_target_pairs={{0,64},{64,0},{128,192},{192,128},{1,65},{65,1},{129,193},{193,129... | collective-permute-start | bytes 233480 | tf_op jit(solution)/shard_map/ppermute | solution.py:285
  74.8 15.8 %copy-start.3 = (f32[1,512,128]{2,1,0:T(8,128)S(1)}, f32[1,512,128]{2,1,0:T(8,128)}, u32[]{:S(2)}) copy-start(f32[1,512,128]{2,1,0:T(8,128)} %param.20) | copy-start | bytes 786436
  74.8 15.8 %copy-start.5 = (f32[1,512]{1,0:T(1,128)S(1)}, f32[1,512]{1,0:T(1,128)}, u32[]{:S(2)}) copy-start(f32[1,512]{1,0:T(1,128)} %accum_ref.1) | copy-start | bytes 6148
  90.6 12.7 %collective-permute-start.9 = (bf16[32,32,128]{2,1,0:T(8,128)(2,1)S(1)}, bf16[32,32,128]{2,1,0:T(8,128)(2,1)S(1)}, u32[]{:S(2)}, u32[]{:S(2)}) collective-permute-start(bf16[32,32,128]{2,1,0:T(8,128)(2,1)S(1)} %all_to_all.20.mine_ref), channel_id=1, source_target_pairs={{0,1},{1,0},{2,3},{3,2},{4,5},{5,4},{6,7},{7,6},{8,9},{9,8},{10,11... | collective-permute-start | bytes 786440 | tf_op jit(solution)/shard_map/ppermute | solution.py:290
  91.8 10.1 %collective-permute-start.8 = (bf16[528,128]{1,0:T(8,128)(2,1)S(1)}, bf16[528,128]{1,0:T(8,128)(2,1)S(1)}, u32[]{:S(2)}, u32[]{:S(2)}) collective-permute-start(bf16[528,128]{1,0:T(8,128)(2,1)S(1)} %get-tuple-element.44.s0_ref), channel_id=1, source_target_pairs={{0,192},{64,128},{128,64},{192,0},{1,193},{65,129},{129,65},{193,1... | collective-permute-start | bytes 405512 | tf_op jit(solution)/shard_map/ppermute | solution.py:285
  93.4 8.5 %collective-permute-start.7 = (bf16[528,128]{1,0:T(8,128)(2,1)S(1)}, bf16[528,128]{1,0:T(8,128)(2,1)S(1)}, u32[]{:S(2)}, u32[]{:S(2)}) collective-permute-start(bf16[528,128]{1,0:T(8,128)(2,1)S(1)} %get-tuple-element.44.s0_ref), channel_id=1, source_target_pairs={{0,128},{64,192},{128,0},{192,64},{1,129},{65,193},{129,1},{193,65... | collective-permute-start | bytes 405512 | tf_op jit(solution)/shard_map/ppermute | solution.py:285
  94.2 8.3 %collective-permute-start.6 = (bf16[528,128]{1,0:T(8,128)(2,1)S(1)}, bf16[528,128]{1,0:T(8,128)(2,1)S(1)}, u32[]{:S(2)}, u32[]{:S(2)}) collective-permute-start(bf16[528,128]{1,0:T(8,128)(2,1)S(1)} %get-tuple-element.44.s0_ref), channel_id=1, source_target_pairs={{0,64},{64,0},{128,192},{192,128},{1,65},{65,1},{129,193},{193,129... | collective-permute-start | bytes 405512 | tf_op jit(solution)/shard_map/ppermute | solution.py:285

commit v6 on v5

--- a/solution.py
+++ b/solution.py
@@ -42,7 +42,7 @@
     return jnp.where(mask, 1.0, 0.0).astype(BF16)
 
 
-def call(kernel, outs, specs, args, flops, scratch=()):
+def call(kernel, outs, specs, args, flops, scratch=(), out_specs=None, grid=()):
     bytes_accessed = sum(a.size * a.dtype.itemsize for a in args) + sum(
         o.size * o.dtype.itemsize for o in outs
     )
@@ -50,7 +50,8 @@
         kernel,
         out_shape=outs,
         in_specs=specs,
-        out_specs=[VM] * len(outs),
+        out_specs=out_specs or [VM] * len(outs),
+        grid=grid,
         cost_estimate=pl.CostEstimate(
             flops=flops, bytes_accessed=bytes_accessed, transcendentals=0
         ),
@@ -126,9 +127,9 @@
     owner = ones_where(lax.shift_right_logical(iota((SLOTS, N_ROW), 0), 3) == iota((SLOTS, N_ROW), 1))
     spread = dot(owner, ids_ref[...].astype(F32).astype(BF16))
     mine = iota((SLOTS, D), 1) == (iota((SLOTS, D), 0) & (CAP - 1))
-    column = jnp.sum(jnp.where(mine, spread, 0.0), axis=1, keepdims=True).astype(I32)
+    column = dot(jnp.where(mine, spread, 0.0).astype(BF16), jnp.ones((D, SPAN), BF16))
     here = lax.shift_right_logical(iota((SLOTS, SPAN), 0), 3) & 1 == core_ref[0]
-    match = iota((SLOTS, SPAN), 1) == column
+    match = iota((SLOTS, SPAN), 1) == column.astype(I32)
     rows = dot(ones_where(match & here), table_ref[...])
     rows_ref[...] = (rows + dot(ones_where(match & ~here), other_ref[...])).astype(BF16)
 
@@ -191,8 +192,9 @@
 
 
 def parts_kernel(keep_ref, given_ref, row_grad_ref, out_ref):
-    out_ref[:, 0:16, :] = (keep_ref[...] + given_ref[...].astype(F32)).astype(BF16)
-    out_ref[:, 16:24, :] = row_grad_ref[...]
+    at = pl.ds(pl.program_id(0) * 16, 16)
+    out_ref[:, 0:16, :] = (keep_ref[at] + given_ref[at].astype(F32)).astype(BF16)
+    out_ref[:, 16:24, :] = row_grad_ref[at]
 
 
 def owned_kernel(got_ref, place_ref, hot_ref, out_ref):
@@ -265,14 +267,15 @@
 
 
 def last_kernel(core_ref, mine_ref, other_ref, top_ref):
+    step = pl.program_id(0)
+    half = pl.ds(pl.multiple_of(step // 2 * 16, 16), 16)
     for ref, core in ((mine_ref, core_ref[0]), (other_ref, 1 - core_ref[0])):
-        for s in range(N_ROW // 2):
+        for s in range(16):
             column = pl.multiple_of((s % 4 * 2 + core) * 128, 128)
-            for half in range(2):
-                line = half * 128 + s // 4 * 16
-                top_ref[line : line + 16, pl.ds(column, 128)] = ref[
-                    s, half * 16 : (half + 1) * 16, :
-                ].astype(F32)
+            line = s // 4 * 16
+            top_ref[line : line + 16, pl.ds(column, 128)] = ref[
+                step % 2 * 16 + s, half, :
+            ].astype(F32)
 
 
 def like(shape, dtype):
@@ -364,6 +367,8 @@
         [VM] * 3,
         (kept, given, row_grad.reshape(N_ROW, CAP, D)),
         1 << 20,
+        out_specs=[pl.BlockSpec((16, 24, D), lambda i: (i, 0, 0))],
+        grid=(4,),
     )
     got = exchange(parts)
     (own,) = call(
@@ -401,7 +406,13 @@
     )
     top_other = other_core(top_mine)
     (top_grad,) = call(
-        last_kernel, [like((2 * D, FF), F32)], [SM] + [VM] * 2, (core, top_mine, top_other), 1 << 20
+        last_kernel,
+        [like((2 * D, FF), F32)],
+        [SM] + [VM] * 2,
+        (core, top_mine, top_other),
+        1 << 20,
+        out_specs=[pl.BlockSpec((64, FF), lambda i: (i, 0))],
+        grid=(4,),
     )
     return new_master[None], new_accum, fresh, fresh_scale.reshape(16), top_grad
 

time: 106 us -> 108 us (1.019)
  the two profiles are of different devices: /device:TPU:8 before, /device:TPU:1 now
where the time goes in v6:
time: 108 us; the launch traced here: 107 us
  waiting for transfers between devices  39.4 us (36%)
  starting transfers between devices  35.9 us (33%)
  blocking collectives  14.8 us (14%)
  Pallas kernels  13.3 us (12%)
  local copies, waits for them, and re-layouts  3.1 us (3%)
    all_to_all x3, waiting for transfers between devices, exchange(): return lax.all_to_all(x, axes, 0, 0, tiled=True)  27.8 us
    all_to_all x3, starting transfers between devices, exchange(): return lax.all_to_all(x, axes, 0, 0, tiled=True)  18.1 us
    all_to_all x1, blocking collectives, exchange(): return lax.all_to_all(x, axes, 0, 0, tiled=True)  14.8 us
    pallas_call x14, Pallas kernels, call(): pl.pallas_call(kernel, out_shape=outs, in_specs=specs, out_specs=out_spec...  13.3 us
    ppermute x4, starting transfers between devices, other_core(): return lax.ppermute(x, 'row_2', [(0, 1), (1, 0)])  11.2 us
    ppermute x6, waiting for transfers between devices, over_groups(): parts.append(lax.ppermute(x, 'grp', [(g, g ^ o) for g in range(N_GRP)]))  10.4 us
    ppermute x6, starting transfers between devices, over_groups(): parts.append(lax.ppermute(x, 'grp', [(g, g ^ o) for g in range(N_GRP)]))  6.59 us
    unnamed x24, local copies, waits for them, and re-layouts  3.1 us
  transfers between devices with their start and end apart: 13, of which 10 were waited for; matrix products, arithmetic and copies ran while one was open for 0% of the time, Pallas kernels for 6%

profile of v6, /device:TPU:1, one launch (start us, length us, event | category | flops | bytes accessed | tf_op | source)
XLA Modules:
  0.0 107.2 jit_solution(4840733727888322563)
XLA Ops:
  0.6 0.0 copy-start
  0.6 0.0 copy-start.1
  0.7 1.1 %copy-done.1 = bf16[2048,128]{1,0:T(8,128)(2,1)S(1)} copy-done((bf16[2048,128]{1,0:T(8,128)(2,1)S(1)}, bf16[2048,128]{1,0:T(8,128)(2,1)}, u32[]{:S(2)}) %copy-start.1) | copy-done | bytes 524312
  1.7 0.0 copy-start.6
  1.7 0.7 copy-done.6
  2.4 0.0 copy-start.9
  2.4 0.7 copy-done.9
  3.1 0.0 copy-start.10
  3.1 0.8 shard_map.147.table_ref
  3.9 3.3 %collective-permute-start = (bf16[256,128]{1,0:T(8,128)(2,1)S(1)}, bf16[256,128]{1,0:T(8,128)(2,1)S(1)}, u32[]{:S(2)}, u32[]{:S(2)}) collective-permute-start(bf16[256,128]{1,0:T(8,128)(2,1)S(1)} %shard_map.147.table_ref), channel_id=1, source_target_pairs={{0,1},{1,0},{2,3},{3,2},{4,5},{5,4},{6,7},{7,6},{8,9},{9,8},{10,11... | collective-permute-start | bytes 196616 | tf_op jit(solution)/shard_map/ppermute | solution.py:293
  7.2 0.0 copy-done.10
  7.2 1.2 %shard_map.146 = s32[64,128]{1,0:T(8,128)} custom-call(s32[1,1024]{1,0:T(1,128)S(1)} %copy-done.10), custom_call_target="tpu_custom_call" | custom-call | flops 67108864 | bytes 36864 | tf_op jit(solution)/shard_map/pallas_call | solution.py:49
  8.3 0.0 copy-start.2
  8.3 9.6 %all-to-all-start = ((s32[32,2,128]{2,1,0:T(2,128)}), s32[32,2,128]{2,1,0:T(2,128)S(1)}, u32[]{:S(2)}, u32[]{:S(2)}) async-start(s32[32,2,128]{2,1,0:T(2,128)} %bitcast.2), calls=%async_computation | async-start | bytes 65536 | tf_op jit(solution)/shard_map/all_to_all | solution.py:297
  18.0 0.0 copy-start.4
  18.0 0.0 copy-start.8
  18.0 0.0 copy-done
  18.0 0.0 copy-done.2
  18.0 0.6 copy-done.4
  18.7 0.0 copy-done.8
  18.7 0.3 shard_map.148
  19.0 7.8 %all-to-all-done = s32[32,2,128]{2,1,0:T(2,128)S(1)} async-done(((s32[32,2,128]{2,1,0:T(2,128)}), s32[32,2,128]{2,1,0:T(2,128)S(1)}, u32[]{:S(2)}, u32[]{:S(2)}) %all-to-all-start) | async-done | bytes 32800 | tf_op jit(solution)/shard_map/all_to_all | solution.py:297
  26.7 0.0 collective-permute-done.other_ref
  26.7 1.2 %shard_map.149 = bf16[512,128]{1,0:T(8,128)(2,1)} custom-call(s32[1]{0:T(128)} %bitcast.1.core_ref, s32[64,128]{1,0:T(8,128)S(1)} %bitcast.16, bf16[256,128]{1,0:T(8,128)(2,1)S(1)} %shard_map.147.table_ref, bf16[256,128]{1,0:T(8,128)(2,1)S(1)} %collective-permute-done.other_ref), custom_call_target="tpu_custom_call" | custom-call | flops 67108864 | bytes 294916 | tf_op jit(solution)/shard_map/pallas_call | solution.py:49
  28.0 0.0 copy-start.11
  28.0 4.0 %all-to-all-start.1 = ((bf16[32,16,128]{2,1,0:T(8,128)(2,1)}), bf16[32,16,128]{2,1,0:T(8,128)(2,1)S(1)}, u32[]{:S(2)}, u32[]{:S(2)}) async-start(bf16[32,16,128]{2,1,0:T(8,128)(2,1)} %bitcast.7), calls=%async_computation.1 | async-start | bytes 262144 | tf_op jit(solution)/shard_map/all_to_all | solution.py:297
  32.0 0.0 copy-done.11
  32.0 1.9 %shard_map.150 = (bf16[256,512]{1,0:T(8,128)(2,1)S(1)}, bf16[512,256]{1,0:T(8,128)(2,1)S(1)}) custom-call(s32[1,1024]{1,0:T(1,128)S(1)} %copy-done.10, s32[1,256]{1,0:T(1,128)S(1)} %copy-done.11), custom_call_target="tpu_custom_call" | custom-call | flops 536870912 | bytes 529408 | tf_op jit(solution)/shard_map/pallas_call | solution.py:49
  33.9 7.2 %all-to-all-done.1 = bf16[32,16,128]{2,1,0:T(8,128)(2,1)S(1)} async-done(((bf16[32,16,128]{2,1,0:T(8,128)(2,1)}), bf16[32,16,128]{2,1,0:T(8,128)(2,1)S(1)}, u32[]{:S(2)}, u32[]{:S(2)}) %all-to-all-start.1) | async-done | bytes 131104 | tf_op jit(solution)/shard_map/all_to_all | solution.py:297
  41.1 1.0 shard_map.151
  42.1 2.8 %collective-permute-start.1 = (bf16[64,16,128]{2,1,0:T(8,128)(2,1)S(1)}, bf16[64,16,128]{2,1,0:T(8,128)(2,1)S(1)}, u32[]{:S(2)}, u32[]{:S(2)}) collective-permute-start(bf16[64,16,128]{2,1,0:T(8,128)(2,1)S(1)} %get-tuple-element.40), channel_id=1, source_target_pairs={{0,1},{1,0},{2,3},{3,2},{4,5},{5,4},{6,7},{7,6},{8,9},{9,8},{10,11... | collective-permute-start | bytes 786440 | tf_op jit(solution)/shard_map/ppermute | solution.py:293
  44.9 0.9 shard_map.152
  45.8 0.3 collective-permute-done.1.given_ref
  46.0 1.3 %shard_map.153 = bf16[64,24,128]{2,1,0:T(8,128)(2,1)} custom-call(f32[64,16,128]{2,1,0:T(8,128)S(1)} %get-tuple-element.39.keep_ref, bf16[64,16,128]{2,1,0:T(8,128)(2,1)S(1)} %collective-permute-done.1.given_ref, bf16[64,8,128]{2,1,0:T(8,128)(2,1)S(1)} %bitcast.20), custom_call_target="tpu_custom_call" | custom-call | flops 1048576 | bytes 1310720 | tf_op jit(solution)/shard_map/pallas_call | solution.py:49
  47.4 4.4 %all-to-all-start.2 = ((bf16[64,24,128]{2,1,0:T(8,128)(2,1)}), bf16[64,24,128]{2,1,0:T(8,128)(2,1)S(1)}, u32[]{:S(2)}, u32[]{:S(2)}) async-start(bf16[64,24,128]{2,1,0:T(8,128)(2,1)} %shard_map.153), calls=%async_computation.2 | async-start | bytes 786432 | tf_op jit(solution)/shard_map/all_to_all | solution.py:297
  51.8 0.7 collective-permute-start.2
  52.5 0.9 collective-permute-done.2.other_ref
  53.3 0.4 shard_map.154.place_ref
  53.7 0.0 copy-start.7
  53.7 12.8 %all-to-all-done.2 = bf16[64,24,128]{2,1,0:T(8,128)(2,1)S(1)} async-done(((bf16[64,24,128]{2,1,0:T(8,128)(2,1)}), bf16[64,24,128]{2,1,0:T(8,128)(2,1)S(1)}, u32[]{:S(2)}, u32[]{:S(2)}) %all-to-all-start.2) | async-done | bytes 393248 | tf_op jit(solution)/shard_map/all_to_all | solution.py:297
  66.5 0.0 copy-done.7
  66.5 0.8 shard_map.155.x0_ref
  67.3 2.6 %collective-permute-start.5 = (bf16[304,128]{1,0:T(8,128)(2,1)S(1)}, bf16[304,128]{1,0:T(8,128)(2,1)S(1)}, u32[]{:S(2)}, u32[]{:S(2)}) collective-permute-start(bf16[304,128]{1,0:T(8,128)(2,1)S(1)} %shard_map.155.x0_ref), channel_id=1, source_target_pairs={{0,192},{64,128},{128,64},{192,0},{1,193},{65,129},{129,65},{193,1... | collective-permute-start | bytes 233480 | tf_op jit(solution)/shard_map/ppermute | solution.py:288
  69.8 0.5 collective-permute-start.4
  70.3 0.3 collective-permute-start.3
  70.6 1.5 %collective-permute-done.5.x3_ref = bf16[304,128]{1,0:T(8,128)(2,1)S(1)} collective-permute-done((bf16[304,128]{1,0:T(8,128)(2,1)S(1)}, bf16[304,128]{1,0:T(8,128)(2,1)S(1)}, u32[]{:S(2)}, u32[]{:S(2)}) %collective-permute-start.5) | collective-permute-done | bytes 77856 | tf_op jit(solution)/shard_map/ppermute | solution.py:288
  72.1 2.5 %collective-permute-done.4.x2_ref = bf16[304,128]{1,0:T(8,128)(2,1)S(1)} collective-permute-done((bf16[304,128]{1,0:T(8,128)(2,1)S(1)}, bf16[304,128]{1,0:T(8,128)(2,1)S(1)}, u32[]{:S(2)}, u32[]{:S(2)}) %collective-permute-start.4) | collective-permute-done | bytes 77856 | tf_op jit(solution)/shard_map/ppermute | solution.py:288
  74.6 0.1 collective-permute-done.3.x1_ref
  74.7 0.0 copy-start.3
  74.8 0.0 copy-start.5
  74.8 14.8 %all_to_all.20.mine_ref = bf16[32,32,128]{2,1,0:T(8,128)(2,1)S(1)} all-to-all(bf16[32,32,128]{2,1,0:T(8,128)(2,1)S(1)} %shard_map.158), channel_id=1, replica_groups=mesh['grp'=4,'row_0'=4,'row_1'=8,'row_2'=2] {'row_0','row_1'}, dimensions={0} | all-to-all | bytes 524288 | tf_op jit(solution)/shard_map/all_to_all | solution.py:297
  89.6 4.5 %collective-permute-start.9 = (bf16[32,32,128]{2,1,0:T(8,128)(2,1)S(1)}, bf16[32,32,128]{2,1,0:T(8,128)(2,1)S(1)}, u32[]{:S(2)}, u32[]{:S(2)}) collective-permute-start(bf16[32,32,128]{2,1,0:T(8,128)(2,1)S(1)} %all_to_all.20.mine_ref), channel_id=1, source_target_pairs={{0,1},{1,0},{2,3},{3,2},{4,5},{5,4},{6,7},{7,6},{8,9},{9,8},{10,11... | collective-permute-start | bytes 786440 | tf_op jit(solution)/shard_map/ppermute | solution.py:293
  94.1 0.0 copy-done.3
  94.1 0.0 copy-done.5
  94.1 1.2 %shard_map.156 = (f32[512,128]{1,0:T(8,128)}, f32[1,512]{1,0:T(1,128)}, bf16[528,128]{1,0:T(8,128)(2,1)S(1)}) custom-call(s32[1]{0:T(128)} %bitcast.me_ref, bf16[304,128]{1,0:T(8,128)(2,1)S(1)} %shard_map.155.x0_ref, bf16[304,128]{1,0:T(8,128)(2,1)S(1)} %collective-permute-done.3.x1_ref, bf16[304,128]{1,0:T(8,128)(2,1)S(1)} %collective-permute-done.4.x2_ref, ...), custom_call_target="tpu_custom_call" | custom-call | flops 4194304 | bytes 974852 | tf_op jit(solution)/shard_map/pallas_call | solution.py:49
  95.2 0.9 collective-permute-start.8
  96.2 0.5 collective-permute-start.7
  96.7 1.8 %collective-permute-start.6 = (bf16[528,128]{1,0:T(8,128)(2,1)S(1)}, bf16[528,128]{1,0:T(8,128)(2,1)S(1)}, u32[]{:S(2)}, u32[]{:S(2)}) collective-permute-start(bf16[528,128]{1,0:T(8,128)(2,1)S(1)} %get-tuple-element.44.s0_ref), channel_id=1, source_target_pairs={{0,64},{64,0},{128,192},{192,128},{1,65},{65,1},{129,193},{193,129... | collective-permute-start | bytes 405512 | tf_op jit(solution)/shard_map/ppermute | solution.py:288
  98.5 6.0 %collective-permute-done.8.s3_ref = bf16[528,128]{1,0:T(8,128)(2,1)S(1)} collective-permute-done((bf16[528,128]{1,0:T(8,128)(2,1)S(1)}, bf16[528,128]{1,0:T(8,128)(2,1)S(1)}, u32[]{:S(2)}, u32[]{:S(2)}) %collective-permute-start.8) | collective-permute-done | bytes 135200 | tf_op jit(solution)/shard_map/ppermute | solution.py:288
  104.5 0.0 collective-permute-done.7.s2_ref
  104.5 0.3 collective-permute-done.6.s1_ref
  104.8 0.8 shard_map.157
  105.7 0.0 collective-permute-done.9.other_ref
  105.7 1.5 %shard_map.159 = f32[256,1024]{1,0:T(8,128)} custom-call(s32[1]{0:T(128)} %bitcast.1.core_ref, bf16[32,32,128]{2,1,0:T(8,128)(2,1)S(1)} %all_to_all.20.mine_ref, bf16[32,32,128]{2,1,0:T(8,128)(2,1)S(1)} %collective-permute-done.9.other_ref), custom_call_target="tpu_custom_call" | custom-call | flops 1048576 | bytes 1572868 | tf_op jit(solution)/shard_map/pallas_call | solution.py:49
  (1 shorter events, 0.0 us)
Async XLA Ops:
  0.6 17.4 %copy-start = (bf16[256,1024]{1,0:T(8,128)(2,1)S(1)}, bf16[256,1024]{1,0:T(8,128)(2,1)}, u32[]{:S(2)}) copy-start(bf16[256,1024]{1,0:T(8,128)(2,1)} %w_ref.5) | copy-start | bytes 1572868
  0.6 1.1 %copy-start.1 = (bf16[2048,128]{1,0:T(8,128)(2,1)S(1)}, bf16[2048,128]{1,0:T(8,128)(2,1)}, u32[]{:S(2)}) copy-start(bf16[2048,128]{1,0:T(8,128)(2,1)} %serving_ref.1) | copy-start | bytes 1572868
  1.7 0.7 copy-start.6
  2.4 0.7 copy-start.9
  3.1 4.1 %copy-start.10 = (s32[1,1024]{1,0:T(1,128)S(1)}, s32[1,1024]{1,0:T(1,128)}, u32[]{:S(2)}) copy-start(s32[1,1024]{1,0:T(1,128)} %idx_ref.3) | copy-start | bytes 12292
  3.9 22.9 %collective-permute-start = (bf16[256,128]{1,0:T(8,128)(2,1)S(1)}, bf16[256,128]{1,0:T(8,128)(2,1)S(1)}, u32[]{:S(2)}, u32[]{:S(2)}) collective-permute-start(bf16[256,128]{1,0:T(8,128)(2,1)S(1)} %shard_map.147.table_ref), channel_id=1, source_target_pairs={{0,1},{1,0},{2,3},{3,2},{4,5},{5,4},{6,7},{7,6},{8,9},{9,8},{10,11... | collective-permute-start | bytes 196616 | tf_op jit(solution)/shard_map/ppermute | solution.py:293
  8.3 9.7 %copy-start.2 = (bf16[256,128]{1,0:T(8,128)(2,1)S(1)}, bf16[256,128]{1,0:T(8,128)(2,1)}, u32[]{:S(2)}) copy-start(bf16[256,128]{1,0:T(8,128)(2,1)} %dense_ref.3) | copy-start | bytes 196612
  8.3 18.4 %all-to-all-start = ((s32[32,2,128]{2,1,0:T(2,128)}), s32[32,2,128]{2,1,0:T(2,128)S(1)}, u32[]{:S(2)}, u32[]{:S(2)}) async-start(s32[32,2,128]{2,1,0:T(2,128)} %bitcast.2), calls=%async_computation | async-start | bytes 65536 | tf_op jit(solution)/shard_map/all_to_all | solution.py:297
  18.0 0.7 copy-start.4
  18.0 0.7 copy-start.8
  28.0 4.0 %copy-start.11 = (s32[1,256]{1,0:T(1,128)S(1)}, s32[1,256]{1,0:T(1,128)}, u32[]{:S(2)}) copy-start(s32[1,256]{1,0:T(1,128)} %len_ref.1) | copy-start | bytes 3076
  28.0 13.1 %all-to-all-start.1 = ((bf16[32,16,128]{2,1,0:T(8,128)(2,1)}), bf16[32,16,128]{2,1,0:T(8,128)(2,1)S(1)}, u32[]{:S(2)}, u32[]{:S(2)}) async-start(bf16[32,16,128]{2,1,0:T(8,128)(2,1)} %bitcast.7), calls=%async_computation.1 | async-start | bytes 262144 | tf_op jit(solution)/shard_map/all_to_all | solution.py:297
  42.1 3.9 %collective-permute-start.1 = (bf16[64,16,128]{2,1,0:T(8,128)(2,1)S(1)}, bf16[64,16,128]{2,1,0:T(8,128)(2,1)S(1)}, u32[]{:S(2)}, u32[]{:S(2)}) collective-permute-start(bf16[64,16,128]{2,1,0:T(8,128)(2,1)S(1)} %get-tuple-element.40), channel_id=1, source_target_pairs={{0,1},{1,0},{2,3},{3,2},{4,5},{5,4},{6,7},{7,6},{8,9},{9,8},{10,11... | collective-permute-start | bytes 786440 | tf_op jit(solution)/shard_map/ppermute | solution.py:293
  47.4 19.1 %all-to-all-start.2 = ((bf16[64,24,128]{2,1,0:T(8,128)(2,1)}), bf16[64,24,128]{2,1,0:T(8,128)(2,1)S(1)}, u32[]{:S(2)}, u32[]{:S(2)}) async-start(bf16[64,24,128]{2,1,0:T(8,128)(2,1)} %shard_map.153), calls=%async_computation.2 | async-start | bytes 786432 | tf_op jit(solution)/shard_map/all_to_all | solution.py:297
  51.8 1.5 %collective-permute-start.2 = (s32[64,128]{1,0:T(8,128)S(1)}, s32[64,128]{1,0:T(8,128)S(1)}, u32[]{:S(2)}, u32[]{:S(2)}) collective-permute-start(s32[64,128]{1,0:T(8,128)S(1)} %bitcast.17), channel_id=1, source_target_pairs={{0,1},{1,0},{2,3},{3,2},{4,5},{5,4},{6,7},{7,6},{8,9},{9,8},{10,11... | collective-permute-start | bytes 98312 | tf_op jit(solution)/shard_map/ppermute | solution.py:293
  53.7 12.8 %copy-start.7 = (s32[1,2]{1,0:T(1,128)S(1)}, s32[1,2]{1,0:T(1,128)}, u32[]{:S(2)}) copy-start(s32[1,2]{1,0:T(1,128)} %hot_ref.3) | copy-start | bytes 28
  67.3 4.8 %collective-permute-start.5 = (bf16[304,128]{1,0:T(8,128)(2,1)S(1)}, bf16[304,128]{1,0:T(8,128)(2,1)S(1)}, u32[]{:S(2)}, u32[]{:S(2)}) collective-permute-start(bf16[304,128]{1,0:T(8,128)(2,1)S(1)} %shard_map.155.x0_ref), channel_id=1, source_target_pairs={{0,192},{64,128},{128,64},{192,0},{1,193},{65,129},{129,65},{193,1... | collective-permute-start | bytes 233480 | tf_op jit(solution)/shard_map/ppermute | solution.py:288
  69.8 4.8 %collective-permute-start.4 = (bf16[304,128]{1,0:T(8,128)(2,1)S(1)}, bf16[304,128]{1,0:T(8,128)(2,1)S(1)}, u32[]{:S(2)}, u32[]{:S(2)}) collective-permute-start(bf16[304,128]{1,0:T(8,128)(2,1)S(1)} %shard_map.155.x0_ref), channel_id=1, source_target_pairs={{0,128},{64,192},{128,0},{192,64},{1,129},{65,193},{129,1},{193,65... | collective-permute-start | bytes 233480 | tf_op jit(solution)/shard_map/ppermute | solution.py:288
  70.3 4.4 %collective-permute-start.3 = (bf16[304,128]{1,0:T(8,128)(2,1)S(1)}, bf16[304,128]{1,0:T(8,128)(2,1)S(1)}, u32[]{:S(2)}, u32[]{:S(2)}) collective-permute-start(bf16[304,128]{1,0:T(8,128)(2,1)S(1)} %shard_map.155.x0_ref), channel_id=1, source_target_pairs={{0,64},{64,0},{128,192},{192,128},{1,65},{65,1},{129,193},{193,129... | collective-permute-start | bytes 233480 | tf_op jit(solution)/shard_map/ppermute | solution.py:288
  74.7 19.3 %copy-start.3 = (f32[1,512,128]{2,1,0:T(8,128)S(1)}, f32[1,512,128]{2,1,0:T(8,128)}, u32[]{:S(2)}) copy-start(f32[1,512,128]{2,1,0:T(8,128)} %param.20) | copy-start | bytes 786436
  74.8 19.3 %copy-start.5 = (f32[1,512]{1,0:T(1,128)S(1)}, f32[1,512]{1,0:T(1,128)}, u32[]{:S(2)}) copy-start(f32[1,512]{1,0:T(1,128)} %accum_ref.1) | copy-start | bytes 6148
  89.6 16.1 %collective-permute-start.9 = (bf16[32,32,128]{2,1,0:T(8,128)(2,1)S(1)}, bf16[32,32,128]{2,1,0:T(8,128)(2,1)S(1)}, u32[]{:S(2)}, u32[]{:S(2)}) collective-permute-start(bf16[32,32,128]{2,1,0:T(8,128)(2,1)S(1)} %all_to_all.20.mine_ref), channel_id=1, source_target_pairs={{0,1},{1,0},{2,3},{3,2},{4,5},{5,4},{6,7},{7,6},{8,9},{9,8},{10,11... | collective-permute-start | bytes 786440 | tf_op jit(solution)/shard_map/ppermute | solution.py:293
  95.2 9.2 %collective-permute-start.8 = (bf16[528,128]{1,0:T(8,128)(2,1)S(1)}, bf16[528,128]{1,0:T(8,128)(2,1)S(1)}, u32[]{:S(2)}, u32[]{:S(2)}) collective-permute-start(bf16[528,128]{1,0:T(8,128)(2,1)S(1)} %get-tuple-element.44.s0_ref), channel_id=1, source_target_pairs={{0,192},{64,128},{128,64},{192,0},{1,193},{65,129},{129,65},{193,1... | collective-permute-start | bytes 405512 | tf_op jit(solution)/shard_map/ppermute | solution.py:288
  96.2 8.3 %collective-permute-start.7 = (bf16[528,128]{1,0:T(8,128)(2,1)S(1)}, bf16[528,128]{1,0:T(8,128)(2,1)S(1)}, u32[]{:S(2)}, u32[]{:S(2)}) collective-permute-start(bf16[528,128]{1,0:T(8,128)(2,1)S(1)} %get-tuple-element.44.s0_ref), channel_id=1, source_target_pairs={{0,128},{64,192},{128,0},{192,64},{1,129},{65,193},{129,1},{193,65... | collective-permute-start | bytes 405512 | tf_op jit(solution)/shard_map/ppermute | solution.py:288
  96.7 8.1 %collective-permute-start.6 = (bf16[528,128]{1,0:T(8,128)(2,1)S(1)}, bf16[528,128]{1,0:T(8,128)(2,1)S(1)}, u32[]{:S(2)}, u32[]{:S(2)}) collective-permute-start(bf16[528,128]{1,0:T(8,128)(2,1)S(1)} %get-tuple-element.44.s0_ref), channel_id=1, source_target_pairs={{0,64},{64,0},{128,192},{192,128},{1,65},{65,1},{129,193},{193,129... | collective-permute-start | bytes 405512 | tf_op jit(solution)/shard_map/ppermute | solution.py:288

commit v7 on v5

--- a/solution.py
+++ b/solution.py
@@ -28,6 +28,7 @@
 I32 = jnp.int32
 VM = pl.BlockSpec(memory_space=pltpu.VMEM)
 SM = pl.BlockSpec(memory_space=pltpu.SMEM)
+ANY = pl.BlockSpec(memory_space=pl.ANY)
 
 
 def iota(shape, dim):
@@ -42,7 +43,7 @@
     return jnp.where(mask, 1.0, 0.0).astype(BF16)
 
 
-def call(kernel, outs, specs, args, flops, scratch=()):
+def call(kernel, outs, specs, args, flops, scratch=(), out_specs=None):
     bytes_accessed = sum(a.size * a.dtype.itemsize for a in args) + sum(
         o.size * o.dtype.itemsize for o in outs
     )
@@ -50,7 +51,7 @@
         kernel,
         out_shape=outs,
         in_specs=specs,
-        out_specs=[VM] * len(outs),
+        out_specs=out_specs or [VM] * len(outs),
         cost_estimate=pl.CostEstimate(
             flops=flops, bytes_accessed=bytes_accessed, transcendentals=0
         ),
@@ -190,9 +191,30 @@
     by_tile(kept_ref, dot(keep_ref[...], dpre, 0, 0))
 
 
-def parts_kernel(keep_ref, given_ref, row_grad_ref, out_ref):
-    out_ref[:, 0:16, :] = (keep_ref[...] + given_ref[...].astype(F32)).astype(BF16)
-    out_ref[:, 16:24, :] = row_grad_ref[...]
+def store_quarters(fill, out_ref, buf, sem):
+    size = out_ref.shape[0] // 4
+    copies = []
+    for i in range(4):
+        fill(i)
+        copies.append(
+            pltpu.make_async_copy(buf.at[i], out_ref.at[pl.ds(i * size, size)], sem.at[i])
+        )
+        copies[i].start()
+    for copy in copies:
+        copy.wait()
+
+
+def quarters_of(shape, dtype):
+    return [pltpu.VMEM((4, shape[0] // 4, *shape[1:]), dtype), pltpu.SemaphoreType.DMA((4,))]
+
+
+def parts_kernel(keep_ref, given_ref, row_grad_ref, out_ref, buf, sem):
+    def fill(i):
+        at = slice(i * 16, (i + 1) * 16)
+        buf[i, :, 0:16, :] = (keep_ref[at] + given_ref[at].astype(F32)).astype(BF16)
+        buf[i, :, 16:24, :] = row_grad_ref[at]
+
+    store_quarters(fill, out_ref, buf, sem)
 
 
 def owned_kernel(got_ref, place_ref, hot_ref, out_ref):
@@ -264,15 +286,18 @@
     scale_ref[...] = scales[0:1, 0:16].astype(BF16)
 
 
-def last_kernel(core_ref, mine_ref, other_ref, top_ref):
-    for ref, core in ((mine_ref, core_ref[0]), (other_ref, 1 - core_ref[0])):
-        for s in range(N_ROW // 2):
-            column = pl.multiple_of((s % 4 * 2 + core) * 128, 128)
-            for half in range(2):
-                line = half * 128 + s // 4 * 16
-                top_ref[line : line + 16, pl.ds(column, 128)] = ref[
-                    s, half * 16 : (half + 1) * 16, :
+def last_kernel(core_ref, mine_ref, other_ref, top_ref, buf, sem):
+    def fill(i):
+        half = slice(i // 2 * 16, i // 2 * 16 + 16)
+        for ref, core in ((mine_ref, core_ref[0]), (other_ref, 1 - core_ref[0])):
+            for s in range(16):
+                column = pl.multiple_of((s % 4 * 2 + core) * 128, 128)
+                line = s // 4 * 16
+                buf[i, line : line + 16, pl.ds(column, 128)] = ref[
+                    i % 2 * 16 + s, half, :
                 ].astype(F32)
+
+    store_quarters(fill, top_ref, buf, sem)
 
 
 def like(shape, dtype):
@@ -364,6 +389,8 @@
         [VM] * 3,
         (kept, given, row_grad.reshape(N_ROW, CAP, D)),
         1 << 20,
+        quarters_of((N_ROW, 24, D), BF16),
+        [ANY],
     )
     got = exchange(parts)
     (own,) = call(
@@ -401,7 +428,13 @@
     )
     top_other = other_core(top_mine)
     (top_grad,) = call(
-        last_kernel, [like((2 * D, FF), F32)], [SM] + [VM] * 2, (core, top_mine, top_other), 1 << 20
+        last_kernel,
+        [like((2 * D, FF), F32)],
+        [SM] + [VM] * 2,
+        (core, top_mine, top_other),
+        1 << 20,
+        quarters_of((2 * D, FF), F32),
+        [ANY],
     )
     return new_master[None], new_accum, fresh, fresh_scale.reshape(16), top_grad
 

time: 106 us -> 106 us (level)
  no operation moved by 1% of the time
where the time goes in v7:
time: 106 us; the launch traced here: 104 us
  waiting for transfers between devices  41.3 us (39%)
  starting transfers between devices  31.2 us (29%)
  blocking collectives  15.8 us (15%)
  Pallas kernels  12.2 us (12%)
  local copies, waits for them, and re-layouts  3.1 us (3%)
    all_to_all x3, waiting for transfers between devices, exchange(): return lax.all_to_all(x, axes, 0, 0, tiled=True)  27.5 us
    all_to_all x3, starting transfers between devices, exchange(): return lax.all_to_all(x, axes, 0, 0, tiled=True)  22.5 us
    all_to_all x1, blocking collectives, exchange(): return lax.all_to_all(x, axes, 0, 0, tiled=True)  15.8 us
    pallas_call x14, Pallas kernels, call(): pl.pallas_call(kernel, out_shape=outs, in_specs=specs, out_specs=out_spec...  12.2 us
    ppermute x6, waiting for transfers between devices, over_groups(): parts.append(lax.ppermute(x, 'grp', [(g, g ^ o) for g in range(N_GRP)]))  12 us
    ppermute x6, starting transfers between devices, over_groups(): parts.append(lax.ppermute(x, 'grp', [(g, g ^ o) for g in range(N_GRP)]))  8.27 us
    unnamed x24, local copies, waits for them, and re-layouts  3.1 us
  transfers between devices with their start and end apart: 13, of which 9 were waited for; matrix products, arithmetic and copies ran while one was open for 0% of the time, Pallas kernels for 6%

profile of v7, /device:TPU:8, one launch (start us, length us, event | category | flops | bytes accessed | tf_op | source)
XLA Modules:
  0.0 104.4 jit_solution(4410570910183539789)
XLA Ops:
  0.6 0.0 copy-start
  0.6 0.0 copy-start.1
  0.7 1.1 %copy-done.1 = bf16[2048,128]{1,0:T(8,128)(2,1)S(1)} copy-done((bf16[2048,128]{1,0:T(8,128)(2,1)S(1)}, bf16[2048,128]{1,0:T(8,128)(2,1)}, u32[]{:S(2)}) %copy-start.1) | copy-done | bytes 524312
  1.7 0.0 copy-start.6
  1.7 0.7 copy-done.6
  2.4 0.0 copy-start.9
  2.4 0.7 copy-done.9
  3.1 0.0 copy-start.10
  3.1 0.8 shard_map.147.table_ref
  3.9 0.1 collective-permute-start
  4.0 0.0 copy-done.10
  4.0 1.2 %shard_map.146 = s32[64,128]{1,0:T(8,128)} custom-call(s32[1,1024]{1,0:T(1,128)S(1)} %copy-done.10), custom_call_target="tpu_custom_call" | custom-call | flops 67108864 | bytes 36864 | tf_op jit(solution)/shard_map/pallas_call | solution.py:50
  5.1 0.0 copy-start.2
  5.2 11.8 %all-to-all-start = ((s32[32,2,128]{2,1,0:T(2,128)}), s32[32,2,128]{2,1,0:T(2,128)S(1)}, u32[]{:S(2)}, u32[]{:S(2)}) async-start(s32[32,2,128]{2,1,0:T(2,128)} %bitcast.2), calls=%async_computation | async-start | bytes 65536 | tf_op jit(solution)/shard_map/all_to_all | solution.py:319
  17.0 0.0 copy-start.4
  17.0 0.0 copy-start.8
  17.0 0.0 copy-done
  17.0 0.0 copy-done.2
  17.0 0.6 copy-done.4
  17.7 0.0 copy-done.8
  17.7 0.3 shard_map.148
  18.0 7.7 %all-to-all-done = s32[32,2,128]{2,1,0:T(2,128)S(1)} async-done(((s32[32,2,128]{2,1,0:T(2,128)}), s32[32,2,128]{2,1,0:T(2,128)S(1)}, u32[]{:S(2)}, u32[]{:S(2)}) %all-to-all-start) | async-done | bytes 32800 | tf_op jit(solution)/shard_map/all_to_all | solution.py:319
  25.7 0.0 collective-permute-done.other_ref
  25.7 1.2 %shard_map.149 = bf16[512,128]{1,0:T(8,128)(2,1)} custom-call(s32[1]{0:T(128)} %bitcast.1.core_ref, s32[64,128]{1,0:T(8,128)S(1)} %bitcast.16, bf16[256,128]{1,0:T(8,128)(2,1)S(1)} %shard_map.147.table_ref, bf16[256,128]{1,0:T(8,128)(2,1)S(1)} %collective-permute-done.other_ref), custom_call_target="tpu_custom_call" | custom-call | flops 67108864 | bytes 294916 | tf_op jit(solution)/shard_map/pallas_call | solution.py:50
  26.9 0.0 copy-start.11
  26.9 5.1 %all-to-all-start.1 = ((bf16[32,16,128]{2,1,0:T(8,128)(2,1)}), bf16[32,16,128]{2,1,0:T(8,128)(2,1)S(1)}, u32[]{:S(2)}, u32[]{:S(2)}) async-start(bf16[32,16,128]{2,1,0:T(8,128)(2,1)} %bitcast.7), calls=%async_computation.1 | async-start | bytes 262144 | tf_op jit(solution)/shard_map/all_to_all | solution.py:319
  32.0 0.0 copy-done.11
  32.0 1.9 %shard_map.150 = (bf16[256,512]{1,0:T(8,128)(2,1)S(1)}, bf16[512,256]{1,0:T(8,128)(2,1)S(1)}) custom-call(s32[1,1024]{1,0:T(1,128)S(1)} %copy-done.10, s32[1,256]{1,0:T(1,128)S(1)} %copy-done.11), custom_call_target="tpu_custom_call" | custom-call | flops 536870912 | bytes 529408 | tf_op jit(solution)/shard_map/pallas_call | solution.py:50
  33.9 7.4 %all-to-all-done.1 = bf16[32,16,128]{2,1,0:T(8,128)(2,1)S(1)} async-done(((bf16[32,16,128]{2,1,0:T(8,128)(2,1)}), bf16[32,16,128]{2,1,0:T(8,128)(2,1)S(1)}, u32[]{:S(2)}, u32[]{:S(2)}) %all-to-all-start.1) | async-done | bytes 131104 | tf_op jit(solution)/shard_map/all_to_all | solution.py:319
  41.3 1.0 shard_map.151
  42.3 0.1 collective-permute-start.1
  42.4 0.9 shard_map.152
  43.3 0.6 collective-permute-done.1.given_ref
  43.9 0.8 shard_map.153
  44.7 5.6 %all-to-all-start.2 = ((bf16[64,24,128]{2,1,0:T(8,128)(2,1)}), bf16[64,24,128]{2,1,0:T(8,128)(2,1)S(1)}, u32[]{:S(2)}, u32[]{:S(2)}) async-start(bf16[64,24,128]{2,1,0:T(8,128)(2,1)} %shard_map.153), calls=%async_computation.2 | async-start | bytes 786432 | tf_op jit(solution)/shard_map/all_to_all | solution.py:319
  50.3 0.2 collective-permute-start.2
  50.5 1.1 %collective-permute-done.2.other_ref = s32[64,128]{1,0:T(8,128)S(1)} collective-permute-done((s32[64,128]{1,0:T(8,128)S(1)}, s32[64,128]{1,0:T(8,128)S(1)}, u32[]{:S(2)}, u32[]{:S(2)}) %collective-permute-start.2) | collective-permute-done | bytes 32800 | tf_op jit(solution)/shard_map/ppermute | solution.py:315
  51.6 0.4 shard_map.154.place_ref
  52.0 0.0 copy-start.7
  52.0 12.4 %all-to-all-done.2 = bf16[64,24,128]{2,1,0:T(8,128)(2,1)S(1)} async-done(((bf16[64,24,128]{2,1,0:T(8,128)(2,1)}), bf16[64,24,128]{2,1,0:T(8,128)(2,1)S(1)}, u32[]{:S(2)}, u32[]{:S(2)}) %all-to-all-start.2) | async-done | bytes 393248 | tf_op jit(solution)/shard_map/all_to_all | solution.py:319
  64.4 0.0 copy-done.7
  64.4 0.7 shard_map.155.x0_ref
  65.2 2.8 %collective-permute-start.5 = (bf16[304,128]{1,0:T(8,128)(2,1)S(1)}, bf16[304,128]{1,0:T(8,128)(2,1)S(1)}, u32[]{:S(2)}, u32[]{:S(2)}) collective-permute-start(bf16[304,128]{1,0:T(8,128)(2,1)S(1)} %shard_map.155.x0_ref), channel_id=1, source_target_pairs={{0,192},{64,128},{128,64},{192,0},{1,193},{65,129},{129,65},{193,1... | collective-permute-start | bytes 233480 | tf_op jit(solution)/shard_map/ppermute | solution.py:310
  68.0 0.8 collective-permute-start.4
  68.8 0.5 collective-permute-start.3
  69.4 2.5 %collective-permute-done.5.x3_ref = bf16[304,128]{1,0:T(8,128)(2,1)S(1)} collective-permute-done((bf16[304,128]{1,0:T(8,128)(2,1)S(1)}, bf16[304,128]{1,0:T(8,128)(2,1)S(1)}, u32[]{:S(2)}, u32[]{:S(2)}) %collective-permute-start.5) | collective-permute-done | bytes 77856 | tf_op jit(solution)/shard_map/ppermute | solution.py:310
  71.9 2.8 %collective-permute-done.4.x2_ref = bf16[304,128]{1,0:T(8,128)(2,1)S(1)} collective-permute-done((bf16[304,128]{1,0:T(8,128)(2,1)S(1)}, bf16[304,128]{1,0:T(8,128)(2,1)S(1)}, u32[]{:S(2)}, u32[]{:S(2)}) %collective-permute-start.4) | collective-permute-done | bytes 77856 | tf_op jit(solution)/shard_map/ppermute | solution.py:310
  74.7 0.0 collective-permute-done.3.x1_ref
  74.8 0.0 copy-start.3
  74.8 0.0 copy-start.5
  74.8 15.8 %all_to_all.20.mine_ref = bf16[32,32,128]{2,1,0:T(8,128)(2,1)S(1)} all-to-all(bf16[32,32,128]{2,1,0:T(8,128)(2,1)S(1)} %shard_map.158), channel_id=1, replica_groups=mesh['grp'=4,'row_0'=4,'row_1'=8,'row_2'=2] {'row_0','row_1'}, dimensions={0} | all-to-all | bytes 524288 | tf_op jit(solution)/shard_map/all_to_all | solution.py:319
  90.6 0.0 collective-permute-start.9
  90.6 0.0 copy-done.3
  90.6 0.0 copy-done.5
  90.6 1.2 %shard_map.156 = (f32[512,128]{1,0:T(8,128)}, f32[1,512]{1,0:T(1,128)}, bf16[528,128]{1,0:T(8,128)(2,1)S(1)}) custom-call(s32[1]{0:T(128)} %bitcast.me_ref, bf16[304,128]{1,0:T(8,128)(2,1)S(1)} %shard_map.155.x0_ref, bf16[304,128]{1,0:T(8,128)(2,1)S(1)} %collective-permute-done.3.x1_ref, bf16[304,128]{1,0:T(8,128)(2,1)S(1)} %collective-permute-done.4.x2_ref, ...), custom_call_target="tpu_custom_call" | custom-call | flops 4194304 | bytes 974852 | tf_op jit(solution)/shard_map/pallas_call | solution.py:50
  91.8 1.6 %collective-permute-start.8 = (bf16[528,128]{1,0:T(8,128)(2,1)S(1)}, bf16[528,128]{1,0:T(8,128)(2,1)S(1)}, u32[]{:S(2)}, u32[]{:S(2)}) collective-permute-start(bf16[528,128]{1,0:T(8,128)(2,1)S(1)} %get-tuple-element.44.s0_ref), channel_id=1, source_target_pairs={{0,192},{64,128},{128,64},{192,0},{1,193},{65,129},{129,65},{193,1... | collective-permute-start | bytes 405512 | tf_op jit(solution)/shard_map/ppermute | solution.py:310
  93.4 0.8 collective-permute-start.7
  94.2 1.6 %collective-permute-start.6 = (bf16[528,128]{1,0:T(8,128)(2,1)S(1)}, bf16[528,128]{1,0:T(8,128)(2,1)S(1)}, u32[]{:S(2)}, u32[]{:S(2)}) collective-permute-start(bf16[528,128]{1,0:T(8,128)(2,1)S(1)} %get-tuple-element.44.s0_ref), channel_id=1, source_target_pairs={{0,64},{64,0},{128,192},{192,128},{1,65},{65,1},{129,193},{193,129... | collective-permute-start | bytes 405512 | tf_op jit(solution)/shard_map/ppermute | solution.py:310
  95.9 6.0 %collective-permute-done.8.s3_ref = bf16[528,128]{1,0:T(8,128)(2,1)S(1)} collective-permute-done((bf16[528,128]{1,0:T(8,128)(2,1)S(1)}, bf16[528,128]{1,0:T(8,128)(2,1)S(1)}, u32[]{:S(2)}, u32[]{:S(2)}) %collective-permute-start.8) | collective-permute-done | bytes 135200 | tf_op jit(solution)/shard_map/ppermute | solution.py:310
  101.9 0.0 collective-permute-done.7.s2_ref
  101.9 0.6 collective-permute-done.6.s1_ref
  102.5 0.8 shard_map.157
  103.3 0.0 collective-permute-done.9.other_ref
  103.3 1.0 shard_map.159
  (1 shorter events, 0.0 us)
Async XLA Ops:
  0.6 16.4 %copy-start = (bf16[256,1024]{1,0:T(8,128)(2,1)S(1)}, bf16[256,1024]{1,0:T(8,128)(2,1)}, u32[]{:S(2)}) copy-start(bf16[256,1024]{1,0:T(8,128)(2,1)} %w_ref.5) | copy-start | bytes 1572868
  0.6 1.1 %copy-start.1 = (bf16[2048,128]{1,0:T(8,128)(2,1)S(1)}, bf16[2048,128]{1,0:T(8,128)(2,1)}, u32[]{:S(2)}) copy-start(bf16[2048,128]{1,0:T(8,128)(2,1)} %serving_ref.1) | copy-start | bytes 1572868
  1.7 0.7 copy-start.6
  2.4 0.7 copy-start.9
  3.1 0.9 copy-start.10
  3.9 21.8 %collective-permute-start = (bf16[256,128]{1,0:T(8,128)(2,1)S(1)}, bf16[256,128]{1,0:T(8,128)(2,1)S(1)}, u32[]{:S(2)}, u32[]{:S(2)}) collective-permute-start(bf16[256,128]{1,0:T(8,128)(2,1)S(1)} %shard_map.147.table_ref), channel_id=1, source_target_pairs={{0,1},{1,0},{2,3},{3,2},{4,5},{5,4},{6,7},{7,6},{8,9},{9,8},{10,11... | collective-permute-start | bytes 196616 | tf_op jit(solution)/shard_map/ppermute | solution.py:315
  5.1 11.9 %copy-start.2 = (bf16[256,128]{1,0:T(8,128)(2,1)S(1)}, bf16[256,128]{1,0:T(8,128)(2,1)}, u32[]{:S(2)}) copy-start(bf16[256,128]{1,0:T(8,128)(2,1)} %dense_ref.3) | copy-start | bytes 196612
  5.2 20.6 %all-to-all-start = ((s32[32,2,128]{2,1,0:T(2,128)}), s32[32,2,128]{2,1,0:T(2,128)S(1)}, u32[]{:S(2)}, u32[]{:S(2)}) async-start(s32[32,2,128]{2,1,0:T(2,128)} %bitcast.2), calls=%async_computation | async-start | bytes 65536 | tf_op jit(solution)/shard_map/all_to_all | solution.py:319
  17.0 0.7 copy-start.4
  17.0 0.7 copy-start.8
  26.9 5.1 %copy-start.11 = (s32[1,256]{1,0:T(1,128)S(1)}, s32[1,256]{1,0:T(1,128)}, u32[]{:S(2)}) copy-start(s32[1,256]{1,0:T(1,128)} %len_ref.1) | copy-start | bytes 3076
  26.9 14.4 %all-to-all-start.1 = ((bf16[32,16,128]{2,1,0:T(8,128)(2,1)}), bf16[32,16,128]{2,1,0:T(8,128)(2,1)S(1)}, u32[]{:S(2)}, u32[]{:S(2)}) async-start(bf16[32,16,128]{2,1,0:T(8,128)(2,1)} %bitcast.7), calls=%async_computation.1 | async-start | bytes 262144 | tf_op jit(solution)/shard_map/all_to_all | solution.py:319
  42.3 1.6 %collective-permute-start.1 = (bf16[64,16,128]{2,1,0:T(8,128)(2,1)S(1)}, bf16[64,16,128]{2,1,0:T(8,128)(2,1)S(1)}, u32[]{:S(2)}, u32[]{:S(2)}) collective-permute-start(bf16[64,16,128]{2,1,0:T(8,128)(2,1)S(1)} %get-tuple-element.40), channel_id=1, source_target_pairs={{0,1},{1,0},{2,3},{3,2},{4,5},{5,4},{6,7},{7,6},{8,9},{9,8},{10,11... | collective-permute-start | bytes 786440 | tf_op jit(solution)/shard_map/ppermute | solution.py:315
  44.7 19.7 %all-to-all-start.2 = ((bf16[64,24,128]{2,1,0:T(8,128)(2,1)}), bf16[64,24,128]{2,1,0:T(8,128)(2,1)S(1)}, u32[]{:S(2)}, u32[]{:S(2)}) async-start(bf16[64,24,128]{2,1,0:T(8,128)(2,1)} %shard_map.153), calls=%async_computation.2 | async-start | bytes 786432 | tf_op jit(solution)/shard_map/all_to_all | solution.py:319
  50.3 1.3 %collective-permute-start.2 = (s32[64,128]{1,0:T(8,128)S(1)}, s32[64,128]{1,0:T(8,128)S(1)}, u32[]{:S(2)}, u32[]{:S(2)}) collective-permute-start(s32[64,128]{1,0:T(8,128)S(1)} %bitcast.17), channel_id=1, source_target_pairs={{0,1},{1,0},{2,3},{3,2},{4,5},{5,4},{6,7},{7,6},{8,9},{9,8},{10,11... | collective-permute-start | bytes 98312 | tf_op jit(solution)/shard_map/ppermute | solution.py:315
  52.0 12.4 %copy-start.7 = (s32[1,2]{1,0:T(1,128)S(1)}, s32[1,2]{1,0:T(1,128)}, u32[]{:S(2)}) copy-start(s32[1,2]{1,0:T(1,128)} %hot_ref.3) | copy-start | bytes 28
  65.2 6.7 %collective-permute-start.5 = (bf16[304,128]{1,0:T(8,128)(2,1)S(1)}, bf16[304,128]{1,0:T(8,128)(2,1)S(1)}, u32[]{:S(2)}, u32[]{:S(2)}) collective-permute-start(bf16[304,128]{1,0:T(8,128)(2,1)S(1)} %shard_map.155.x0_ref), channel_id=1, source_target_pairs={{0,192},{64,128},{128,64},{192,0},{1,193},{65,129},{129,65},{193,1... | collective-permute-start | bytes 233480 | tf_op jit(solution)/shard_map/ppermute | solution.py:310
  68.0 6.7 %collective-permute-start.4 = (bf16[304,128]{1,0:T(8,128)(2,1)S(1)}, bf16[304,128]{1,0:T(8,128)(2,1)S(1)}, u32[]{:S(2)}, u32[]{:S(2)}) collective-permute-start(bf16[304,128]{1,0:T(8,128)(2,1)S(1)} %shard_map.155.x0_ref), channel_id=1, source_target_pairs={{0,128},{64,192},{128,0},{192,64},{1,129},{65,193},{129,1},{193,65... | collective-permute-start | bytes 233480 | tf_op jit(solution)/shard_map/ppermute | solution.py:310
  68.8 5.9 %collective-permute-start.3 = (bf16[304,128]{1,0:T(8,128)(2,1)S(1)}, bf16[304,128]{1,0:T(8,128)(2,1)S(1)}, u32[]{:S(2)}, u32[]{:S(2)}) collective-permute-start(bf16[304,128]{1,0:T(8,128)(2,1)S(1)} %shard_map.155.x0_ref), channel_id=1, source_target_pairs={{0,64},{64,0},{128,192},{192,128},{1,65},{65,1},{129,193},{193,129... | collective-permute-start | bytes 233480 | tf_op jit(solution)/shard_map/ppermute | solution.py:310
  74.8 15.8 %copy-start.3 = (f32[1,512,128]{2,1,0:T(8,128)S(1)}, f32[1,512,128]{2,1,0:T(8,128)}, u32[]{:S(2)}) copy-start(f32[1,512,128]{2,1,0:T(8,128)} %param.20) | copy-start | bytes 786436
  74.8 15.8 %copy-start.5 = (f32[1,512]{1,0:T(1,128)S(1)}, f32[1,512]{1,0:T(1,128)}, u32[]{:S(2)}) copy-start(f32[1,512]{1,0:T(1,128)} %accum_ref.1) | copy-start | bytes 6148
  90.6 12.7 %collective-permute-start.9 = (bf16[32,32,128]{2,1,0:T(8,128)(2,1)S(1)}, bf16[32,32,128]{2,1,0:T(8,128)(2,1)S(1)}, u32[]{:S(2)}, u32[]{:S(2)}) collective-permute-start(bf16[32,32,128]{2,1,0:T(8,128)(2,1)S(1)} %all_to_all.20.mine_ref), channel_id=1, source_target_pairs={{0,1},{1,0},{2,3},{3,2},{4,5},{5,4},{6,7},{7,6},{8,9},{9,8},{10,11... | collective-permute-start | bytes 786440 | tf_op jit(solution)/shard_map/ppermute | solution.py:315
  91.8 10.1 %collective-permute-start.8 = (bf16[528,128]{1,0:T(8,128)(2,1)S(1)}, bf16[528,128]{1,0:T(8,128)(2,1)S(1)}, u32[]{:S(2)}, u32[]{:S(2)}) collective-permute-start(bf16[528,128]{1,0:T(8,128)(2,1)S(1)} %get-tuple-element.44.s0_ref), channel_id=1, source_target_pairs={{0,192},{64,128},{128,64},{192,0},{1,193},{65,129},{129,65},{193,1... | collective-permute-start | bytes 405512 | tf_op jit(solution)/shard_map/ppermute | solution.py:310
  93.4 8.5 %collective-permute-start.7 = (bf16[528,128]{1,0:T(8,128)(2,1)S(1)}, bf16[528,128]{1,0:T(8,128)(2,1)S(1)}, u32[]{:S(2)}, u32[]{:S(2)}) collective-permute-start(bf16[528,128]{1,0:T(8,128)(2,1)S(1)} %get-tuple-element.44.s0_ref), channel_id=1, source_target_pairs={{0,128},{64,192},{128,0},{192,64},{1,129},{65,193},{129,1},{193,65... | collective-permute-start | bytes 405512 | tf_op jit(solution)/shard_map/ppermute | solution.py:310
  94.2 8.3 %collective-permute-start.6 = (bf16[528,128]{1,0:T(8,128)(2,1)S(1)}, bf16[528,128]{1,0:T(8,128)(2,1)S(1)}, u32[]{:S(2)}, u32[]{:S(2)}) collective-permute-start(bf16[528,128]{1,0:T(8,128)(2,1)S(1)} %get-tuple-element.44.s0_ref), channel_id=1, source_target_pairs={{0,64},{64,0},{128,192},{192,128},{1,65},{65,1},{129,193},{193,129... | collective-permute-start | bytes 405512 | tf_op jit(solution)/shard_map/ppermute | solution.py:310

commit v8 on v7

--- a/solution.py
+++ b/solution.py
@@ -31,6 +31,14 @@
 ANY = pl.BlockSpec(memory_space=pl.ANY)
 
 
+def group():
+    return lax.axis_index("grp").astype(I32)
+
+
+def own_core():
+    return lax.axis_index("row_2").astype(I32)
+
+
 def iota(shape, dim):
     return lax.broadcasted_iota(I32, shape, dim)
 
@@ -123,26 +131,29 @@
         table_ref[j * BLOCK : (j + 1) * BLOCK, :] = (buf[j].astype(F32) * own).astype(BF16)
 
 
-def pick_kernel(core_ref, ids_ref, table_ref, other_ref, rows_ref):
+def pick_kernel(ids_ref, table_ref, other_ref, rows_ref):
     owner = ones_where(lax.shift_right_logical(iota((SLOTS, N_ROW), 0), 3) == iota((SLOTS, N_ROW), 1))
     spread = dot(owner, ids_ref[...].astype(F32).astype(BF16))
     mine = iota((SLOTS, D), 1) == (iota((SLOTS, D), 0) & (CAP - 1))
     column = jnp.sum(jnp.where(mine, spread, 0.0), axis=1, keepdims=True).astype(I32)
-    here = lax.shift_right_logical(iota((SLOTS, SPAN), 0), 3) & 1 == core_ref[0]
+    here = lax.shift_right_logical(iota((SLOTS, SPAN), 0), 3) & 1 == own_core()
     match = iota((SLOTS, SPAN), 1) == column
     rows = dot(ones_where(match & here), table_ref[...])
     rows_ref[...] = (rows + dot(ones_where(match & ~here), other_ref[...])).astype(BF16)
 
 
-def place_kernel(core_ref, ids_ref, other_ref, place_ref):
+def place_kernel(hot_ref, ids_ref, other_ref, place_ref, hot_lines_ref):
     slot = iota((SLOTS, N_ROW), 0)
-    line = lax.shift_right_logical(slot, 4) * 2 + core_ref[0] == iota((SLOTS, N_ROW), 1)
-    here = lax.shift_right_logical(slot, 3) & 1 == core_ref[0]
+    line = lax.shift_right_logical(slot, 4) * 2 + own_core() == iota((SLOTS, N_ROW), 1)
+    here = lax.shift_right_logical(slot, 3) & 1 == own_core()
     spread = dot(ids_ref[...].astype(F32).astype(BF16), ones_where(line & here), 0, 1)
     spread = spread + dot(other_ref[...].astype(F32).astype(BF16), ones_where(line & ~here), 0, 1)
     mine = iota((D, SLOTS), 0) == (iota((D, SLOTS), 1) & (CAP - 1))
     line = jnp.sum(jnp.where(mine, spread, 0.0), axis=0, keepdims=True).astype(I32)
     place_ref[...] = ones_where(iota((SPAN, SLOTS), 0) == line)
+    lane = iota((16, D), 1)
+    hot = jnp.where(lane == 0, hot_ref[0, 0], jnp.where(lane == 1, hot_ref[0, 1], 0))
+    hot_lines_ref[...] = hot.astype(F32).astype(BF16)
 
 
 def dense_kernel(dense_ref, w_ref, labels_ref, w_out_ref, pre_ref, labels_out_ref, w_out_out_ref):
@@ -164,7 +175,7 @@
 
 
 def step_kernel(
-    core_ref, rows_ref, use_ref, dense_ref, pre_ref, labels_ref, w_ref, w_out_ref,
+    rows_ref, use_ref, dense_ref, pre_ref, labels_ref, w_ref, w_out_ref,
     give_ref, keep_ref, dpre_ref,
 ):
     pooled = dot(use_ref[...], rows_ref[...]).astype(BF16)
@@ -175,7 +186,7 @@
     dlogit = jax.nn.sigmoid(logit) - labels_ref[:, 0:1]
     dpre = (dlogit * w_out * (sig * (1.0 + pre * (1.0 - sig)))).astype(BF16)
     dpre_ref[...] = dpre
-    first = core_ref[0] == 0
+    first = own_core() == 0
     dense = dense_ref[...]
     by_tile(give_ref, dot(jnp.where(first, dense, pooled), dpre, 0, 0).astype(BF16))
     keep_ref[...] = jnp.where(first, pooled, dense)
@@ -217,7 +228,7 @@
     store_quarters(fill, out_ref, buf, sem)
 
 
-def owned_kernel(got_ref, place_ref, hot_ref, out_ref):
+def owned_kernel(got_ref, place_ref, hot_lines_ref, out_ref):
     grads = got_ref[:, :, 16:24, :].astype(F32).reshape(SLOTS, D).astype(BF16)
     out_ref[0:SPAN, :] = dot(place_ref[...], grads).astype(BF16)
     for half in range(2):
@@ -225,13 +236,11 @@
         out_ref[at : at + 16, :] = jnp.sum(
             got_ref[:, half, 0:16, :].astype(F32), axis=0
         ).astype(BF16)
-    lane = iota((16, D), 1)
-    hot = jnp.where(lane == 0, hot_ref[0, 0], jnp.where(lane == 1, hot_ref[0, 1], 0))
-    out_ref[SPAN + 32 : SPAN + 48, :] = hot.astype(F32).astype(BF16)
-
-
-def top_kernel(me_ref, x0_ref, x1_ref, x2_ref, x3_ref, top_ref, by_group):
-    me = me_ref[0]
+    out_ref[SPAN + 32 : SPAN + 48, :] = hot_lines_ref[...]
+
+
+def top_kernel(x0_ref, x1_ref, x2_ref, x3_ref, top_ref, by_group):
+    me = group()
     for o, ref in enumerate((x0_ref, x1_ref, x2_ref, x3_ref)):
         by_group[me ^ o] = ref[SPAN : SPAN + 32, :]
     top = jnp.zeros((32, D), F32)
@@ -241,10 +250,10 @@
 
 
 def update_kernel(
-    me_ref, x0_ref, x1_ref, x2_ref, x3_ref, master_ref, accum_ref,
+    x0_ref, x1_ref, x2_ref, x3_ref, master_ref, accum_ref,
     new_master_ref, new_accum_ref, coded_ref, by_group,
 ):
-    me = me_ref[0]
+    me = group()
     for o, ref in enumerate((x0_ref, x1_ref, x2_ref, x3_ref)):
         by_group[me ^ o] = ref[...]
     hot = [by_group[g, SPAN + 32 : SPAN + 48, :].astype(F32)[0:1, :] for g in range(N_GRP)]
@@ -276,8 +285,8 @@
     coded_ref[pl.ds(QUARTER, 16), :] = scale_row.astype(BF16)
 
 
-def fresh_kernel(me_ref, s0_ref, s1_ref, s2_ref, s3_ref, serving_ref, scale_ref):
-    me = me_ref[0]
+def fresh_kernel(s0_ref, s1_ref, s2_ref, s3_ref, serving_ref, scale_ref):
+    me = group()
     scales = jnp.zeros((16, D), F32)
     for o, ref in enumerate((s0_ref, s1_ref, s2_ref, s3_ref)):
         start = pl.multiple_of((me ^ o) * QUARTER, QUARTER)
@@ -286,10 +295,10 @@
     scale_ref[...] = scales[0:1, 0:16].astype(BF16)
 
 
-def last_kernel(core_ref, mine_ref, other_ref, top_ref, buf, sem):
+def last_kernel(mine_ref, other_ref, top_ref, buf, sem):
     def fill(i):
         half = slice(i // 2 * 16, i // 2 * 16 + 16)
-        for ref, core in ((mine_ref, core_ref[0]), (other_ref, 1 - core_ref[0])):
+        for ref, core in ((mine_ref, own_core()), (other_ref, 1 - own_core())):
             for s in range(16):
                 column = pl.multiple_of((s % 4 * 2 + core) * 128, 128)
                 line = s // 4 * 16
@@ -322,8 +331,6 @@
 def on_device(
     serving, serving_scale, hot_blocks, bag_lengths, bag_indices, dense_act, labels, w_top, w_out, master, accum,
 ):
-    me = lax.axis_index("grp").astype(I32).reshape(1)
-    core = lax.axis_index("row_2").astype(I32).reshape(1)
     (ids,) = call(ids_kernel, [like((N_ROW, D), I32)], [VM], (bag_indices,), 1 << 26)
     wanted = exchange(ids.reshape(N_ROW // 2, 2, D), CHIPS).reshape(N_ROW, D)
     use, use_t = call(
@@ -353,26 +360,22 @@
         (wanted, table, other_table, pre, labels_column, w_out_line)
     )
     (rows,) = call(
-        pick_kernel,
-        [like((SLOTS, D), BF16)],
-        [SM] + [VM] * 3,
-        (core, wanted, table, other_table),
-        1 << 26,
+        pick_kernel, [like((SLOTS, D), BF16)], [VM] * 3, (wanted, table, other_table), 1 << 26
     )
     fetched = exchange(rows.reshape(N_ROW // 2, 2 * CAP, D), CHIPS).reshape(SLOTS, D)
     other_wanted = other_core(wanted)
-    (place,) = call(
+    place, hot_lines = call(
         place_kernel,
-        [like((SPAN, SLOTS), BF16)],
+        [like((SPAN, SLOTS), BF16), like((16, D), BF16)],
         [SM] + [VM] * 2,
-        (core, wanted, other_wanted),
+        (hot_blocks, wanted, other_wanted),
         1 << 26,
     )
     give, keep, dpre = call(
         step_kernel,
         [like((N_ROW, 16, D), BF16), like((BAGS, D), BF16), like((BAGS, FF), BF16)],
-        [SM] + [VM] * 7,
-        (core, fetched, use, dense_act, pre, labels_column, w_top, w_out_line),
+        [VM] * 7,
+        (fetched, use, dense_act, pre, labels_column, w_top, w_out_line),
         1 << 29,
     )
     given = other_core(give)
@@ -396,16 +399,16 @@
     (own,) = call(
         owned_kernel,
         [like((SPAN + 48, D), BF16)],
-        [VM, VM, SM],
-        (got.reshape(N_ROW // 2, 2, 24, D), place, hot_blocks),
+        [VM] * 3,
+        (got.reshape(N_ROW // 2, 2, 24, D), place, hot_lines),
         1 << 26,
     )
     owned = over_groups(own)
     (top_part,) = call(
         top_kernel,
         [like((N_ROW // 2, 32, D), BF16)],
-        [SM] + [VM] * 4,
-        (me, *owned),
+        [VM] * 4,
+        tuple(owned),
         1 << 16,
         [pltpu.VMEM((N_GRP, 32, D), BF16)],
     )
@@ -413,8 +416,8 @@
     new_master, new_accum, coded = call(
         update_kernel,
         [like((QUARTER, D), F32), like((1, QUARTER), F32), like((QUARTER + 16, D), BF16)],
-        [SM] + [VM] * 6,
-        (me, *owned, master[0], accum),
+        [VM] * 6,
+        (*owned, master[0], accum),
         1 << 22,
         [pltpu.VMEM((N_GRP, SPAN + 48, D), BF16)],
     )
@@ -422,16 +425,16 @@
     fresh, fresh_scale = call(
         fresh_kernel,
         [like((4 * QUARTER, D), BF16), like((1, 16), BF16)],
-        [SM] + [VM] * 4,
-        (me, *quarters),
+        [VM] * 4,
+        tuple(quarters),
         1 << 20,
     )
     top_other = other_core(top_mine)
     (top_grad,) = call(
         last_kernel,
         [like((2 * D, FF), F32)],
-        [SM] + [VM] * 2,
-        (core, top_mine, top_other),
+        [VM] * 2,
+        (top_mine, top_other),
         1 << 20,
         quarters_of((2 * D, FF), F32),
         [ANY],

time: 106 us -> 106 us (level)
  the two profiles are of different devices: /device:TPU:8 before, /device:TPU:1 now
where the time goes in v8:
time: 106 us
  waiting for transfers between devices  38.9 us (37%)
  starting transfers between devices  35.9 us (34%)
  blocking collectives  14.8 us (14%)
  Pallas kernels  12.2 us (12%)
  local copies, waits for them, and re-layouts  3.08 us (3%)
    all_to_all x3, waiting for transfers between devices, exchange(): return lax.all_to_all(x, axes, 0, 0, tiled=True)  27.3 us
    all_to_all x3, starting transfers between devices, exchange(): return lax.all_to_all(x, axes, 0, 0, tiled=True)  18.1 us
    all_to_all x1, blocking collectives, exchange(): return lax.all_to_all(x, axes, 0, 0, tiled=True)  14.8 us
    pallas_call x14, Pallas kernels, call(): pl.pallas_call(kernel, out_shape=outs, in_specs=specs, out_specs=out_spec...  12.2 us
    ppermute x4, starting transfers between devices, other_core(): return lax.ppermute(x, 'row_2', [(0, 1), (1, 0)])  11.2 us
    ppermute x6, waiting for transfers between devices, over_groups(): parts.append(lax.ppermute(x, 'grp', [(g, g ^ o) for g in range(N_GRP)]))  10.4 us
    ppermute x6, starting transfers between devices, over_groups(): parts.append(lax.ppermute(x, 'grp', [(g, g ^ o) for g in range(N_GRP)]))  6.59 us
    unnamed x24, local copies, waits for them, and re-layouts  3.08 us
  transfers between devices with their start and end apart: 13, of which 10 were waited for; matrix products, arithmetic and copies ran while one was open for 0% of the time, Pallas kernels for 7%

profile of v8, /device:TPU:1, one launch (start us, length us, event | category | flops | bytes accessed | tf_op | source)
XLA Modules:
  0.0 105.6 jit_solution(7432725720884901979)
XLA Ops:
  0.6 0.0 copy-start
  0.6 0.0 copy-start.1
  0.7 1.1 %copy-done.1 = bf16[2048,128]{1,0:T(8,128)(2,1)S(1)} copy-done((bf16[2048,128]{1,0:T(8,128)(2,1)S(1)}, bf16[2048,128]{1,0:T(8,128)(2,1)}, u32[]{:S(2)}) %copy-start.1) | copy-done | bytes 524312
  1.7 0.0 copy-start.7
  1.7 0.7 copy-done.7
  2.4 0.0 copy-start.8
  2.4 0.7 copy-done.8
  3.1 0.0 copy-start.10
  3.1 0.8 shard_map.147.table_ref
  3.9 3.3 %collective-permute-start = (bf16[256,128]{1,0:T(8,128)(2,1)S(1)}, bf16[256,128]{1,0:T(8,128)(2,1)S(1)}, u32[]{:S(2)}, u32[]{:S(2)}) collective-permute-start(bf16[256,128]{1,0:T(8,128)(2,1)S(1)} %shard_map.147.table_ref), channel_id=1, source_target_pairs={{0,1},{1,0},{2,3},{3,2},{4,5},{5,4},{6,7},{7,6},{8,9},{9,8},{10,11... | collective-permute-start | bytes 196616 | tf_op jit(solution)/shard_map/ppermute | solution.py:324
  7.2 0.0 copy-done.10
  7.2 1.2 %shard_map.146 = s32[64,128]{1,0:T(8,128)} custom-call(s32[1,1024]{1,0:T(1,128)S(1)} %copy-done.10), custom_call_target="tpu_custom_call" | custom-call | flops 67108864 | bytes 36864 | tf_op jit(solution)/shard_map/pallas_call | solution.py:58
  8.3 0.0 copy-start.2
  8.3 0.0 copy-start.4
  8.3 9.6 %all-to-all-start = ((s32[32,2,128]{2,1,0:T(2,128)}), s32[32,2,128]{2,1,0:T(2,128)S(1)}, u32[]{:S(2)}, u32[]{:S(2)}) async-start(s32[32,2,128]{2,1,0:T(2,128)} %bitcast), calls=%async_computation | async-start | bytes 65536 | tf_op jit(solution)/shard_map/all_to_all | solution.py:328
  18.0 0.0 copy-start.6
  18.0 0.0 copy-done
  18.0 0.0 copy-done.2
  18.0 0.0 copy-done.4
  18.0 0.6 copy-done.6
  18.7 0.3 shard_map.148
  18.9 7.8 %all-to-all-done = s32[32,2,128]{2,1,0:T(2,128)S(1)} async-done(((s32[32,2,128]{2,1,0:T(2,128)}), s32[32,2,128]{2,1,0:T(2,128)S(1)}, u32[]{:S(2)}, u32[]{:S(2)}) %all-to-all-start) | async-done | bytes 32800 | tf_op jit(solution)/shard_map/all_to_all | solution.py:328
  26.7 0.0 collective-permute-done.other_ref
  26.7 1.2 %shard_map.149 = bf16[512,128]{1,0:T(8,128)(2,1)} custom-call(s32[64,128]{1,0:T(8,128)S(1)} %bitcast.16, bf16[256,128]{1,0:T(8,128)(2,1)S(1)} %shard_map.147.table_ref, bf16[256,128]{1,0:T(8,128)(2,1)S(1)} %collective-permute-done.other_ref), custom_call_target="tpu_custom_call" | custom-call | flops 67108864 | bytes 294912 | tf_op jit(solution)/shard_map/pallas_call | solution.py:58
  27.9 0.0 copy-start.11
  27.9 4.0 %all-to-all-start.1 = ((bf16[32,16,128]{2,1,0:T(8,128)(2,1)}), bf16[32,16,128]{2,1,0:T(8,128)(2,1)S(1)}, u32[]{:S(2)}, u32[]{:S(2)}) async-start(bf16[32,16,128]{2,1,0:T(8,128)(2,1)} %bitcast.5), calls=%async_computation.1 | async-start | bytes 262144 | tf_op jit(solution)/shard_map/all_to_all | solution.py:328
  31.9 0.0 copy-done.11
  31.9 1.9 %shard_map.150 = (bf16[256,512]{1,0:T(8,128)(2,1)S(1)}, bf16[512,256]{1,0:T(8,128)(2,1)S(1)}) custom-call(s32[1,1024]{1,0:T(1,128)S(1)} %copy-done.10, s32[1,256]{1,0:T(1,128)S(1)} %copy-done.11), custom_call_target="tpu_custom_call" | custom-call | flops 536870912 | bytes 529408 | tf_op jit(solution)/shard_map/pallas_call | solution.py:58
  33.8 7.2 %all-to-all-done.1 = bf16[32,16,128]{2,1,0:T(8,128)(2,1)S(1)} async-done(((bf16[32,16,128]{2,1,0:T(8,128)(2,1)}), bf16[32,16,128]{2,1,0:T(8,128)(2,1)S(1)}, u32[]{:S(2)}, u32[]{:S(2)}) %all-to-all-start.1) | async-done | bytes 131104 | tf_op jit(solution)/shard_map/all_to_all | solution.py:328
  41.1 1.0 shard_map.151
  42.1 2.8 %collective-permute-start.1 = (bf16[64,16,128]{2,1,0:T(8,128)(2,1)S(1)}, bf16[64,16,128]{2,1,0:T(8,128)(2,1)S(1)}, u32[]{:S(2)}, u32[]{:S(2)}) collective-permute-start(bf16[64,16,128]{2,1,0:T(8,128)(2,1)S(1)} %get-tuple-element.42), channel_id=1, source_target_pairs={{0,1},{1,0},{2,3},{3,2},{4,5},{5,4},{6,7},{7,6},{8,9},{9,8},{10,11... | collective-permute-start | bytes 786440 | tf_op jit(solution)/shard_map/ppermute | solution.py:324
  44.8 0.9 shard_map.152
  45.7 0.3 collective-permute-done.1.given_ref
  46.0 0.8 shard_map.153
  46.8 0.0 copy-start.9
  46.8 4.4 %all-to-all-start.2 = ((bf16[64,24,128]{2,1,0:T(8,128)(2,1)}), bf16[64,24,128]{2,1,0:T(8,128)(2,1)S(1)}, u32[]{:S(2)}, u32[]{:S(2)}) async-start(bf16[64,24,128]{2,1,0:T(8,128)(2,1)} %shard_map.153), calls=%async_computation.2 | async-start | bytes 786432 | tf_op jit(solution)/shard_map/all_to_all | solution.py:328
  51.3 0.7 collective-permute-start.2
  51.9 0.9 collective-permute-done.2.other_ref
  52.8 0.0 copy-done.9
  52.8 0.9 shard_map.154
  53.7 12.2 %all-to-all-done.2 = bf16[64,24,128]{2,1,0:T(8,128)(2,1)S(1)} async-done(((bf16[64,24,128]{2,1,0:T(8,128)(2,1)}), bf16[64,24,128]{2,1,0:T(8,128)(2,1)S(1)}, u32[]{:S(2)}, u32[]{:S(2)}) %all-to-all-start.2) | async-done | bytes 393248 | tf_op jit(solution)/shard_map/all_to_all | solution.py:328
  65.9 0.2 shard_map.155.x0_ref
  66.1 2.6 %collective-permute-start.5 = (bf16[304,128]{1,0:T(8,128)(2,1)S(1)}, bf16[304,128]{1,0:T(8,128)(2,1)S(1)}, u32[]{:S(2)}, u32[]{:S(2)}) collective-permute-start(bf16[304,128]{1,0:T(8,128)(2,1)S(1)} %shard_map.155.x0_ref), channel_id=1, source_target_pairs={{0,192},{64,128},{128,64},{192,0},{1,193},{65,129},{129,65},{193,1... | collective-permute-start | bytes 233480 | tf_op jit(solution)/shard_map/ppermute | solution.py:319
  68.7 0.5 collective-permute-start.4
  69.2 0.3 collective-permute-start.3
  69.5 1.5 %collective-permute-done.5.x3_ref = bf16[304,128]{1,0:T(8,128)(2,1)S(1)} collective-permute-done((bf16[304,128]{1,0:T(8,128)(2,1)S(1)}, bf16[304,128]{1,0:T(8,128)(2,1)S(1)}, u32[]{:S(2)}, u32[]{:S(2)}) %collective-permute-start.5) | collective-permute-done | bytes 77856 | tf_op jit(solution)/shard_map/ppermute | solution.py:319
  71.0 2.5 %collective-permute-done.4.x2_ref = bf16[304,128]{1,0:T(8,128)(2,1)S(1)} collective-permute-done((bf16[304,128]{1,0:T(8,128)(2,1)S(1)}, bf16[304,128]{1,0:T(8,128)(2,1)S(1)}, u32[]{:S(2)}, u32[]{:S(2)}) %collective-permute-start.4) | collective-permute-done | bytes 77856 | tf_op jit(solution)/shard_map/ppermute | solution.py:319
  73.5 0.1 collective-permute-done.3.x1_ref
  73.6 0.0 copy-start.3
  73.6 0.0 copy-start.5
  73.7 14.8 %all_to_all.20.mine_ref = bf16[32,32,128]{2,1,0:T(8,128)(2,1)S(1)} all-to-all(bf16[32,32,128]{2,1,0:T(8,128)(2,1)S(1)} %shard_map.158), channel_id=1, replica_groups=mesh['grp'=4,'row_0'=4,'row_1'=8,'row_2'=2] {'row_0','row_1'}, dimensions={0} | all-to-all | bytes 524288 | tf_op jit(solution)/shard_map/all_to_all | solution.py:328
  88.4 4.5 %collective-permute-start.9 = (bf16[32,32,128]{2,1,0:T(8,128)(2,1)S(1)}, bf16[32,32,128]{2,1,0:T(8,128)(2,1)S(1)}, u32[]{:S(2)}, u32[]{:S(2)}) collective-permute-start(bf16[32,32,128]{2,1,0:T(8,128)(2,1)S(1)} %all_to_all.20.mine_ref), channel_id=1, source_target_pairs={{0,1},{1,0},{2,3},{3,2},{4,5},{5,4},{6,7},{7,6},{8,9},{9,8},{10,11... | collective-permute-start | bytes 786440 | tf_op jit(solution)/shard_map/ppermute | solution.py:324
  92.9 0.0 copy-done.3
  92.9 0.0 copy-done.5
  92.9 1.2 %shard_map.156 = (f32[512,128]{1,0:T(8,128)}, f32[1,512]{1,0:T(1,128)}, bf16[528,128]{1,0:T(8,128)(2,1)S(1)}) custom-call(bf16[304,128]{1,0:T(8,128)(2,1)S(1)} %shard_map.155.x0_ref, bf16[304,128]{1,0:T(8,128)(2,1)S(1)} %collective-permute-done.3.x1_ref, bf16[304,128]{1,0:T(8,128)(2,1)S(1)} %collective-permute-done.4.x2_ref, ...), custom_call_target="tpu_custom_call" | custom-call | flops 4194304 | bytes 974848 | tf_op jit(solution)/shard_map/pallas_call | solution.py:58
  94.1 0.9 collective-permute-start.8
  95.1 0.5 collective-permute-start.7
  95.6 1.8 %collective-permute-start.6 = (bf16[528,128]{1,0:T(8,128)(2,1)S(1)}, bf16[528,128]{1,0:T(8,128)(2,1)S(1)}, u32[]{:S(2)}, u32[]{:S(2)}) collective-permute-start(bf16[528,128]{1,0:T(8,128)(2,1)S(1)} %get-tuple-element.48.s0_ref), channel_id=1, source_target_pairs={{0,64},{64,0},{128,192},{192,128},{1,65},{65,1},{129,193},{193,129... | collective-permute-start | bytes 405512 | tf_op jit(solution)/shard_map/ppermute | solution.py:319
  97.4 6.0 %collective-permute-done.8.s3_ref = bf16[528,128]{1,0:T(8,128)(2,1)S(1)} collective-permute-done((bf16[528,128]{1,0:T(8,128)(2,1)S(1)}, bf16[528,128]{1,0:T(8,128)(2,1)S(1)}, u32[]{:S(2)}, u32[]{:S(2)}) %collective-permute-start.8) | collective-permute-done | bytes 135200 | tf_op jit(solution)/shard_map/ppermute | solution.py:319
  103.4 0.0 collective-permute-done.7.s2_ref
  103.4 0.3 collective-permute-done.6.s1_ref
  103.7 0.8 shard_map.157
  104.6 0.0 collective-permute-done.9.other_ref
  104.6 1.0 shard_map.159
  (1 shorter events, 0.0 us)
Async XLA Ops:
  0.6 17.4 %copy-start = (bf16[256,1024]{1,0:T(8,128)(2,1)S(1)}, bf16[256,1024]{1,0:T(8,128)(2,1)}, u32[]{:S(2)}) copy-start(bf16[256,1024]{1,0:T(8,128)(2,1)} %w_ref.5) | copy-start | bytes 1572868
  0.6 1.1 %copy-start.1 = (bf16[2048,128]{1,0:T(8,128)(2,1)S(1)}, bf16[2048,128]{1,0:T(8,128)(2,1)}, u32[]{:S(2)}) copy-start(bf16[2048,128]{1,0:T(8,128)(2,1)} %serving_ref.1) | copy-start | bytes 1572868
  1.7 0.7 copy-start.7
  2.4 0.7 copy-start.8
  3.1 4.1 %copy-start.10 = (s32[1,1024]{1,0:T(1,128)S(1)}, s32[1,1024]{1,0:T(1,128)}, u32[]{:S(2)}) copy-start(s32[1,1024]{1,0:T(1,128)} %idx_ref.3) | copy-start | bytes 12292
  3.9 22.9 %collective-permute-start = (bf16[256,128]{1,0:T(8,128)(2,1)S(1)}, bf16[256,128]{1,0:T(8,128)(2,1)S(1)}, u32[]{:S(2)}, u32[]{:S(2)}) collective-permute-start(bf16[256,128]{1,0:T(8,128)(2,1)S(1)} %shard_map.147.table_ref), channel_id=1, source_target_pairs={{0,1},{1,0},{2,3},{3,2},{4,5},{5,4},{6,7},{7,6},{8,9},{9,8},{10,11... | collective-permute-start | bytes 196616 | tf_op jit(solution)/shard_map/ppermute | solution.py:324
  8.3 9.7 %copy-start.2 = (bf16[256,128]{1,0:T(8,128)(2,1)S(1)}, bf16[256,128]{1,0:T(8,128)(2,1)}, u32[]{:S(2)}) copy-start(bf16[256,128]{1,0:T(8,128)(2,1)} %dense_ref.3) | copy-start | bytes 196612
  8.3 9.7 %copy-start.4 = (f32[1024]{0:T(1024)S(1)}, f32[1024]{0:T(1024)}, u32[]{:S(2)}) copy-start(f32[1024]{0:T(1024)} %param.19) | copy-start | bytes 12292
  8.3 18.4 %all-to-all-start = ((s32[32,2,128]{2,1,0:T(2,128)}), s32[32,2,128]{2,1,0:T(2,128)S(1)}, u32[]{:S(2)}, u32[]{:S(2)}) async-start(s32[32,2,128]{2,1,0:T(2,128)} %bitcast), calls=%async_computation | async-start | bytes 65536 | tf_op jit(solution)/shard_map/all_to_all | solution.py:328
  18.0 0.7 copy-start.6
  27.9 4.0 %copy-start.11 = (s32[1,256]{1,0:T(1,128)S(1)}, s32[1,256]{1,0:T(1,128)}, u32[]{:S(2)}) copy-start(s32[1,256]{1,0:T(1,128)} %len_ref.1) | copy-start | bytes 3076
  27.9 13.1 %all-to-all-start.1 = ((bf16[32,16,128]{2,1,0:T(8,128)(2,1)}), bf16[32,16,128]{2,1,0:T(8,128)(2,1)S(1)}, u32[]{:S(2)}, u32[]{:S(2)}) async-start(bf16[32,16,128]{2,1,0:T(8,128)(2,1)} %bitcast.5), calls=%async_computation.1 | async-start | bytes 262144 | tf_op jit(solution)/shard_map/all_to_all | solution.py:328
  42.1 3.9 %collective-permute-start.1 = (bf16[64,16,128]{2,1,0:T(8,128)(2,1)S(1)}, bf16[64,16,128]{2,1,0:T(8,128)(2,1)S(1)}, u32[]{:S(2)}, u32[]{:S(2)}) collective-permute-start(bf16[64,16,128]{2,1,0:T(8,128)(2,1)S(1)} %get-tuple-element.42), channel_id=1, source_target_pairs={{0,1},{1,0},{2,3},{3,2},{4,5},{5,4},{6,7},{7,6},{8,9},{9,8},{10,11... | collective-permute-start | bytes 786440 | tf_op jit(solution)/shard_map/ppermute | solution.py:324
  46.8 6.0 %copy-start.9 = (s32[1,2]{1,0:T(1,128)S(1)}, s32[1,2]{1,0:T(1,128)}, u32[]{:S(2)}) copy-start(s32[1,2]{1,0:T(1,128)} %hot_ref.3) | copy-start | bytes 28
  46.8 19.1 %all-to-all-start.2 = ((bf16[64,24,128]{2,1,0:T(8,128)(2,1)}), bf16[64,24,128]{2,1,0:T(8,128)(2,1)S(1)}, u32[]{:S(2)}, u32[]{:S(2)}) async-start(bf16[64,24,128]{2,1,0:T(8,128)(2,1)} %shard_map.153), calls=%async_computation.2 | async-start | bytes 786432 | tf_op jit(solution)/shard_map/all_to_all | solution.py:328
  51.3 1.5 %collective-permute-start.2 = (s32[64,128]{1,0:T(8,128)S(1)}, s32[64,128]{1,0:T(8,128)S(1)}, u32[]{:S(2)}, u32[]{:S(2)}) collective-permute-start(s32[64,128]{1,0:T(8,128)S(1)} %bitcast.17), channel_id=1, source_target_pairs={{0,1},{1,0},{2,3},{3,2},{4,5},{5,4},{6,7},{7,6},{8,9},{9,8},{10,11... | collective-permute-start | bytes 98312 | tf_op jit(solution)/shard_map/ppermute | solution.py:324
  66.1 4.8 %collective-permute-start.5 = (bf16[304,128]{1,0:T(8,128)(2,1)S(1)}, bf16[304,128]{1,0:T(8,128)(2,1)S(1)}, u32[]{:S(2)}, u32[]{:S(2)}) collective-permute-start(bf16[304,128]{1,0:T(8,128)(2,1)S(1)} %shard_map.155.x0_ref), channel_id=1, source_target_pairs={{0,192},{64,128},{128,64},{192,0},{1,193},{65,129},{129,65},{193,1... | collective-permute-start | bytes 233480 | tf_op jit(solution)/shard_map/ppermute | solution.py:319
  68.7 4.8 %collective-permute-start.4 = (bf16[304,128]{1,0:T(8,128)(2,1)S(1)}, bf16[304,128]{1,0:T(8,128)(2,1)S(1)}, u32[]{:S(2)}, u32[]{:S(2)}) collective-permute-start(bf16[304,128]{1,0:T(8,128)(2,1)S(1)} %shard_map.155.x0_ref), channel_id=1, source_target_pairs={{0,128},{64,192},{128,0},{192,64},{1,129},{65,193},{129,1},{193,65... | collective-permute-start | bytes 233480 | tf_op jit(solution)/shard_map/ppermute | solution.py:319
  69.2 4.4 %collective-permute-start.3 = (bf16[304,128]{1,0:T(8,128)(2,1)S(1)}, bf16[304,128]{1,0:T(8,128)(2,1)S(1)}, u32[]{:S(2)}, u32[]{:S(2)}) collective-permute-start(bf16[304,128]{1,0:T(8,128)(2,1)S(1)} %shard_map.155.x0_ref), channel_id=1, source_target_pairs={{0,64},{64,0},{128,192},{192,128},{1,65},{65,1},{129,193},{193,129... | collective-permute-start | bytes 233480 | tf_op jit(solution)/shard_map/ppermute | solution.py:319
  73.6 19.3 %copy-start.3 = (f32[1,512,128]{2,1,0:T(8,128)S(1)}, f32[1,512,128]{2,1,0:T(8,128)}, u32[]{:S(2)}) copy-start(f32[1,512,128]{2,1,0:T(8,128)} %param.20) | copy-start | bytes 786436
  73.6 19.3 %copy-start.5 = (f32[1,512]{1,0:T(1,128)S(1)}, f32[1,512]{1,0:T(1,128)}, u32[]{:S(2)}) copy-start(f32[1,512]{1,0:T(1,128)} %accum_ref.1) | copy-start | bytes 6148
  88.4 16.1 %collective-permute-start.9 = (bf16[32,32,128]{2,1,0:T(8,128)(2,1)S(1)}, bf16[32,32,128]{2,1,0:T(8,128)(2,1)S(1)}, u32[]{:S(2)}, u32[]{:S(2)}) collective-permute-start(bf16[32,32,128]{2,1,0:T(8,128)(2,1)S(1)} %all_to_all.20.mine_ref), channel_id=1, source_target_pairs={{0,1},{1,0},{2,3},{3,2},{4,5},{5,4},{6,7},{7,6},{8,9},{9,8},{10,11... | collective-permute-start | bytes 786440 | tf_op jit(solution)/shard_map/ppermute | solution.py:324
  94.1 9.2 %collective-permute-start.8 = (bf16[528,128]{1,0:T(8,128)(2,1)S(1)}, bf16[528,128]{1,0:T(8,128)(2,1)S(1)}, u32[]{:S(2)}, u32[]{:S(2)}) collective-permute-start(bf16[528,128]{1,0:T(8,128)(2,1)S(1)} %get-tuple-element.48.s0_ref), channel_id=1, source_target_pairs={{0,192},{64,128},{128,64},{192,0},{1,193},{65,129},{129,65},{193,1... | collective-permute-start | bytes 405512 | tf_op jit(solution)/shard_map/ppermute | solution.py:319
  95.1 8.3 %collective-permute-start.7 = (bf16[528,128]{1,0:T(8,128)(2,1)S(1)}, bf16[528,128]{1,0:T(8,128)(2,1)S(1)}, u32[]{:S(2)}, u32[]{:S(2)}) collective-permute-start(bf16[528,128]{1,0:T(8,128)(2,1)S(1)} %get-tuple-element.48.s0_ref), channel_id=1, source_target_pairs={{0,128},{64,192},{128,0},{192,64},{1,129},{65,193},{129,1},{193,65... | collective-permute-start | bytes 405512 | tf_op jit(solution)/shard_map/ppermute | solution.py:319
  95.6 8.1 %collective-permute-start.6 = (bf16[528,128]{1,0:T(8,128)(2,1)S(1)}, bf16[528,128]{1,0:T(8,128)(2,1)S(1)}, u32[]{:S(2)}, u32[]{:S(2)}) collective-permute-start(bf16[528,128]{1,0:T(8,128)(2,1)S(1)} %get-tuple-element.48.s0_ref), channel_id=1, source_target_pairs={{0,64},{64,0},{128,192},{192,128},{1,65},{65,1},{129,193},{193,129... | collective-permute-start | bytes 405512 | tf_op jit(solution)/shard_map/ppermute | solution.py:319
